TPU v7x, 32 devices: a whole 2x2x4 slice. The times are simulated.
32 devices in a mesh: dp: 16 (over z, x, core), mlp: 2 (over y).
Axes of the slice: x: 2, y: 2, z: 4, core: 2. Of those that a mesh axis runs over, the one named last changes fastest.
Arguments:
- patches: bfloat16 [24576, 768], P(('dp', 'mlp')), may hold values from -6 to 6
- image_of_patch: int32 [16, 1536], P('dp'), may hold values from 0 to 3, never falling along the last dimension, each value on 1 to 576 neighbouring positions
- patch_row: int32 [16, 1536], P('dp'), may hold values from 0 to 23
- patch_col: int32 [16, 1536], P('dp'), may hold values from 0 to 23
- ln1_gain: float32 [768], replicated, may hold values from 0.1 to 1.9
- ln1_bias: float32 [768], replicated, may hold values from -1.75 to 1.75
- w_qkv: bfloat16 [768, 2304], replicated, may hold values from -0.21875 to 0.21875
- b_qkv: float32 [2304], replicated, may hold values from -1.75 to 1.75
- freqs: float32 [2, 384], replicated, may hold values from -0.5 to 0.5
- w_out: bfloat16 [768, 768], replicated, may hold values from -1.75 to 1.75
- b_out: float32 [768], replicated, may hold values from -1.75 to 1.75
- ln2_gain: float32 [768], replicated, may hold values from 0.1 to 1.9
- ln2_bias: float32 [768], replicated, may hold values from -1.75 to 1.75
- w_up: bfloat16 [768, 3072], P(None, 'mlp'), may hold values from -0.21875 to 0.21875
- b_up: float32 [3072], P('mlp'), may hold values from -1.75 to 1.75
- w_down: bfloat16 [3072, 768], P('mlp'), may hold values from -0.109375 to 0.109375
- b_down: float32 [768], replicated, may hold values from -1.75 to 1.75
- out_cotangent: bfloat16 [24576, 768], P(('dp', 'mlp')), may hold values from -6 to 6
Outputs:
- block_out: bfloat16 [24576, 768], P(('dp', 'mlp'))
- grad_patches: bfloat16 [24576, 768], P(('dp', 'mlp'))
- grad_ln1_gain: float32 [768], replicated
- grad_ln1_bias: float32 [768], replicated
- grad_w_qkv: float32 [768, 2304], replicated
- grad_b_qkv: float32 [2304], replicated
- grad_freqs: float32 [2, 384], replicated
- grad_w_out: float32 [768, 768], replicated
- grad_b_out: float32 [768], replicated
- grad_ln2_gain: float32 [768], replicated
- grad_ln2_bias: float32 [768], replicated
- grad_w_up: float32 [768, 3072], P(None, 'mlp')
- grad_b_up: float32 [3072], P('mlp')
- grad_w_down: float32 [3072, 768], P('mlp')
- grad_b_down: float32 [768], replicated
Inputs may be any that keep to these rules, and one draw needn't show every extreme that they name: `image_of_patch`: within each group the image numbers never fall, every image has 1 to 576 patches, and some image has exactly 576.
All inputs are finite; a program needn't handle non-finite values.
Results may differ from a plain program's by a relative error of at most 0.013.
Values may be sent and summed in bfloat16 or wider, within the bound.
A program may use at most 192 MiB of HBM per device.

v0:
```python
from functools import partial

import jax
import jax.numpy as jnp
from jax import lax
from jax.sharding import PartitionSpec as P

H = 12
HD = 64


EPSILON = 1e-06


def layer_norm(values, gain, shift):
    center = values - jnp.mean(values, axis=-1, keepdims=True)
    spread = jnp.mean(center * center, axis=-1, keepdims=True)
    return center * lax.rsqrt(spread + EPSILON) * gain + shift


def angles(row_pos, col_pos, freq_table):
    freq_row = freq_table[0].reshape(H, HD // 2)
    freq_col = freq_table[1].reshape(H, HD // 2)
    return row_pos[:, None, None] * freq_row[None] + col_pos[:, None, None] * freq_col[None]


def rotate(values, angle):
    half = values.shape[-1] // 2
    first = values[..., :half]
    second = values[..., half:]
    cosine = jnp.cos(angle)
    sine = jnp.sin(angle)
    return jnp.concatenate(
        [first * cosine - second * sine, first * sine + second * cosine], axis=-1
    )


def transpose_dot(left, right):
    return lax.dot_general(
        left, right, (((0,), (0,)), ((), ())), preferred_element_type=jnp.float32
    )


def dot_transposed(left, right):
    return lax.dot_general(
        left, right, (((1,), (1,)), ((), ())), preferred_element_type=jnp.float32
    )


def split_heads(values):
    return jnp.transpose(values.reshape(values.shape[0], H, HD), (1, 0, 2))


def join_heads(values):
    return jnp.transpose(values, (1, 0, 2)).reshape(values.shape[1], H * HD)


def per_device(
    patches,
    image_of_patch,
    patch_row,
    patch_col,
    ln1_gain,
    ln1_bias,
    w_qkv,
    b_qkv,
    freqs,
    w_out,
    b_out,
    ln2_gain,
    ln2_bias,
    w_up,
    b_up,
    w_down,
    b_down,
    out_cotangent,
):
    own_rows = patches.shape[0]
    width = patches.shape[1]
    scale = HD ** (-0.5)
    offset = lax.axis_index("mlp") * own_rows
    image_all = image_of_patch[0]
    row_all = patch_row[0].astype(jnp.float32)
    col_all = patch_col[0].astype(jnp.float32)
    image_own = lax.dynamic_slice_in_dim(image_all, offset, own_rows)
    row_own = lax.dynamic_slice_in_dim(row_all, offset, own_rows)
    col_own = lax.dynamic_slice_in_dim(col_all, offset, own_rows)
    same_image = image_own[:, None] == image_all[None, :]
    inputs = patches.astype(jnp.float32)
    normed_full, norm1_back = jax.vjp(layer_norm, inputs, ln1_gain, ln1_bias)
    normed = normed_full.astype(jnp.bfloat16)
    w_query = w_qkv[:, :width]
    w_pair = w_qkv[:, width:]
    pair_all = (
        jnp.dot(
            lax.all_gather(normed, "mlp", axis=0, tiled=True),
            w_pair,
            preferred_element_type=jnp.float32,
        )
        + b_qkv[width:]
    )
    seq_rows = pair_all.shape[0]
    query_pre = (
        jnp.dot(normed, w_query, preferred_element_type=jnp.float32) + b_qkv[:width]
    ).reshape(own_rows, H, HD)

    def rotate_own(values, freq_table):
        return rotate(values, angles(row_own, col_own, freq_table))

    query_rot, query_back = jax.vjp(rotate_own, query_pre, freqs)
    key_rot = rotate(pair_all[:, :width].reshape(seq_rows, H, HD), angles(row_all, col_all, freqs))
    query_heads = jnp.transpose(query_rot, (1, 0, 2)).astype(jnp.bfloat16)
    key_heads = jnp.transpose(key_rot, (1, 0, 2)).astype(jnp.bfloat16)
    value_heads = split_heads(pair_all[:, width:].astype(jnp.bfloat16))

    def masked_scores(query, keys, allowed):
        raw = dot_transposed(query, keys) * scale
        return jnp.where(allowed, raw, -1e30)

    def head_forward(item):
        query, keys, values = item
        scores = masked_scores(query, keys, same_image)
        peak = jnp.max(scores, axis=-1, keepdims=True)
        expo = jnp.exp(scores - peak)
        total = jnp.sum(expo, axis=-1, keepdims=True)
        weights = (expo / total).astype(jnp.bfloat16)
        return (jnp.dot(weights, values, preferred_element_type=jnp.float32), peak + jnp.log(total))

    mixed_heads, log_totals = lax.map(head_forward, (query_heads, key_heads, value_heads))
    mixed = join_heads(mixed_heads).astype(jnp.bfloat16)
    attended = jnp.dot(mixed, w_out, preferred_element_type=jnp.float32) + b_out
    middle = inputs + attended
    normed2_full, norm2_back = jax.vjp(layer_norm, middle, ln2_gain, ln2_bias)
    normed2 = normed2_full.astype(jnp.bfloat16)
    normed2_all = lax.all_gather(normed2, "mlp", axis=0, tiled=True)
    pre_all = jnp.dot(normed2_all, w_up, preferred_element_type=jnp.float32) + b_up
    hidden_full, gelu_back = jax.vjp(partial(jax.nn.gelu, approximate=False), pre_all)
    hidden = hidden_full.astype(jnp.bfloat16)
    branch_out = lax.psum_scatter(
        jnp.dot(
            lax.slice_in_dim(hidden, 0, own_rows * lax.axis_size("mlp"), axis=0),
            w_down,
            preferred_element_type=jnp.float32,
        ).astype(jnp.bfloat16),
        "mlp",
        scatter_dimension=0,
        tiled=True,
    ).astype(jnp.float32)
    block_out = (middle + branch_out + b_down).astype(jnp.bfloat16)
    grad_out = out_cotangent.astype(jnp.float32)
    piece = lax.all_gather(out_cotangent, "mlp", axis=0, tiled=True)
    start = jnp.int32(0)
    grad_weight = jnp.zeros((hidden.shape[1], width), jnp.float32)
    grad_hidden = jnp.zeros(hidden.shape, jnp.float32)
    hidden_rows = lax.dynamic_slice_in_dim(hidden, start, piece.shape[0], 0)
    grad_weight = grad_weight + transpose_dot(hidden_rows, piece)
    grad_hidden = lax.dynamic_update_slice_in_dim(
        grad_hidden, dot_transposed(piece, w_down), start, 0
    )
    grad_w_down, grad_hidden = (grad_weight, grad_hidden)
    grad_pre = gelu_back(grad_hidden)[0].astype(jnp.bfloat16)
    grad_b_up = jnp.sum(grad_pre.astype(jnp.float32), axis=0)
    grad_w_up = transpose_dot(normed2_all, grad_pre)
    grad_normed2 = lax.psum_scatter(
        dot_transposed(grad_pre, w_up), "mlp", scatter_dimension=0, tiled=True
    )
    grad_from_norm2, grad_ln2_gain, grad_ln2_bias = norm2_back(grad_normed2)
    grad_middle = grad_out + grad_from_norm2
    grad_b_down = jnp.sum(grad_out, axis=0)
    grad_attended = grad_middle.astype(jnp.bfloat16)
    grad_b_out = jnp.sum(grad_attended.astype(jnp.float32), axis=0)
    grad_w_out = transpose_dot(mixed, grad_attended)
    grad_mixed_heads = split_heads(dot_transposed(grad_attended, w_out).astype(jnp.bfloat16))

    def score_grads(query, keys, values, grad_mix, log_total, allowed):
        scores = masked_scores(query, keys, allowed)
        weights = jnp.exp(scores - log_total)
        grad_weights = dot_transposed(grad_mix, values)
        inner = jnp.sum(weights * grad_weights, axis=-1, keepdims=True)
        return (weights, grad_weights, inner)

    def query_backward(item):
        query, keys, values, grad_mix, log_total = item
        weights, grad_weights, inner = score_grads(
            query, keys, values, grad_mix, log_total, same_image
        )
        grad_scores = (weights * (grad_weights - inner)).astype(jnp.bfloat16)
        grad_query = jnp.dot(grad_scores, keys, preferred_element_type=jnp.float32) * scale
        return (grad_query, inner)

    grad_q_heads, inners = lax.map(
        query_backward, (query_heads, key_heads, value_heads, grad_mixed_heads, log_totals)
    )
    query_group, grad_mix_group = (
        lax.all_gather(query_heads, "mlp", axis=1, tiled=True),
        lax.all_gather(grad_mixed_heads, "mlp", axis=1, tiled=True),
    )
    log_group, inner_group = (
        lax.all_gather(log_totals, "mlp", axis=1, tiled=True),
        lax.all_gather(inners, "mlp", axis=1, tiled=True),
    )
    key_own = lax.dynamic_slice_in_dim(key_heads, offset, own_rows, 1)
    value_own = lax.dynamic_slice_in_dim(value_heads, offset, own_rows, 1)
    same_columns = image_all[:, None] == image_own[None, :]

    def key_backward(item):
        query, keys, values, grad_mix, log_total, inner = item
        scores = masked_scores(query, keys, same_columns)
        weights = jnp.exp(scores - log_total)
        grad_weights = dot_transposed(grad_mix, values)
        grad_scores = (weights * (grad_weights - inner)).astype(jnp.bfloat16)
        grad_keys = transpose_dot(grad_scores, query) * scale
        grad_values = transpose_dot(weights.astype(jnp.bfloat16), grad_mix)
        return (grad_keys, grad_values)

    grad_k_heads, grad_v_heads = lax.map(
        key_backward, (query_group, key_own, value_own, grad_mix_group, log_group, inner_group)
    )
    key_grad = join_heads(grad_k_heads)
    value_grad = join_heads(grad_v_heads)
    key_pre_own = lax.dynamic_slice_in_dim(pair_all, offset, own_rows, 0)[:, :width].reshape(
        own_rows, H, HD
    )
    rotated_again, key_back = jax.vjp(rotate_own, key_pre_own, freqs)
    grad_query_pre, grad_freq_query = query_back(jnp.transpose(grad_q_heads, (1, 0, 2)))
    grad_key_pre, grad_freq_key = key_back(key_grad.reshape(own_rows, H, HD))
    grad_qkv = jnp.concatenate(
        [
            grad_query_pre.reshape(own_rows, width),
            grad_key_pre.reshape(own_rows, width),
            value_grad,
        ],
        axis=1,
    ).astype(jnp.bfloat16)
    grad_b_qkv = jnp.sum(grad_qkv.astype(jnp.float32), axis=0)
    grad_w_qkv = transpose_dot(normed, grad_qkv)
    grad_normed = dot_transposed(grad_qkv, w_qkv)
    grad_from_norm1, grad_ln1_gain, grad_ln1_bias = norm1_back(grad_normed)
    grad_patches = (grad_middle + grad_from_norm1).astype(jnp.bfloat16)
    grad_freqs = grad_freq_query + grad_freq_key
    small_grads = jnp.concatenate(
        [
            grad_ln1_gain,
            grad_ln1_bias,
            grad_b_qkv,
            grad_freqs.reshape(-1),
            grad_b_out,
            grad_ln2_gain,
            grad_ln2_bias,
            grad_b_down,
        ]
    )
    shared = lax.psum((grad_w_qkv, grad_w_out, small_grads), ("dp", "mlp"))
    sharded = lax.psum((grad_w_up, grad_b_up, grad_w_down), "dp")
    small_total = shared[2]
    return (
        block_out,
        grad_patches,
        small_total[0:width],
        small_total[width : 2 * width],
        shared[0],
        small_total[2 * width : 5 * width],
        small_total[5 * width : 6 * width].reshape(2, width // 2),
        shared[1],
        small_total[6 * width : 7 * width],
        small_total[7 * width : 8 * width],
        small_total[8 * width : 9 * width],
        sharded[0],
        sharded[1],
        sharded[2],
        small_total[9 * width : 10 * width],
    )


def solution(mesh):
    in_specs = (
        P(("dp", "mlp"), None),
        P("dp", None),
        P("dp", None),
        P("dp", None),
        P(),
        P(),
        P(),
        P(),
        P(),
        P(),
        P(),
        P(),
        P(),
        P(None, "mlp"),
        P("mlp"),
        P("mlp", None),
        P(),
        P(("dp", "mlp"), None),
    )
    out_specs = (
        P(("dp", "mlp"), None),
        P(("dp", "mlp"), None),
        P(),
        P(),
        P(),
        P(),
        P(),
        P(),
        P(),
        P(),
        P(),
        P(None, "mlp"),
        P("mlp"),
        P("mlp", None),
        P(),
    )
    return jax.shard_map(
        per_device, mesh=mesh, in_specs=in_specs, out_specs=out_specs, check_vma=False
    )
```

profile of v0, /device:TPU:0, one launch (start us, length us, event | category | flops | bytes accessed | tf_op | source)
XLA Modules:
  0.0 912.0 jit_solution(1805536335612958809)
XLA Ops:
  24.2 5.2 subtract_convert_fusion.1
  30.5 3.7 copy.51
  38.4 12.9 %all-gather.6.cloned.1.call-done = bf16[1536,768]{0,1:T(8,128)(2,1)} async-done(((bf16[768,768]{0,1:T(8,128)(2,1)}), bf16[1536,768]{0,1:T(8,128)(2,1)}) %all-gather.6.cloned.1.call-update) | async-done | bytes 2359312 | tf_op jit(solution)/shard_map/all_gather | solution.py:96
  51.2 6.2 convolution_add_fusion.1
  57.8 3.3 copy-done.17
  62.8 9.4 %subtract_convert_fusion = (bf16[1536,12,32]{0,2,1:T(8,128)(2,1)S(1)}, bf16[1536,12,32]{0,2,1:T(8,128)(2,1)S(1)}) fusion(f32[1536,12,64]{0,2,1:T(8,128)S(1)} %bitcast.151, f32[12,32]{1,0:T(8,128)S(1)} %copy-done.31, f32[1536]{0:T(1024)S(1)} %copy-done.52, f32[12,32]{1,0:T(8,128)S(1)} %mul.348, f32[1536]{0:T(1024)S(1)} %copy-done.53), kind=kLoop, calls=%fused_computation.128 | loop fusion | flops 6488064 | bytes 7093248 | tf_op jit(solution)/shard_map/convert.8
  75.2 5.9 copy.52
  81.1 5.9 copy.50
  87.7 75.5 %while.39 = (s32[]{:T(128)}, bf16[12,768,64]{1,2,0:T(8,128)(2,1)}, f32[12,768,1]{1,2,0:T(1,128)}, bf16[12,768,64]{2,1,0:T(8,128)(2,1)}, bf16[12,1536,64]{2,1,0:T...) while((s32[]{:T(128)}, bf16[12,768,64]{1,2,0:T(8,128)(2,1)}, ...), condition=%wide.region_5.6_spmd.clone, body=%wide.region_2.5_spmd.clone.sunk | while | flops 312605952 | bytes 15378013 | solution.py:129
  169.7 35.4 %all-gather.8.cloned.1.call-done = bf16[1536,768]{0,1:T(8,128)(2,1)} async-done(((bf16[768,768]{0,1:T(8,128)(2,1)}), bf16[1536,768]{0,1:T(8,128)(2,1)}) %all-gather.8.cloned.1.call-update) | async-done | bytes 2359312 | tf_op jit(solution)/shard_map/all_gather | solution.py:135
  205.1 26.9 %multiply_convert_fusion.9 = (bf16[1536,1536]{1,0:T(8,128)(2,1)}, f32[1536,1536]{1,0:T(8,128)}, f32[1536,1536]{1,0:T(8,128)}) fusion(f32[1536]{0:T(1024)S(1)} %copy-done.68, bf16[1536,768]{0,1:T(8,128)(2,1)} %all-gather.8.cloned.1.call-done, bf16[768,1536]{1,0:T(8,128)(2,1)S(1)} %copy-done), kind=kOutput, calls=%fused_computation.75 | convolution fusion | flops 3779592192 | bytes 28317696 | tf_op jit(solution)/shard_map/dot_general | solution.py:136
  232.1 10.7 %all-gather.10.cloned.1.call-done = bf16[1536,768]{1,0:T(8,128)(2,1)} async-done(((bf16[768,768]{1,0:T(8,128)(2,1)}), bf16[1536,768]{1,0:T(8,128)(2,1)}) %all-gather.10.cloned.1.call-update) | async-done | bytes 2359312 | tf_op jit(solution)/shard_map/all_gather | solution.py:151
  242.8 13.4 %convert_reduce_fusion = (f32[1536]{0:T(1024)}, bf16[1536,1536]{1,0:T(8,128)(2,1)S(1)}) fusion(f32[1536,1536]{1,0:T(8,128)} %get-tuple-element.398, f32[1536,1536]{1,0:T(8,128)} %get-tuple-element.429, bf16[1536,768]{1,0:T(8,128)(2,1)} %all-gather.10.cloned.1.call-done, bf16[1536,768]{1,0:T(8,128)(2,1)} %param.39), kind=kOutput, calls=%fused_computation.73 | convolution fusion | flops 3661625856 | bytes 28317696 | tf_op jit(solution)/shard_map/dot_general | solution.py:45
  258.3 5.4 fusion.109
  265.4 7.7 convolution_convert_fusion
  275.4 48.6 %reduce-scatter.5.cloned.1.call-done = f32[768,768]{0,1:T(8,128)} async-done(((f32[1536,768]{0,1:T(8,128)}), f32[768,768]{0,1:T(8,128)}) %reduce-scatter.5.cloned.1.call-update) | async-done | bytes 2359312 | tf_op jit(solution)/shard_map/reduce_scatter | solution.py:164
  323.9 3.1 multiply_reduce_fusion.1
  327.7 33.2 %reduce-scatter.3.cloned.1.call-done = bf16[768,768]{0,1:T(8,128)(2,1)} async-done(((bf16[1536,768]{0,1:T(8,128)(2,1)}), bf16[768,768]{0,1:T(8,128)(2,1)}) %reduce-scatter.3.cloned.1.call-update) | async-done | bytes 1179664 | tf_op jit(solution)/shard_map/reduce_scatter | solution.py:139
  360.8 3.9 fusion.102
  369.1 3.9 copy.56
  373.1 5.8 all_gather.25
  380.0 3.2 dynamic-slice_bitcast_fusion
  383.3 3.3 constant_dynamic-slice_fusion
  386.6 7.9 fusion.111
  394.5 5.7 fusion.112
  401.5 3.8 fusion.110
  407.6 102.6 %while.40 = (s32[]{:T(128)}, f32[12,768,64]{1,2,0:T(8,128)}, f32[12,768,1]{1,2,0:T(1,128)}, bf16[12,768,64]{2,1,0:T(8,128)(2,1)}, bf16[12,1536,64]{2,1,0:T(8,128...) while((s32[]{:T(128)}, f32[12,768,64]{1,2,0:T(8,128)}, ...), condition=%wide.region_14.15_spmd.clone, body=%wide.region_12.14_spmd.clone.sunk | while | flops 463650048 | bytes 25409164 | solution.py:191
  510.1 8.5 multiply_add_fusion.2
  518.6 4.8 all_gather.27
  526.3 152.9 %while.41 = (s32[]{:T(128)}, f32[12,768,64]{1,2,0:T(8,128)}, bf16[12,768,64]{1,2,0:T(8,128)(2,1)S(1)}, bf16[12,1536,64]{1,2,0:T(8,128)(2,1)}, bf16[12,768,64]{1,...) while((s32[]{:T(128)}, f32[12,768,64]{1,2,0:T(8,128)}, ...), condition=%wide.region_16.17_spmd.clone, body=%wide.region_15.16_spmd.clone.sunk | while | flops 613466112 | bytes 16073849 | solution.py:216
  527.0 4.4 subtract_exponential_fusion.4
  531.4 4.6 fusion.169
  539.7 4.5 subtract_exponential_fusion.4
  544.2 4.5 fusion.169
  552.5 4.4 subtract_exponential_fusion.4
  556.9 4.5 fusion.169
  565.2 4.4 subtract_exponential_fusion.4
  569.6 4.5 fusion.169
  577.8 4.4 subtract_exponential_fusion.4
  582.3 4.5 fusion.169
  586.8 3.3 fusion.170
  590.8 4.5 subtract_exponential_fusion.4
  595.3 4.6 fusion.169
  603.7 4.4 subtract_exponential_fusion.4
  608.1 4.6 fusion.169
  612.7 3.1 fusion.170
  616.5 4.4 subtract_exponential_fusion.4
  621.0 4.5 fusion.169
  629.2 4.4 subtract_exponential_fusion.4
  633.7 4.5 fusion.169
  642.0 4.4 subtract_exponential_fusion.4
  646.4 4.5 fusion.169
  654.6 4.4 subtract_exponential_fusion.4
  659.0 4.5 fusion.169
  667.2 4.4 subtract_exponential_fusion.4
  671.6 4.5 fusion.169
  679.1 8.9 multiply_add_fusion.1
  690.1 7.5 fusion.99
  698.3 34.4 %psum.46 = f32[1536]{0:T(1024)} all-reduce(f32[1536]{0:T(1024)S(1)} %copy-done.61), channel_id=1, replica_groups=mesh['dp'=16,'mlp'=2] {'dp'}, use_global_device_ids=true, to_apply=%region_35.36 | all-reduce | flops 1536 | bytes 12288 | tf_op jit(solution)/shard_map/psum | solution.py:254
  739.8 7.3 fusion.108
  747.1 3.2 copy.62
  766.5 37.4 %psum.42 = f32[7680]{0:T(1024)S(1)} all-reduce(f32[7680]{0:T(1024)} %constant_dynamic-update-slice_fusion), channel_id=1, replica_groups=mesh['dp'=16,'mlp'=2] {'dp','mlp'}, use_global_device_ids=true, to_apply=%region_30.31 | all-reduce | flops 7680 | bytes 61440 | tf_op jit(solution)/shard_map/psum | solution.py:253
  807.1 83.1 %all-reduce.13.cloned.1.call-done = (f32[768,2304]{1,0:T(8,128)}, f32[768,768]{1,0:T(8,128)}) async-done(((f32[768,2304]{1,0:T(8,128)}, f32[768,768]{1,0:T(8,128)}), (f32[768,2304]{1,0:T(8,128)}, f32[768,768]{1,0:T(8,128)})) %all-reduce.13.cloned.1.call-update) | async-done | bytes 9437200 | tf_op jit(solution)/shard_map/psum | solution.py:253
  890.2 6.6 copy.117
  (407 shorter events, 305.9 us)
Async XLA Ops:
  7.2 198.0 %copy-start = (bf16[768,1536]{1,0:T(8,128)(2,1)S(1)}, bf16[768,1536]{1,0:T(8,128)(2,1)}, u32[]{:S(2)}) copy-start(bf16[768,1536]{1,0:T(8,128)(2,1)} %param.37) | copy-start | bytes 7077892
  7.2 3.6 copy-start.43
  7.2 3.6 copy-start.62
  7.2 44.0 %all-gather.6.cloned.1.call-start = ((), (), s32[]{:S(2)}) async-start(), calls=%async_computation.2 | async-start | bytes 3538944 | tf_op jit(solution)/shard_map/all_gather | solution.py:96
  9.0 154.2 %copy-start.2 = (bf16[768,768]{0,1:T(8,128)(2,1)}, bf16[768,768]{0,1:T(8,128)(2,1)S(1)}, u32[]{:S(2)}) copy-start(bf16[768,768]{0,1:T(8,128)(2,1)S(1)} %copy.49) | copy-start | bytes 3538948
  9.2 7.0 copy-start.54
  12.3 192.8 %all-gather.8.cloned.1.call-start = ((), (), s32[]{:S(2)}) async-start(), calls=%async_computation.3 | async-start | bytes 3538944 | tf_op jit(solution)/shard_map/all_gather | solution.py:135
  18.3 44.5 %copy-start.28 = (f32[12,32]{1,0:T(8,128)}, f32[12,32]{1,0:T(8,128)S(1)}, u32[]{:S(2)}) copy-start(f32[12,32]{1,0:T(8,128)S(1)} %mul.348) | copy-start | bytes 4612
  19.0 3.7 copy-start.30
  19.8 3.0 copy-start.37
  19.8 3.0 copy-start.39
  34.9 2.8 copy-start.55
  35.0 2.8 copy-start.56
  57.5 3.6 copy-start.17
  81.1 6.6 copy-start.32
  87.7 75.5 %copy-start.69 = (f32[768]{0:T(1024)S(1)}, f32[768]{0:T(1024)}, u32[]{:S(2)}) copy-start(f32[768]{0:T(1024)} %param.34) | copy-start | bytes 9220
  167.5 37.6 %copy-start.68 = (f32[1536]{0:T(1024)S(1)}, f32[1536]{0:T(1024)}, u32[]{:S(2)}) copy-start(f32[1536]{0:T(1024)} %param.38) | copy-start | bytes 18436
  168.9 73.8 %all-gather.10.cloned.1.call-start = ((), (), s32[]{:S(2)}) async-start(), calls=%async_computation.5 | async-start | bytes 3538944 | tf_op jit(solution)/shard_map/all_gather | solution.py:151
  169.7 154.3 %reduce-scatter.5.cloned.1.call-start = ((), (), s32[]{:S(2)}) async-start(), calls=%async_computation.6 | async-start | bytes 7077888 | tf_op jit(solution)/shard_map/reduce_scatter | solution.py:164
  263.7 97.1 %reduce-scatter.3.cloned.1.call-start = ((), (), s32[]{:S(2)}) async-start(), calls=%async_computation.4 | async-start | bytes 3538944 | tf_op jit(solution)/shard_map/reduce_scatter | solution.py:139
  273.1 50.9 %copy-start.5 = (f32[768,768]{0,1:T(8,128)S(1)}, f32[768,768]{0,1:T(8,128)}, u32[]{:S(2)}) copy-start(f32[768,768]{0,1:T(8,128)} %copy-done.4) | copy-start | bytes 7077892
  273.1 251.5 %all-gather.12.cloned.1.call-start = ((), (), s32[]{:S(2)}) async-start(), calls=%async_computation.7 | async-start | bytes 3538944 | tf_op jit(solution)/shard_map/all_gather | solution.py:195
  273.7 251.0 %all-gather.14.cloned.1.call-start = ((), (), s32[]{:S(2)}) async-start(), calls=%async_computation.8 | async-start | bytes 7077888 | tf_op jit(solution)/shard_map/all_gather | solution.py:196
  323.9 3.1 copy-start.51
  366.2 2.9 copy-start.26
  369.1 9.8 %copy-start.12 = (bf16[1536,12,32]{0,2,1:T(8,128)(2,1)S(1)}, bf16[1536,12,32]{0,2,1:T(8,128)(2,1)}, u32[]{:S(2)}) copy-start(bf16[1536,12,32]{0,2,1:T(8,128)(2,1)} %copy-done.11) | copy-start | bytes 3538948
  369.1 9.8 %copy-start.14 = (bf16[1536,12,32]{0,2,1:T(8,128)(2,1)S(1)}, bf16[1536,12,32]{0,2,1:T(8,128)(2,1)}, u32[]{:S(2)}) copy-start(bf16[1536,12,32]{0,2,1:T(8,128)(2,1)} %copy-done.13) | copy-start | bytes 3538948
  373.0 434.1 %all-reduce.15.cloned.1.call-start = ((), (), s32[]{:S(2)}) async-start(), calls=%async_computation.10 | async-start | bytes 18874368 | tf_op jit(solution)/shard_map/psum | solution.py:254
  383.3 3.4 copy-start.65
  383.3 11.2 %slice-start.2 = ((s8[4718592]{0:T(1024)(128)(4,1)}), s8[4194304]{0:T(1024)(128)(4,1)S(1)}, s32[]{:S(2)}) async-start(s8[4718592]{0:T(1024)(128)(4,1)} %bitcast.174), calls=%async_computation.13 | async-start | bytes 8388608
  386.6 7.9 copy-start.66
  386.6 7.9 slice-start.3
  400.2 490.0 %all-reduce.13.cloned.1.call-start = ((), (), s32[]{:S(2)}) async-start(), calls=%async_computation.9 | async-start | bytes 18874368 | tf_op jit(solution)/shard_map/psum | solution.py:253
  407.6 102.6 %copy-start.16 = (f32[768,768]{0,1:T(8,128)S(1)}, f32[768,768]{0,1:T(8,128)}, u32[]{:S(2)}) copy-start(f32[768,768]{0,1:T(8,128)} %copy-done.15) | copy-start | bytes 7077892
  407.6 102.6 %copy-start.29 = (f32[12,32]{1,0:T(8,128)S(1)}, f32[12,32]{1,0:T(8,128)}, u32[]{:S(2)}) copy-start(f32[12,32]{1,0:T(8,128)} %copy-done.28) | copy-start | bytes 4612
  407.8 3.0 copy-start.33
  416.7 2.6 copy-start.33
  433.6 2.6 copy-start.33
  442.1 2.6 copy-start.33
  450.6 2.6 copy-start.33
  459.1 2.6 copy-start.33
  484.6 2.6 copy-start.33
  493.1 2.6 copy-start.33
  501.6 2.6 copy-start.33
  523.5 2.8 copy-start.10
  523.5 2.8 copy-start.34
  697.7 37.5 %copy-start.18 = (f32[768,12,32]{0,2,1:T(8,128)S(1)}, f32[768,12,32]{0,2,1:T(8,128)}, u32[]{:S(2)}) copy-start(f32[768,12,32]{0,2,1:T(8,128)} %get-tuple-element.407) | copy-start | bytes 3538948
  697.7 37.4 %copy-start.38 = (f32[768]{0:T(1024)S(1)}, f32[768]{0:T(1024)}, u32[]{:S(2)}) copy-start(f32[768]{0:T(1024)} %copy-done.37) | copy-start | bytes 9220
  697.7 37.4 %copy-start.40 = (f32[768]{0:T(1024)S(1)}, f32[768]{0:T(1024)}, u32[]{:S(2)}) copy-start(f32[768]{0:T(1024)} %copy-done.39) | copy-start | bytes 9220
  747.1 3.2 copy-start.3
  747.1 3.2 copy-start.36
  747.1 3.2 copy-start.44
  752.6 4.0 copy-start.22
  752.6 4.0 copy-start.24
  753.8 6.2 copy-start.59
  753.8 7.5 copy-start.58
  753.8 8.8 copy-start.57
  753.8 10.1 %copy-start.8 = (f32[768,768]{0,1:T(8,128)S(1)}, f32[768,768]{0,1:T(8,128)}, u32[]{:S(2)}) copy-start(f32[768,768]{0,1:T(8,128)} %copy-done.7) | copy-start | bytes 7077892
  753.9 10.0 %copy-start.47 = (f32[768]{0:T(1024)S(1)}, f32[768]{0:T(1024)}, u32[]{:S(2)}) copy-start(f32[768]{0:T(1024)} %copy-done.46) | copy-start | bytes 9220
  890.2 6.6 copy-start.25
  890.2 8.0 copy-start.19
  896.8 4.7 slice-start
  898.2 3.6 slice-start.1
  901.8 3.4 copy-start.1
  (31 other events, 49.7 us)
Sparse Core Ops, SparseCore 0:
  12.4 38.7 all-gather.5
  169.1 36.0 all-gather.7
  206.7 36.0 all-gather.9
  263.8 60.0 reduce-scatter.4
  326.0 34.7 reduce-scatter.2
  362.2 36.8 all-gather.11
  400.6 62.6 all-gather.13
  467.0 184.6 all-reduce.14
  697.8 192.3 all-reduce.12
where the time goes:
time: 920 us; the launch traced here: 912 us
  matrix products  389 us (42%)
  waiting for transfers between devices  225 us (24%)
  local copies, waits for them, and re-layouts  129 us (14%)
  blocking collectives  82.4 us (9%)
  other arithmetic  70 us (8%)
  between operations  14.7 us (2%)
    dot_general x52, matrix products, dot_transposed(): lax.dot_general(left, right, (((1,), (1,)), ((), ())), preferred_element_...  161 us
    dot_general x28, matrix products, transpose_dot(): lax.dot_general(left, right, (((0,), (0,)), ((), ())), preferred_element_...  116 us
    psum x1, waiting for transfers between devices, per_device(): shared = lax.psum((grad_w_qkv, grad_w_out, small_grads), ('dp', 'mlp'))  83.1 us
    unnamed x166, local copies, waits for them, and re-layouts  60.1 us
    reduce_scatter x1, waiting for transfers between devices, per_device(): lax.psum_scatter(dot_transposed(grad_pre, w_up), 'mlp', scatter_dimension...  48.6 us
    psum x1, blocking collectives, per_device(): shared = lax.psum((grad_w_qkv, grad_w_out, small_grads), ('dp', 'mlp'))  37.4 us
    all_gather x1, waiting for transfers between devices, per_device(): normed2_all = lax.all_gather(normed2, 'mlp', axis=0, tiled=True)  35.4 us
    psum x1, blocking collectives, per_device(): sharded = lax.psum((grad_w_up, grad_b_up, grad_w_down), 'dp')  34.4 us
  transfers between devices with their start and end apart: 9, of which 6 were waited for; matrix products, arithmetic and copies ran while one was open for 46% of the time, Pallas kernels for 0%

commit v1 on v0

v1 whole, which is shorter than its diff:
```python
from functools import partial

import jax
import jax.numpy as jnp
from jax import lax
from jax.experimental import pallas as pl
from jax.experimental.pallas import tpu as pltpu
from jax.sharding import PartitionSpec as P

H = 12
HD = 64
PAIRS = H // 2
LANES = 128
EPSILON = 1e-06
MOST = 576
SIDE = 24
KEY_TILE = 128
QUERY_TILE = 256
EDGE = -(-(MOST - 1) // KEY_TILE) * KEY_TILE
VMEM_LIMIT = 60 * 1024 * 1024
BF = jnp.bfloat16
F32 = jnp.float32


def dot(left, right):
    return jnp.dot(left, right, preferred_element_type=F32)


def dot_nt(left, right):
    return lax.dot_general(left, right, (((1,), (1,)), ((), ())), preferred_element_type=F32)


def dot_tn(left, right):
    return lax.dot_general(left, right, (((0,), (0,)), ((), ())), preferred_element_type=F32)


def split3(values):
    high = lax.reduce_precision(values, 8, 7)
    rest = values - high
    mid = lax.reduce_precision(rest, 8, 7)
    low = rest - mid
    return jnp.concatenate([high, mid, low], axis=0).astype(BF)


def rope_table(freqs):
    wide = jnp.concatenate([freqs.reshape(2, H, 1, HD // 2)] * 2, axis=2).reshape(2, H * HD)
    steps = jnp.arange(SIDE, dtype=F32)[:, None]
    row_angle = steps * wide[0][None]
    col_angle = steps * wide[1][None]
    row_part = jnp.concatenate([split3(jnp.cos(row_angle)), split3(jnp.sin(row_angle))], axis=1)
    col_part = jnp.concatenate([split3(jnp.cos(col_angle)), split3(jnp.sin(col_angle))], axis=1)
    zero = jnp.zeros_like(row_part)
    table = jnp.concatenate(
        [jnp.concatenate([row_part, zero], axis=1), jnp.concatenate([zero, col_part], axis=1)],
        axis=0,
    )
    return jnp.pad(table, ((0, 256 - table.shape[0]), (0, 0)))


def cos_sin(row_pos, col_pos, table, first, width):
    rows = row_pos.shape[0]
    full = H * HD
    lane = lax.broadcasted_iota(jnp.int32, (rows, 256), 1)
    part = lane % SIDE
    part = jnp.where(lane < 6 * SIDE, part, -1)
    hot = jnp.where(jnp.where(lane < 3 * SIDE, row_pos, col_pos) == part, 1.0, 0.0).astype(BF)
    parts = [dot(hot, table[:, k * full + first : k * full + first + width]) for k in range(4)]
    cos_r, sin_r, cos_c, sin_c = parts
    cosine = cos_r * cos_c - sin_r * sin_c
    sine = sin_r * cos_c + cos_r * sin_c
    lane_out = lax.broadcasted_iota(jnp.int32, (rows, width), 1)
    signed = jnp.where(lane_out % HD < HD // 2, -sine, sine)
    return cosine, signed


def swap_halves(slab):
    lane = lax.broadcasted_iota(jnp.int32, slab.shape, 1)
    return jnp.where(
        lane % HD < HD // 2,
        pltpu.roll(slab, LANES - HD // 2, 1),
        pltpu.roll(slab, HD // 2, 1),
    )


def input_kernel(with_query, x_ref, row_ref, col_ref, gain_ref, bias_ref, w_ref, b_ref, t_ref, *outs):
    width = x_ref.shape[1]
    if with_query:
        normed_ref, q_ref, k_ref, v_ref = outs
    else:
        normed_ref, k_ref, v_ref = outs
        q_ref = None
    values = x_ref[...].astype(F32)
    center = values - jnp.mean(values, axis=-1, keepdims=True)
    spread = jnp.mean(center * center, axis=-1, keepdims=True)
    normed = (center * lax.rsqrt(spread + EPSILON) * gain_ref[...] + bias_ref[...]).astype(BF)
    normed_ref[...] = normed
    row_pos = row_ref[...]
    col_pos = col_ref[...]
    for pair in range(PAIRS):
        cut = slice(pair * LANES, (pair + 1) * LANES)
        cosine, sine = cos_sin(row_pos, col_pos, t_ref, pair * LANES, LANES)
        for kind, out_ref in ((0, q_ref), (1, k_ref)):
            if out_ref is None:
                continue
            here = slice(kind * width + pair * LANES, kind * width + (pair + 1) * LANES)
            pre = dot(normed, w_ref[:, here]) + b_ref[:, here]
            out_ref[:, cut] = (pre * cosine + swap_halves(pre) * sine).astype(BF)
    v_ref[...] = (dot(normed, w_ref[:, 2 * width :]) + b_ref[:, 2 * width :]).astype(BF)


def input_stage(x, row_col, col_col, gain, bias, w_qkv, b_qkv, table, with_query, tile):
    rows, width = x.shape
    tiled = lambda cols: pl.BlockSpec((tile, cols), lambda i: (i, 0))
    whole = lambda a: pl.BlockSpec(a.shape, lambda i: (0, 0))
    outs = 4 if with_query else 3
    return pl.pallas_call(
        partial(input_kernel, with_query),
        grid=(rows // tile,),
        in_specs=[tiled(width), tiled(1), tiled(1)] + [whole(a) for a in (gain, bias, w_qkv, b_qkv, table)],
        out_specs=[tiled(width)] * outs,
        out_shape=[jax.ShapeDtypeStruct((rows, width), BF)] * outs,
        compiler_params=pltpu.CompilerParams(vmem_limit_bytes=VMEM_LIMIT),
        cost_estimate=pl.CostEstimate(
            flops=2 * rows * width * width * (4 if with_query else 3),
            bytes_accessed=int(w_qkv.size * 2 + rows * width * 2 * 5),
            transcendentals=0,
        ),
        name="ln_qkv_rope",
    )(x, row_col, col_col, gain, bias, w_qkv, b_qkv, table)


def head_lanes(shape, side):
    lane = lax.broadcasted_iota(jnp.int32, shape, 1)
    return (lane < HD) if side == 0 else (lane >= HD)


def visible(ids_ref, query_tile, key_tile):
    q0 = query_tile * QUERY_TILE
    k0 = key_tile * KEY_TILE
    return (ids_ref[0, k0] <= ids_ref[0, q0 + QUERY_TILE - 1]) & (
        ids_ref[0, k0 + KEY_TILE - 1] >= ids_ref[0, q0]
    )


def attend_kernel(ids_ref, q_ref, k_own_ref, k_edge_ref, v_own_ref, v_edge_ref, idk_ref, idq_ref,
                  mixed_ref, out_t_ref, lse_ref, key_sc, value_t_sc, peak_sc, total_sc, acc_sc):
    own = k_own_ref.shape[0]
    rows = key_sc.shape[0]
    step = pl.program_id(0)

    @pl.when(step == 0)
    def _():
        key_sc[0:own, :] = k_own_ref[...]
        key_sc[own:rows, :] = k_edge_ref[...]
        for start in range(0, rows, KEY_TILE):
            for pair in range(PAIRS):
                cut = slice(pair * LANES, (pair + 1) * LANES)
                if start < own:
                    block = v_own_ref[start : start + KEY_TILE, cut]
                else:
                    block = v_edge_ref[start - own : start - own + KEY_TILE, cut]
                value_t_sc[start // KEY_TILE, cut, :] = jnp.transpose(block.astype(F32)).astype(BF)

    peak_sc[...] = jnp.full(peak_sc.shape, -1e30, F32)
    total_sc[...] = jnp.zeros(total_sc.shape, F32)
    acc_sc[...] = jnp.zeros(acc_sc.shape, F32)
    scale = HD ** (-0.5)

    @pl.loop(0, rows // KEY_TILE)
    def _(tile):
        @pl.when(visible(ids_ref, step, tile))
        def _():
            k0 = pl.multiple_of(tile * KEY_TILE, KEY_TILE)
            allowed = idk_ref[pl.ds(k0, KEY_TILE), :] == idq_ref[...]
            for head in range(H):
                pair, side = head // 2, head % 2
                cut = slice(pair * LANES, (pair + 1) * LANES)
                query = q_ref[:, cut]
                query = jnp.where(head_lanes(query.shape, side), query * BF(scale), BF(0))
                scores = dot_nt(key_sc[pl.ds(k0, KEY_TILE), cut], query)
                scores = jnp.where(allowed, scores, -1e30)
                before = peak_sc[head : head + 1, :]
                peak = jnp.maximum(before, jnp.max(scores, axis=0, keepdims=True))
                expo = jnp.exp(scores - peak)
                fade = jnp.exp(before - peak)
                peak_sc[head : head + 1, :] = peak
                total_sc[head : head + 1, :] = fade * total_sc[head : head + 1, :] + jnp.sum(
                    expo, axis=0, keepdims=True
                )
                part = slice(head * HD, (head + 1) * HD)
                acc_sc[part, :] = fade * acc_sc[part, :] + dot(value_t_sc[tile, part, :], expo.astype(BF))

    lse_ref[...] = peak_sc[...] + jnp.log(jnp.maximum(total_sc[...], 1e-30))
    for head in range(H):
        part = slice(head * HD, (head + 1) * HD)
        acc_sc[part, :] = acc_sc[part, :] / total_sc[head : head + 1, :]
    out_t_ref[...] = acc_sc[...]
    for pair in range(PAIRS):
        cut = slice(pair * LANES, (pair + 1) * LANES)
        mixed_ref[:, cut] = jnp.transpose(acc_sc[cut, :]).astype(BF)


def attend(ids, q, k_own, k_edge, v_own, v_edge, id_col, id_row):
    own, width = q.shape
    rows = own + k_edge.shape[0]
    whole = lambda a: pl.BlockSpec(a.shape, lambda i: (0, 0))
    return pl.pallas_call(
        attend_kernel,
        grid=(own // QUERY_TILE,),
        in_specs=[
            pl.BlockSpec(memory_space=pltpu.SMEM),
            pl.BlockSpec((QUERY_TILE, width), lambda i: (i, 0)),
            whole(k_own), whole(k_edge), whole(v_own), whole(v_edge), whole(id_col),
            pl.BlockSpec((1, QUERY_TILE), lambda i: (0, i)),
        ],
        out_specs=[
            pl.BlockSpec((QUERY_TILE, width), lambda i: (i, 0)),
            pl.BlockSpec((width, QUERY_TILE), lambda i: (0, i)),
            pl.BlockSpec((16, QUERY_TILE), lambda i: (0, i)),
        ],
        out_shape=[
            jax.ShapeDtypeStruct((own, width), BF),
            jax.ShapeDtypeStruct((width, own), F32),
            jax.ShapeDtypeStruct((16, own), F32),
        ],
        scratch_shapes=[
            pltpu.VMEM((rows, width), BF),
            pltpu.VMEM((rows // KEY_TILE, width, KEY_TILE), BF),
            pltpu.VMEM((16, QUERY_TILE), F32),
            pltpu.VMEM((16, QUERY_TILE), F32),
            pltpu.VMEM((width, QUERY_TILE), F32),
        ],
        compiler_params=pltpu.CompilerParams(vmem_limit_bytes=VMEM_LIMIT),
        cost_estimate=pl.CostEstimate(
            flops=4 * own * rows * width, bytes_accessed=int(rows * width * 8), transcendentals=own * rows * H // 2
        ),
        name="attend",
    )(ids, q, k_own, k_edge, v_own, v_edge, id_col, id_row)


def unrotate(grad, rotated, row_pos, col_pos, table, first):
    cosine, sine = cos_sin(row_pos, col_pos, table, first, LANES)
    lane = lax.broadcasted_iota(jnp.int32, grad.shape, 1)
    turned = swap_halves(rotated)
    angle = grad * jnp.where(lane % HD < HD // 2, -turned, turned)
    return grad * cosine - swap_halves(grad) * sine, angle


def attend_back_kernel(ids_ref, q_ref, g_ref, k_own_ref, k_edge_ref, v_own_ref, v_edge_ref, idk_ref,
                       idq_ref, out_t_ref, lse_ref, row_ref, col_ref, rowq_ref, colq_ref, t_ref,
                       dq_ref, dk_ref, dv_ref, freq_ref, sums_ref,
                       key_sc, value_sc, key_t_sc, dk_sc, dv_sc, dq_t_sc, delta_sc):
    own, width = k_own_ref.shape
    rows = key_sc.shape[0]
    step = pl.program_id(0)
    scale = HD ** (-0.5)

    @pl.when(step == 0)
    def _():
        key_sc[0:own, :] = k_own_ref[...]
        key_sc[own:rows, :] = k_edge_ref[...]
        value_sc[0:own, :] = v_own_ref[...]
        value_sc[own:rows, :] = v_edge_ref[...]
        for start in range(0, rows, KEY_TILE):
            for pair in range(PAIRS):
                cut = slice(pair * LANES, (pair + 1) * LANES)
                if start < own:
                    block = k_own_ref[start : start + KEY_TILE, cut]
                else:
                    block = k_edge_ref[start - own : start - own + KEY_TILE, cut]
                key_t_sc[start // KEY_TILE, cut, :] = jnp.transpose(block.astype(F32)).astype(BF)
        dk_sc[...] = jnp.zeros(dk_sc.shape, F32)
        dv_sc[...] = jnp.zeros(dv_sc.shape, F32)
        freq_ref[...] = jnp.zeros(freq_ref.shape, F32)
        sums_ref[...] = jnp.zeros(sums_ref.shape, F32)

    dq_t_sc[...] = jnp.zeros(dq_t_sc.shape, F32)
    for pair in range(PAIRS):
        cut = slice(pair * LANES, (pair + 1) * LANES)
        grad_t = jnp.transpose(g_ref[:, cut].astype(F32)) * out_t_ref[cut, :]
        for side in range(2):
            delta_sc[2 * pair + side : 2 * pair + side + 1, :] = jnp.sum(
                grad_t[side * HD : (side + 1) * HD, :], axis=0, keepdims=True
            )

    @pl.loop(0, rows // KEY_TILE)
    def _(tile):
        @pl.when(visible(ids_ref, step, tile))
        def _():
            k0 = pl.multiple_of(tile * KEY_TILE, KEY_TILE)
            allowed = idk_ref[pl.ds(k0, KEY_TILE), :] == idq_ref[...]
            for pair in range(PAIRS):
                cut = slice(pair * LANES, (pair + 1) * LANES)
                keys = key_sc[pl.ds(k0, KEY_TILE), cut]
                values = value_sc[pl.ds(k0, KEY_TILE), cut]
                add_k = None
                add_v = None
                for side in range(2):
                    head = 2 * pair + side
                    query = q_ref[:, cut]
                    mine = head_lanes(query.shape, side)
                    query = jnp.where(mine, query * BF(scale), BF(0))
                    grad = jnp.where(mine, g_ref[:, cut], BF(0))
                    scores = dot_nt(keys, query)
                    weights = jnp.where(allowed, jnp.exp(scores - lse_ref[head : head + 1, :]), 0.0)
                    grad_w = dot_nt(values, grad)
                    grad_s = (weights * (grad_w - delta_sc[head : head + 1, :])).astype(BF)
                    one_v = dot(weights.astype(BF), grad)
                    one_k = dot(grad_s, query)
                    add_v = one_v if side == 0 else add_v + one_v
                    add_k = one_k if side == 0 else add_k + one_k
                    part = slice(head * HD, (head + 1) * HD)
                    dq_t_sc[part, :] += dot(key_t_sc[tile, part, :], grad_s)
                dv_sc[pl.ds(k0, KEY_TILE), cut] += add_v
                dk_sc[pl.ds(k0, KEY_TILE), cut] += add_k

    row_f = rowq_ref[...].astype(F32)
    col_f = colq_ref[...].astype(F32)
    for pair in range(PAIRS):
        cut = slice(pair * LANES, (pair + 1) * LANES)
        grad = jnp.transpose(dq_t_sc[cut, :]) * scale
        back, angle = unrotate(grad, q_ref[:, cut].astype(F32), rowq_ref[...], colq_ref[...], t_ref, pair * LANES)
        back = back.astype(BF)
        dq_ref[:, cut] = back
        freq_ref[0:1, cut] += jnp.sum(angle * row_f, axis=0, keepdims=True)
        freq_ref[1:2, cut] += jnp.sum(angle * col_f, axis=0, keepdims=True)
        sums_ref[0:1, cut] += jnp.sum(back.astype(F32), axis=0, keepdims=True)

    @pl.when(step == pl.num_programs(0) - 1)
    def _():
        @pl.loop(0, rows // KEY_TILE)
        def _(tile):
            k0 = pl.multiple_of(tile * KEY_TILE, KEY_TILE)
            here = pl.ds(k0, KEY_TILE)
            row_pos = row_ref[here, :]
            col_pos = col_ref[here, :]
            for pair in range(PAIRS):
                cut = slice(pair * LANES, (pair + 1) * LANES)
                back, angle = unrotate(
                    dk_sc[here, cut], key_sc[here, cut].astype(F32), row_pos, col_pos, t_ref, pair * LANES
                )
                back = back.astype(BF)
                dk_ref[here, cut] = back
                freq_ref[0:1, cut] += jnp.sum(angle * row_pos.astype(F32), axis=0, keepdims=True)
                freq_ref[1:2, cut] += jnp.sum(angle * col_pos.astype(F32), axis=0, keepdims=True)
                sums_ref[1:2, cut] += jnp.sum(back.astype(F32), axis=0, keepdims=True)
                grad_v = dv_sc[here, cut].astype(BF)
                dv_ref[here, cut] = grad_v
                sums_ref[2:3, cut] += jnp.sum(grad_v.astype(F32), axis=0, keepdims=True)


def attend_back(ids, q, grad_mixed, k_own, k_edge, v_own, v_edge, id_col, id_row, out_t, lse, row_col, col_col, table):
    own, width = q.shape
    rows = own + k_edge.shape[0]
    whole = lambda a: pl.BlockSpec(a.shape, lambda i: (0, 0))
    tiled = pl.BlockSpec((QUERY_TILE, width), lambda i: (i, 0))
    across = lambda n: pl.BlockSpec((n, QUERY_TILE), lambda i: (0, i))
    thin = pl.BlockSpec((QUERY_TILE, 1), lambda i: (i, 0))
    full = pl.BlockSpec((rows, width), lambda i: (0, 0))
    small = pl.BlockSpec((8, width), lambda i: (0, 0))
    return pl.pallas_call(
        attend_back_kernel,
        grid=(own // QUERY_TILE,),
        in_specs=[
            pl.BlockSpec(memory_space=pltpu.SMEM), tiled, tiled,
            whole(k_own), whole(k_edge), whole(v_own), whole(v_edge), whole(id_col),
            across(1), across(width), across(16), whole(row_col), whole(col_col), thin, thin, whole(table),
        ],
        out_specs=[tiled, full, full, small, small],
        out_shape=[
            jax.ShapeDtypeStruct((own, width), BF),
            jax.ShapeDtypeStruct((rows, width), BF),
            jax.ShapeDtypeStruct((rows, width), BF),
            jax.ShapeDtypeStruct((8, width), F32),
            jax.ShapeDtypeStruct((8, width), F32),
        ],
        scratch_shapes=[
            pltpu.VMEM((rows, width), BF),
            pltpu.VMEM((rows, width), BF),
            pltpu.VMEM((rows // KEY_TILE, width, KEY_TILE), BF),
            pltpu.VMEM((rows, width), F32),
            pltpu.VMEM((rows, width), F32),
            pltpu.VMEM((width, QUERY_TILE), F32),
            pltpu.VMEM((16, QUERY_TILE), F32),
        ],
        compiler_params=pltpu.CompilerParams(vmem_limit_bytes=VMEM_LIMIT),
        cost_estimate=pl.CostEstimate(
            flops=10 * own * rows * width, bytes_accessed=int(rows * width * 16), transcendentals=own * rows * H // 2
        ),
        name="attend_back",
    )(ids, q, grad_mixed, k_own, k_edge, v_own, v_edge, id_col, id_row, out_t, lse,
      row_col, col_col, row_col, col_col, table)


def ffn_kernel(n2_ref, g_ref, up_ref, b_ref, down_ref, hidden_ref, grad_ref, out_ref, back_ref, sums_ref, out_sc, back_sc):
    step = pl.program_id(0)

    @pl.when(step == 0)
    def _():
        out_sc[...] = jnp.zeros(out_sc.shape, F32)
        back_sc[...] = jnp.zeros(back_sc.shape, F32)

    rows = n2_ref.shape[0]
    block = 256
    sums_ref[...] = jnp.zeros(sums_ref.shape, F32)

    @pl.loop(0, rows // block)
    def _(i):
        here = pl.ds(pl.multiple_of(i * block, block), block)
        pre = dot(n2_ref[here, :], up_ref[...]) + b_ref[...]
        grad_hidden = dot_nt(g_ref[here, :], down_ref[...])
        phi = 0.5 * (1.0 + lax.erf(pre * (0.5 ** 0.5)))
        hidden = (pre * phi).astype(BF)
        slope = phi + pre * (jnp.exp(pre * pre * (-0.5)) * 0.3989422804014327)
        grad_pre = (grad_hidden * slope).astype(BF)
        hidden_ref[here, :] = hidden
        grad_ref[here, :] = grad_pre
        out_sc[here, :] += dot(hidden, down_ref[...])
        back_sc[here, :] += dot_nt(grad_pre, up_ref[...])
        sums_ref[0:1, :] += jnp.sum(grad_pre.astype(F32), axis=0, keepdims=True)

    @pl.when(step == pl.num_programs(0) - 1)
    def _():
        out_ref[...] = out_sc[...].astype(out_ref.dtype)
        back_ref[...] = back_sc[...].astype(back_ref.dtype)


def ffn(n2, g, w_up, b_up, w_down, dtype):
    rows, width = n2.shape
    units = w_up.shape[1]
    block = 256
    whole = pl.BlockSpec((rows, width), lambda j: (0, 0))
    across = pl.BlockSpec((rows, block), lambda j: (0, j))
    return pl.pallas_call(
        ffn_kernel,
        grid=(units // block,),
        in_specs=[
            whole, whole,
            pl.BlockSpec((width, block), lambda j: (0, j)),
            pl.BlockSpec((1, block), lambda j: (0, j)),
            pl.BlockSpec((block, width), lambda j: (j, 0)),
        ],
        out_specs=[across, across, whole, whole, pl.BlockSpec((8, block), lambda j: (0, j))],
        out_shape=[
            jax.ShapeDtypeStruct((rows, units), BF),
            jax.ShapeDtypeStruct((rows, units), BF),
            jax.ShapeDtypeStruct((rows, width), dtype),
            jax.ShapeDtypeStruct((rows, width), dtype),
            jax.ShapeDtypeStruct((8, units), F32),
        ],
        scratch_shapes=[pltpu.VMEM((rows, width), F32), pltpu.VMEM((rows, width), F32)],
        compiler_params=pltpu.CompilerParams(vmem_limit_bytes=VMEM_LIMIT),
        cost_estimate=pl.CostEstimate(
            flops=8 * rows * width * units, bytes_accessed=int(4 * width * units + 4 * rows * units + 8 * rows * width),
            transcendentals=2 * rows * units,
        ),
        name="ffn",
    )(n2, g, w_up, b_up, w_down)


def norm_back(values, gain, grad):
    center = values - jnp.mean(values, axis=-1, keepdims=True)
    inverse = lax.rsqrt(jnp.mean(center * center, axis=-1, keepdims=True) + EPSILON)
    unit = center * inverse
    scaled = grad * gain
    first = jnp.mean(scaled, axis=-1, keepdims=True)
    second = jnp.mean(scaled * unit, axis=-1, keepdims=True)
    back = (scaled - first - unit * second) * inverse
    return back, jnp.sum(grad * unit, axis=0), jnp.sum(grad, axis=0)


def per_device(
    axes, patches, image_of_patch, patch_row, patch_col, ln1_gain, ln1_bias, w_qkv, b_qkv, freqs, w_out, b_out,
    ln2_gain, ln2_bias, w_up, b_up, w_down, b_down, out_cotangent,
):
    own, width = patches.shape
    me = lax.axis_index("mlp")
    other = [(0, 1), (1, 0)]
    swap = lambda a: lax.ppermute(a, "mlp", other)
    edge = min(own, EDGE)
    mine_start = jnp.where(me == 0, own - edge, 0)
    edge_start = jnp.where(me == 0, own, own - edge)
    x_edge = swap(lax.dynamic_slice_in_dim(patches, mine_start, edge))
    g_other = swap(out_cotangent)

    def local(a):
        return jnp.concatenate(
            [lax.dynamic_slice_in_dim(a[0], me * own, own), lax.dynamic_slice_in_dim(a[0], edge_start, edge)]
        )

    ids = local(image_of_patch)
    row_pos = local(patch_row)[:, None]
    col_pos = local(patch_col)[:, None]
    id_row = ids[None, :]
    id_col = ids[:, None]
    id_own = id_row[:, :own]
    table = rope_table(freqs)
    gain1, bias1, bias_qkv = ln1_gain[None], ln1_bias[None], b_qkv[None]
    normed, q, k_own, v_own = input_stage(
        patches, row_pos[:own], col_pos[:own], gain1, bias1, w_qkv, bias_qkv, table, True, 256
    )
    normed_edge, k_edge, v_edge = input_stage(
        x_edge, row_pos[own:], col_pos[own:], gain1, bias1, w_qkv, bias_qkv, table, False, edge // 2
    )
    mixed, out_t, lse = attend(id_row, q, k_own, k_edge, v_own, v_edge, id_col, id_own)
    inputs = patches.astype(F32)
    middle = inputs + dot(mixed, w_out) + b_out
    center = middle - jnp.mean(middle, axis=-1, keepdims=True)
    spread = jnp.mean(center * center, axis=-1, keepdims=True)
    normed2 = (center * lax.rsqrt(spread + EPSILON) * ln2_gain + ln2_bias).astype(BF)
    n2_other = swap(normed2)
    bias_up = b_up[None]
    hid_a, gp_a, out_a, back_a, sum_a = ffn(normed2, out_cotangent, w_up, bias_up, w_down, F32)
    hid_b, gp_b, out_b, back_b, sum_b = ffn(n2_other, g_other, w_up, bias_up, w_down, BF)
    back_in = swap(back_b)
    out_in = swap(out_b)
    grad_b_up = sum_a[0] + sum_b[0]
    grad_w_up = (dot_tn(normed2, gp_a) + dot_tn(n2_other, gp_b)).astype(BF)
    grad_w_down = (dot_tn(hid_a, out_cotangent) + dot_tn(hid_b, g_other)).astype(BF)
    block_out = (middle + out_a + out_in.astype(F32) + b_down).astype(BF)
    grad_out = out_cotangent.astype(F32)
    grad_n2 = back_a + back_in.astype(F32)
    from_norm2, grad_ln2_gain, grad_ln2_bias = norm_back(middle, ln2_gain, grad_n2)
    grad_middle = grad_out + from_norm2
    grad_b_down = jnp.sum(grad_out, axis=0)
    grad_attended = grad_middle.astype(BF)
    grad_b_out = jnp.sum(grad_attended.astype(F32), axis=0)
    grad_w_out = dot_tn(mixed, grad_attended).astype(BF)
    grad_mixed = dot_nt(grad_attended, w_out).astype(BF)
    dq, dk, dv, freq, sums = attend_back(
        id_row, q, grad_mixed, k_own, k_edge, v_own, v_edge, id_col, id_own, out_t, lse, row_pos, col_pos, table
    )
    w_q, w_k, w_v = (w_qkv[:, i * width : (i + 1) * width] for i in range(3))
    gn_edge = (dot_nt(dk[own:], w_k) + dot_nt(dv[own:], w_v)).astype(BF)
    gn_in = swap(gn_edge)
    grad_w_qkv = jnp.concatenate(
        [
            dot_tn(normed, dq).astype(BF),
            (dot_tn(normed, dk[:own]) + dot_tn(normed_edge, dk[own:])).astype(BF),
            (dot_tn(normed, dv[:own]) + dot_tn(normed_edge, dv[own:])).astype(BF),
        ],
        axis=1,
    )
    gn = dot_nt(dq, w_q) + dot_nt(dk[:own], w_k) + dot_nt(dv[:own], w_v)
    spread_in = lax.dynamic_update_slice_in_dim(jnp.zeros((own, width), BF), gn_in, mine_start, 0)
    grad_normed = gn + spread_in.astype(F32)
    from_norm1, grad_ln1_gain, grad_ln1_bias = norm_back(inputs, ln1_gain, grad_normed)
    grad_patches = (grad_middle + from_norm1).astype(BF)
    grad_freqs = jnp.sum(freq[:2].reshape(2, H, 2, HD // 2), axis=2)
    small = jnp.concatenate(
        [
            grad_ln1_gain, grad_ln1_bias, sums[:3].reshape(-1), grad_freqs.reshape(-1),
            grad_b_out, grad_ln2_gain, grad_ln2_bias, grad_b_down,
        ]
    )
    everyone = axes + ("mlp",)
    grad_w_up, grad_w_down = lax.psum((grad_w_up, grad_w_down), axes)
    grad_w_out = lax.psum(grad_w_out, everyone)
    grad_w_qkv = lax.psum(grad_w_qkv, everyone)
    units = b_up.shape[0]
    slots = jnp.zeros((2 * units,), F32)
    slots = lax.dynamic_update_slice_in_dim(slots, grad_b_up, me * units, 0)
    total = lax.psum(jnp.concatenate([small, slots]), everyone)
    grad_b_up = lax.dynamic_slice_in_dim(total, small.shape[0] + me * units, units)
    return (
        block_out, grad_patches, total[0:width], total[width : 2 * width], grad_w_qkv.astype(F32),
        total[2 * width : 5 * width], total[5 * width : 6 * width].reshape(2, width // 2), grad_w_out.astype(F32),
        total[6 * width : 7 * width], total[7 * width : 8 * width], total[8 * width : 9 * width],
        grad_w_up.astype(F32), grad_b_up, grad_w_down.astype(F32), total[9 * width : 10 * width],
    )


def solution(mesh):
    rows = P(("dp", "mlp"), None)
    group = P("dp", None)
    in_specs = (rows, group, group, group) + (P(),) * 9 + (P(None, "mlp"), P("mlp"), P("mlp", None), P(), rows)
    out_specs = (rows, rows) + (P(),) * 9 + (P(None, "mlp"), P("mlp"), P("mlp", None), P())
    return jax.shard_map(
        partial(per_device, ("dp",)), mesh=mesh, in_specs=in_specs, out_specs=out_specs, check_vma=False
    )
```

time: 920 us -> 469 us (0.51)
  matrix products: 389 us -> 51.8 us
  Pallas kernels: 0 us -> 175 us
  waiting for transfers between devices: 225 us -> 90.2 us
  local copies, waits for them, and re-layouts: 129 us -> 45.2 us
  blocking collectives: 82.4 us -> 43.6 us
  other arithmetic: 70 us -> 34.8 us
    dot_general x109 -> x17, matrix products: 389 us -> 51.8 us  [the longest x10 31.9 us: dot_tn(): lax.dot_general(left, right, (((0,), (0,)), ((), ())), preferred_element_...]
    pallas_call x0 -> x6, Pallas kernels: none -> 175 us  [the longest x1 74.6 us: attend_back(): pl.pallas_call(attend_back_kernel, grid=(own // QUERY_TILE,), in_specs=[p...]
    reduce_scatter x2 -> x0, waiting for transfers between devices: 81.7 us -> none  [the longest x1 48.6 us: per_device(): lax.psum_scatter(dot_transposed(grad_pre, w_up), 'mlp', scatter_dimension...]
    all_gather x5 -> x0, waiting for transfers between devices: 59 us -> none  [the longest x1 35.4 us: per_device(): normed2_all = lax.all_gather(normed2, 'mlp', axis=0, tiled=True)]
    unnamed x166 -> x96, local copies, waits for them, and re-layouts: 60.1 us -> 19 us
    psum x2 -> x1, blocking collectives: 71.8 us -> 43.6 us  [per_device(): total = lax.psum(jnp.concatenate([small, slots]), everyone)]
    ppermute x0 -> x6, waiting for transfers between devices: none -> 26.7 us  [per_device(): swap = lambda a: lax.ppermute(a, 'mlp', other)]
    psum x2, waiting for transfers between devices: 83.1 us -> 63.5 us  [the longest x1 63.5 us: per_device(): grad_w_qkv = lax.psum(grad_w_qkv, everyone)]
  transfers between devices with their start and end apart: 9 -> 8, of which waited for: 6 -> 3; matrix products, arithmetic and copies ran while one was open for 46% -> 26% of each run, Pallas kernels for 0% -> 34%
where the time goes in v1:
time: 469 us; the launch traced here: 461 us
  Pallas kernels  175 us (37%)
  waiting for transfers between devices  90.2 us (19%)
  matrix products  51.8 us (11%)
  local copies, waits for them, and re-layouts  45.2 us (10%)
  blocking collectives  43.6 us (9%)
  other arithmetic  34.8 us (7%)
  between operations  14.8 us (3%)
  starting transfers between devices  5.38 us (1%)
    pallas_call x1, Pallas kernels, attend_back(): pl.pallas_call(attend_back_kernel, grid=(own // QUERY_TILE,), in_specs=[p...  74.6 us
    psum x1, waiting for transfers between devices, per_device(): grad_w_qkv = lax.psum(grad_w_qkv, everyone)  63.5 us
    psum x1, blocking collectives, per_device(): total = lax.psum(jnp.concatenate([small, slots]), everyone)  43.6 us
    pallas_call x1, Pallas kernels, attend(): pl.pallas_call(attend_kernel, grid=(own // QUERY_TILE,), in_specs=[pl.Blo...  43 us
    pallas_call x2, Pallas kernels, ffn(): pl.pallas_call(ffn_kernel, grid=(units // block,), in_specs=[whole, whole...  36.1 us
    dot_general x10, matrix products, dot_tn(): lax.dot_general(left, right, (((0,), (0,)), ((), ())), preferred_element_...  31.9 us
    ppermute x6, waiting for transfers between devices, per_device(): swap = lambda a: lax.ppermute(a, 'mlp', other)  26.7 us
    pallas_call x2, Pallas kernels, input_stage(): pl.pallas_call(partial(input_kernel, with_query), grid=(rows // tile,), i...  21.3 us
  transfers between devices with their start and end apart: 8, of which 3 were waited for; matrix products, arithmetic and copies ran while one was open for 26% of the time, Pallas kernels for 34%

profile of v1, /device:TPU:0, one launch (start us, length us, event | category | flops | bytes accessed | tf_op | source)
XLA Modules:
  0.0 460.8 jit_solution(9227431726565210195)
XLA Ops:
  7.3 1.4 constant_dynamic-slice_fusion.2
  8.7 3.1 collective-permute-start
  14.8 1.1 broadcast_in_dim.61.idk_ref
  16.4 0.9 copy.37.row_ref
  17.3 0.9 copy.38.col_ref
  20.1 0.9 copy.39.row_ref
  21.0 0.9 copy.40.col_ref
  23.1 1.2 broadcast_in_dim.62.row_ref.rowq_ref
  24.2 1.2 broadcast_in_dim.63.col_ref.colq_ref
  25.4 1.2 reduce-precision_convert_fusion.3
  26.7 5.3 %fusion.31.t_ref = bf16[256,3072]{1,0:T(8,128)(2,1)} fusion(bf16[72,1536]{1,0:T(8,128)(2,1)S(1)} %broadcast_in_dim.26, bf16[24,768]{1,0:T(8,128)(2,1)} %get-tuple-element.139, bf16[24,768]{1,0:T(8,128)(2,1)S(1)} %get-tuple-element.137, bf16[24,768]{1,0:T(8,128)(2,1)S(1)} %get-tuple-element.135, bf16[24,768]{1,0:T(8,128)(2,1)S(1)} %get-tuple-element.138, ...), kind=kLoop, calls=%fused_computation.54 | loop fusion | flops 33816576 | bytes 2236416 | tf_op jit(solution)/shard_map/concatenate | solution.py:53
  33.0 12.3 %ln_qkv_rope.2 = (bf16[768,768]{1,0:T(8,128)(2,1)}, bf16[768,768]{1,0:T(8,128)(2,1)}, bf16[768,768]{1,0:T(8,128)(2,1)}, bf16[768,768]{1,0:T(8,128)(2,1)}) custom-call(bf16[768,768]{1,0:T(8,128)(2,1)} %x_ref.1, s32[768,1]{1,0:T(8,128)} %copy.37.row_ref, s32[768,1]{1,0:T(8,128)} %copy.38.col_ref, f32[1,768]{1,0:T(1,128)} %broadcast_in_dim.23.gain_ref, ...), custom_call_target="tpu_custom_call" | custom-call | flops 3623878656 | bytes 9437184 | tf_op jit(solution)/shard_map/ln_qkv_rope/pallas_call | solution.py:116
  45.3 9.0 %ln_qkv_rope.3 = (bf16[640,768]{1,0:T(8,128)(2,1)}, bf16[640,768]{1,0:T(8,128)(2,1)}, bf16[640,768]{1,0:T(8,128)(2,1)}) custom-call(bf16[640,768]{1,0:T(8,128)(2,1)} %collective-permute-done.x_ref, s32[640,1]{1,0:T(8,128)} %copy.39.row_ref, s32[640,1]{1,0:T(8,128)} %copy.40.col_ref, f32[1,768]{1,0:T(1,128)} %broadcast_in_dim.23.gain_ref, ...), custom_call_target="tpu_custom_call" | custom-call | flops 2264924160 | bytes 8454144 | tf_op jit(solution)/shard_map/ln_qkv_rope/pallas_call | solution.py:116
  54.3 43.0 %attend.1 = (bf16[768,768]{1,0:T(8,128)(2,1)}, f32[768,768]{1,0:T(8,128)}, f32[16,768]{1,0:T(8,128)}) custom-call(s32[1,1408]{1,0:T(1,128)} %copy-done.22, bf16[768,768]{1,0:T(8,128)(2,1)} %get-tuple-element.40.q_ref, bf16[768,768]{1,0:T(8,128)(2,1)} %get-tuple-element.41.k_own_ref, bf16[640,768]{1,0:T(8,128)(2,1)} %get-tuple-element.42.k_edge_ref, ...), custom_call_target="tpu_custom_call" | custom-call | flops 3321888768 | bytes 8650752 | tf_op jit(solution)/shard_map/attend/pallas_call | solution.py:207
  97.3 2.8 fusion.79
  100.8 1.4 add_convert_fusion.5.n2_ref
  102.3 18.6 %ffn.2 = (bf16[768,1536]{1,0:T(8,128)(2,1)}, bf16[768,1536]{1,0:T(8,128)(2,1)}, f32[768,768]{1,0:T(8,128)}, f32[768,768]{1,0:T(8,128)}, f32[8,1536]{1,0:T(8,128)}) custom-call(bf16[768,768]{1,0:T(8,128)(2,1)} %add_convert_fusion.5.n2_ref, bf16[768,768]{1,0:T(8,128)(2,1)} %g_ref.1, bf16[768,1536]{1,0:T(8,128)(2,1)} %up_ref.3, ...), custom_call_target="tpu_custom_call" | custom-call | flops 7247757312 | bytes 14155776 | tf_op jit(solution)/shard_map/ffn/pallas_call | solution.py:434
  120.9 6.4 %fusion.80 = f32[768,1536]{1,0:T(8,128)} fusion(bf16[768,768]{1,0:T(8,128)(2,1)} %add_convert_fusion.5.n2_ref, bf16[768,1536]{1,0:T(8,128)(2,1)} %get-tuple-element.61), kind=kOutput, calls=%fused_computation.155 | convolution fusion | flops 1811939328 | bytes 8257536 | tf_op jit(solution)/shard_map/dot_general | solution.py:34
  127.3 4.3 fusion.81
  131.6 17.5 %ffn.3 = (bf16[768,1536]{1,0:T(8,128)(2,1)}, bf16[768,1536]{1,0:T(8,128)(2,1)}, bf16[768,768]{1,0:T(8,128)(2,1)}, bf16[768,768]{1,0:T(8,128)(2,1)}, f32[8,1536]{1,0:T(8,128)}) custom-call(bf16[768,768]{1,0:T(8,128)(2,1)} %collective-permute-done.1.n2_ref, bf16[768,768]{1,0:T(8,128)(2,1)} %collective-permute-done.2.g_ref, bf16[768,1536]{1,0:T(8,128)(2,1)} %up_ref.3, ...), custom_call_target="tpu_custom_call" | custom-call | flops 7247757312 | bytes 14155776 | tf_op jit(solution)/shard_map/ffn/pallas_call | solution.py:434
  149.1 2.1 collective-permute-start.4
  151.2 7.0 %add_convert_fusion.1 = bf16[768,1536]{1,0:T(8,128)(2,1)} fusion(f32[768,1536]{1,0:T(8,128)} %fusion.80, bf16[768,768]{1,0:T(8,128)(2,1)} %collective-permute-done.1.n2_ref, bf16[768,1536]{1,0:T(8,128)(2,1)} %get-tuple-element.62), kind=kOutput, calls=%fused_computation.1 | convolution fusion | flops 1814298624 | bytes 10616832 | tf_op jit(solution)/shard_map/dot_general | solution.py:34
  158.2 4.7 %add_convert_fusion = bf16[1536,768]{1,0:T(8,128)(2,1)} fusion(f32[1536,768]{1,0:T(8,128)S(1)} %copy-done.39, bf16[768,1536]{1,0:T(8,128)(2,1)S(1)} %copy-done.42, bf16[768,768]{1,0:T(8,128)(2,1)} %collective-permute-done.2.g_ref), kind=kOutput, calls=%fused_computation | convolution fusion | flops 1814298624 | bytes 10616832 | tf_op jit(solution)/shard_map/dot_general | solution.py:34
  163.0 1.4 add_reduce_fusion
  165.1 1.9 dynamic_update_slice.7
  167.0 11.3 %collective-permute-done.4 = bf16[768,768]{1,0:T(8,128)(2,1)} collective-permute-done((bf16[768,768]{1,0:T(8,128)(2,1)}, bf16[768,768]{1,0:T(8,128)(2,1)}, u32[]{:S(2)}, u32[]{:S(2)}) %collective-permute-start.4) | collective-permute-done | bytes 1179680 | tf_op jit(solution)/shard_map/ppermute | solution.py:479
  178.3 3.9 multiply_reduce_fusion
  182.2 15.4 %collective-permute-done.3 = bf16[768,768]{1,0:T(8,128)(2,1)} collective-permute-done((bf16[768,768]{1,0:T(8,128)(2,1)}, bf16[768,768]{1,0:T(8,128)(2,1)}, u32[]{:S(2)}, u32[]{:S(2)}) %collective-permute-start.3) | collective-permute-done | bytes 1179680 | tf_op jit(solution)/shard_map/ppermute | solution.py:479
  197.7 4.6 convert_reduce_fusion.2
  202.2 2.1 convolution_convert_fusion.2.g_ref
  204.4 74.6 %attend_back.1 = (bf16[768,768]{1,0:T(8,128)(2,1)}, bf16[1408,768]{1,0:T(8,128)(2,1)}, bf16[1408,768]{1,0:T(8,128)(2,1)}, f32[8,768]{1,0:T(8,128)}, f32[8,768]{1,0:T(8,128)}) custom-call(s32[1,1408]{1,0:T(1,128)} %copy-done.22, bf16[768,768]{1,0:T(8,128)(2,1)} %get-tuple-element.40.q_ref, bf16[768,768]{1,0:T(8,128)(2,1)} %convolution_convert_fusion.2.g_ref, ...), custom_call_target="tpu_custom_call" | custom-call | flops 8304721920 | bytes 17301504 | tf_op jit(solution)/shard_map/attend_back/pallas_call | solution.py:361
  278.9 2.5 fusion.47
  281.5 3.6 add_convert_fusion.6
  285.2 1.2 convolution_convert_fusion.1
  288.0 2.6 fusion.51
  290.6 1.2 fusion.44
  291.8 1.2 add_convert_fusion.3
  293.0 1.2 add_convert_fusion.2
  294.2 2.0 pad_maximum_fusion
  296.2 0.8 copy-done.5
  297.4 2.2 convolution_convert_fusion
  299.6 2.9 fusion.42
  302.5 2.4 fusion.49
  305.1 1.5 constant_dynamic-update-slice_fusion.11
  307.4 3.5 fusion.24
  310.9 1.3 constant_dynamic-update-slice_fusion.2
  312.2 1.3 constant_dynamic-update-slice_fusion.10
  313.5 1.3 constant_dynamic-update-slice_fusion.9
  314.8 1.3 constant_dynamic-update-slice_fusion.8
  316.1 1.3 constant_dynamic-update-slice_fusion.7
  317.4 1.3 constant_dynamic-update-slice_fusion.6
  318.7 1.3 constant_dynamic-update-slice_fusion.5
  320.0 1.3 constant_dynamic-update-slice_fusion.4
  321.3 1.3 constant_dynamic-update-slice_fusion.3
  322.7 43.6 %psum.35 = f32[10752]{0:T(1024)} all-reduce(f32[10752]{0:T(1024)} %constant_dynamic-update-slice_fusion.3), channel_id=1, replica_groups=mesh['dp'=16,'mlp'=2] {'dp','mlp'}, use_global_device_ids=true, to_apply=%region_15.16 | all-reduce | flops 10752 | bytes 86016 | tf_op jit(solution)/shard_map/psum | solution.py:563
  366.3 1.3 slice.130
  367.6 1.4 fusion.77
  369.6 1.4 dynamic_slice.49
  372.3 3.1 fusion.23
  375.4 4.6 %convert_element_type.91 = f32[768,1536]{1,0:T(8,128)} convert(bf16[768,1536]{1,0:T(8,128)(2,1)} %get-tuple-element.105) | non-fusion elementwise | flops 1179648 | bytes 7077888 | tf_op jit(solution)/shard_map/convert_element_type | solution.py:569
  380.1 2.5 convert_element_type.93
  382.6 63.5 %all-reduce.6.cloned.1.call-done = (bf16[768,2304]{0,1:T(8,128)(2,1)}, bf16[768,768]{1,0:T(8,128)(2,1)}) async-done(((bf16[768,2304]{0,1:T(8,128)(2,1)}, bf16[768,768]{1,0:T(8,128)(2,1)}), (bf16[768,2304]{0,1:T(8,128)(2,1)}, bf16[768,768]{1,0:T(8,128)(2,1)})) %all-reduce.6.cloned.1.call-update) | async-done | bytes 4718608 | tf_op jit(solution)/shard_map/psum | solution.py:559
  446.1 6.1 %copy.48 = f32[768,2304]{1,0:T(8,128)} copy(bf16[768,2304]{0,1:T(8,128)(2,1)} %get-tuple-element.103) | data formatting | bytes 10616832
  452.2 1.6 convert_element_type.89
  (141 shorter events, 14.0 us)
Async XLA Ops:
  7.2 90.1 %copy-start = (bf16[768,768]{1,0:T(8,128)(2,1)S(1)}, bf16[768,768]{1,0:T(8,128)(2,1)}, u32[]{:S(2)}) copy-start(bf16[768,768]{1,0:T(8,128)(2,1)} %param.27) | copy-start | bytes 3538948
  7.2 8.7 %copy-start.2 = (bf16[768,768]{1,0:T(8,128)(2,1)S(1)}, bf16[768,768]{1,0:T(8,128)(2,1)}, u32[]{:S(2)}) copy-start(bf16[768,768]{1,0:T(8,128)(2,1)} %x_ref.1) | copy-start | bytes 3538948
  7.2 8.9 %copy-start.29 = (f32[2,384]{1,0:T(2,128)S(1)}, f32[2,384]{1,0:T(2,128)}, u32[]{:S(2)}) copy-start(f32[2,384]{1,0:T(2,128)} %param.26) | copy-start | bytes 9220
  7.2 368.2 %all-reduce.8.cloned.1.call-start = ((), (), s32[]{:S(2)}) async-start(), calls=%async_computation.1 | async-start | bytes 9437184 | tf_op jit(solution)/shard_map/psum | solution.py:557
  7.3 11.0 %copy-start.23 = (f32[2304]{0:T(1024)S(1)}, f32[2304]{0:T(1024)}, u32[]{:S(2)}) copy-start(f32[2304]{0:T(1024)} %param.25) | copy-start | bytes 27652
  7.3 11.6 %copy-start.14 = (f32[768]{0:T(1024)S(1)}, f32[768]{0:T(1024)}, u32[]{:S(2)}) copy-start(f32[768]{0:T(1024)} %param.22) | copy-start | bytes 9220
  7.3 12.2 %copy-start.28 = (f32[768]{0:T(1024)S(1)}, f32[768]{0:T(1024)}, u32[]{:S(2)}) copy-start(f32[768]{0:T(1024)} %param.23) | copy-start | bytes 9220
  8.7 13.7 %copy-start.24 = (f32[1536]{0:T(1024)S(1)}, f32[1536]{0:T(1024)}, u32[]{:S(2)}) copy-start(f32[1536]{0:T(1024)} %param.32) | copy-start | bytes 18436
  8.7 36.6 %collective-permute-start = (bf16[640,768]{1,0:T(8,128)(2,1)S(1)}, bf16[640,768]{1,0:T(8,128)(2,1)}, u32[]{:S(2)}, u32[]{:S(2)}) collective-permute-start(bf16[640,768]{1,0:T(8,128)(2,1)S(1)} %constant_dynamic-slice_fusion.2), channel_id=1, source_target_pairs={{0,1},{1,0},{2,3},{3,2},{4,5},{5,4},{6,7},{7,6},{8,9},{9,8},{10,11... | collective-permute-start | bytes 2949128 | tf_op jit(solution)/shard_map/ppermute | solution.py:479
  11.8 119.8 %collective-permute-start.2 = (bf16[768,768]{1,0:T(8,128)(2,1)}, bf16[768,768]{1,0:T(8,128)(2,1)}, u32[]{:S(2)}, u32[]{:S(2)}) collective-permute-start(bf16[768,768]{1,0:T(8,128)(2,1)} %g_ref.1), channel_id=1, source_target_pairs={{0,1},{1,0},{2,3},{3,2},{4,5},{5,4},{6,7},{7,6},{8,9},{9,8},{10,11... | collective-permute-start | bytes 3538952 | tf_op jit(solution)/shard_map/ppermute | solution.py:479
  14.8 10.7 %copy-start.22 = (s32[1,1408]{1,0:T(1,128)}, s32[1,1408]{1,0:T(1,128)S(1)}, u32[]{:S(2)}) copy-start(s32[1,1408]{1,0:T(1,128)S(1)} %broadcast_in_dim.22.ids_ref) | copy-start | bytes 16900
  54.3 43.0 %copy-start.31 = (f32[768]{0:T(1024)S(1)}, f32[768]{0:T(1024)}, u32[]{:S(2)}) copy-start(f32[768]{0:T(1024)} %param.28) | copy-start | bytes 9220
  100.1 0.7 copy-start.13
  100.1 0.7 copy-start.26
  102.3 29.3 %collective-permute-start.1 = (bf16[768,768]{1,0:T(8,128)(2,1)}, bf16[768,768]{1,0:T(8,128)(2,1)}, u32[]{:S(2)}, u32[]{:S(2)}) collective-permute-start(bf16[768,768]{1,0:T(8,128)(2,1)} %add_convert_fusion.5.n2_ref), channel_id=1, source_target_pairs={{0,1},{1,0},{2,3},{3,2},{4,5},{5,4},{6,7},{7,6},{8,9},{9,8},{10,11... | collective-permute-start | bytes 3538952 | tf_op jit(solution)/shard_map/ppermute | solution.py:479
  120.9 6.4 %copy-start.9 = (bf16[768,768]{1,0:T(8,128)(2,1)S(1)}, bf16[768,768]{1,0:T(8,128)(2,1)}, u32[]{:S(2)}) copy-start(bf16[768,768]{1,0:T(8,128)(2,1)} %g_ref.1) | copy-start | bytes 3538948
  120.9 6.4 %copy-start.40 = (bf16[768,1536]{1,0:T(8,128)(2,1)S(1)}, bf16[768,1536]{1,0:T(8,128)(2,1)}, u32[]{:S(2)}) copy-start(bf16[768,1536]{1,0:T(8,128)(2,1)} %get-tuple-element.63) | copy-start | bytes 7077892
  149.1 29.2 %collective-permute-start.4 = (bf16[768,768]{1,0:T(8,128)(2,1)}, bf16[768,768]{1,0:T(8,128)(2,1)}, u32[]{:S(2)}, u32[]{:S(2)}) collective-permute-start(bf16[768,768]{1,0:T(8,128)(2,1)} %get-tuple-element.49), channel_id=1, source_target_pairs={{0,1},{1,0},{2,3},{3,2},{4,5},{5,4},{6,7},{7,6},{8,9},{9,8},{10,11... | collective-permute-start | bytes 3538952 | tf_op jit(solution)/shard_map/ppermute | solution.py:479
  151.1 46.5 %collective-permute-start.3 = (bf16[768,768]{1,0:T(8,128)(2,1)}, bf16[768,768]{1,0:T(8,128)(2,1)}, u32[]{:S(2)}, u32[]{:S(2)}) collective-permute-start(bf16[768,768]{1,0:T(8,128)(2,1)} %get-tuple-element.47), channel_id=1, source_target_pairs={{0,1},{1,0},{2,3},{3,2},{4,5},{5,4},{6,7},{7,6},{8,9},{9,8},{10,11... | collective-permute-start | bytes 3538952 | tf_op jit(solution)/shard_map/ppermute | solution.py:479
  151.2 7.0 %copy-start.39 = (f32[1536,768]{1,0:T(8,128)S(1)}, f32[1536,768]{1,0:T(8,128)}, u32[]{:S(2)}) copy-start(f32[1536,768]{1,0:T(8,128)} %fusion.81) | copy-start | bytes 14155780
  151.2 7.0 %copy-start.42 = (bf16[768,1536]{1,0:T(8,128)(2,1)S(1)}, bf16[768,1536]{1,0:T(8,128)(2,1)}, u32[]{:S(2)}) copy-start(bf16[768,1536]{1,0:T(8,128)(2,1)} %get-tuple-element.64) | copy-start | bytes 7077892
  163.0 283.1 %all-reduce.6.cloned.1.call-start = ((), (), s32[]{:S(2)}) async-start(), calls=%async_computation | async-start | bytes 9437184 | tf_op jit(solution)/shard_map/psum | solution.py:559
  178.3 19.3 %copy-start.6 = (f32[768,768]{1,0:T(8,128)S(1)}, f32[768,768]{1,0:T(8,128)}, u32[]{:S(2)}) copy-start(f32[768,768]{1,0:T(8,128)} %get-tuple-element.48) | copy-start | bytes 7077892
  178.3 19.3 %copy-start.8 = (f32[768,768]{1,0:T(8,128)S(1)}, f32[768,768]{1,0:T(8,128)}, u32[]{:S(2)}) copy-start(f32[768,768]{1,0:T(8,128)} %get-tuple-element.46) | copy-start | bytes 7077892
  178.3 19.3 %copy-start.10 = (bf16[768,768]{1,0:T(8,128)(2,1)S(1)}, bf16[768,768]{1,0:T(8,128)(2,1)}, u32[]{:S(2)}) copy-start(bf16[768,768]{1,0:T(8,128)(2,1)} %g_ref.1) | copy-start | bytes 3538948
  178.3 19.3 %copy-start.27 = (f32[768]{0:T(1024)S(1)}, f32[768]{0:T(1024)}, u32[]{:S(2)}) copy-start(f32[768]{0:T(1024)} %param.34) | copy-start | bytes 9220
  202.2 2.2 copy-start.4
  281.5 3.7 copy-start.35
  281.5 3.7 copy-start.37
  285.2 19.8 %collective-permute-start.5 = (bf16[640,768]{1,0:T(8,128)(2,1)}, bf16[640,768]{1,0:T(8,128)(2,1)}, u32[]{:S(2)}, u32[]{:S(2)}) collective-permute-start(bf16[640,768]{1,0:T(8,128)(2,1)} %add_convert_fusion.6), channel_id=1, source_target_pairs={{0,1},{1,0},{2,3},{3,2},{4,5},{5,4},{6,7},{7,6},{8,9},{9,8},{10,11... | collective-permute-start | bytes 2949128 | tf_op jit(solution)/shard_map/ppermute | solution.py:479
  285.2 1.2 copy-start.25
  285.2 2.8 copy-start.32
  287.9 2.6 copy-start.33
  288.0 2.6 copy-start.38
  290.6 1.2 copy-start.34
  294.1 2.8 copy-start.5
  294.2 3.2 copy-start.41
  299.6 2.9 copy-start.30
  304.9 1.7 copy-start.3
  304.9 1.7 copy-start.15
  305.0 1.7 copy-start.16
  305.0 2.4 copy-start.36
  307.4 7.4 %copy-start.21 = (f32[768]{0:T(1024)S(1)}, f32[768]{0:T(1024)}, u32[]{:S(2)}) copy-start(f32[768]{0:T(1024)} %reshape.119) | copy-start | bytes 9220
  307.4 8.7 %copy-start.20 = (f32[768]{0:T(1024)S(1)}, f32[768]{0:T(1024)}, u32[]{:S(2)}) copy-start(f32[768]{0:T(1024)} %get-tuple-element.107) | copy-start | bytes 9220
  307.4 10.0 %copy-start.18 = (f32[768]{0:T(1024)S(1)}, f32[768]{0:T(1024)}, u32[]{:S(2)}) copy-start(f32[768]{0:T(1024)} %get-tuple-element.95) | copy-start | bytes 9220
  307.4 11.3 %copy-start.17 = (f32[768]{0:T(1024)S(1)}, f32[768]{0:T(1024)}, u32[]{:S(2)}) copy-start(f32[768]{0:T(1024)} %get-tuple-element.100) | copy-start | bytes 9220
  307.4 12.6 %copy-start.19 = (f32[768]{0:T(1024)S(1)}, f32[768]{0:T(1024)}, u32[]{:S(2)}) copy-start(f32[768]{0:T(1024)} %get-tuple-element.110) | copy-start | bytes 9220
  307.4 13.9 %copy-start.12 = (f32[3072]{0:T(1024)S(1)}, f32[3072]{0:T(1024)}, u32[]{:S(2)}) copy-start(f32[3072]{0:T(1024)} %dynamic_update_slice.7) | copy-start | bytes 36868
  375.4 4.7 %copy-start.7 = (bf16[1536,768]{1,0:T(8,128)(2,1)S(1)}, bf16[1536,768]{1,0:T(8,128)(2,1)}, u32[]{:S(2)}) copy-start(bf16[1536,768]{1,0:T(8,128)(2,1)} %get-tuple-element.106) | copy-start | bytes 7077892
  446.1 6.1 %copy-start.11 = (bf16[768,768]{1,0:T(8,128)(2,1)S(1)}, bf16[768,768]{1,0:T(8,128)(2,1)}, u32[]{:S(2)}) copy-start(bf16[768,768]{1,0:T(8,128)(2,1)} %get-tuple-element.104) | copy-start | bytes 3538948
  446.1 7.7 %copy-start.1 = (bf16[768,768]{1,0:T(8,128)(2,1)S(1)}, bf16[768,768]{1,0:T(8,128)(2,1)}, u32[]{:S(2)}) copy-start(bf16[768,768]{1,0:T(8,128)(2,1)} %param.27) | copy-start | bytes 3538948
Sparse Core Ops, SparseCore 0:
  163.1 118.9 all-reduce.7
  299.7 146.2 all-reduce.5

commit v2 on v1

v2 whole, which is shorter than its diff:
```python
from functools import partial

import jax
import jax.numpy as jnp
from jax import lax
from jax.experimental import pallas as pl
from jax.experimental.pallas import tpu as pltpu
from jax.sharding import PartitionSpec as P

H = 12
HD = 64
PAIRS = H // 2
LANES = 128
EPSILON = 1e-06
MOST = 576
SLOT = 32
KEY_TILE = 128
QUERY_TILE = 256
AHEAD = 3
EDGE = -(-(MOST - 1) // KEY_TILE) * KEY_TILE
VMEM_LIMIT = 60 * 1024 * 1024
BF = jnp.bfloat16
F32 = jnp.float32


def dot(left, right):
    return jnp.dot(left, right, preferred_element_type=F32)


def dot_nt(left, right):
    return lax.dot_general(left, right, (((1,), (1,)), ((), ())), preferred_element_type=F32)


def dot_tn(left, right):
    return lax.dot_general(left, right, (((0,), (0,)), ((), ())), preferred_element_type=F32)


def fill_table(freq_ref, table_ref):
    full = freq_ref.shape[1]
    steps = lax.broadcasted_iota(jnp.int32, (SLOT, full), 0).astype(F32)
    table_ref[...] = jnp.zeros(table_ref.shape, BF)
    for axis in range(2):
        angle = steps * freq_ref[axis : axis + 1, :]
        for kind, values in enumerate((jnp.cos(angle), jnp.sin(angle))):
            first = (2 * axis + kind) * full
            rest = values
            for part in range(3):
                piece = rest.astype(BF)
                start = (3 * axis + part) * SLOT
                table_ref[start : start + SLOT, first : first + full] = piece
                rest = rest - piece.astype(F32)


def one_hot(row_pos, col_pos):
    rows = row_pos.shape[0]
    lane = lax.broadcasted_iota(jnp.int32, (rows, 256), 1)
    part = jnp.where(lane < 6 * SLOT, lane % SLOT, -1)
    return jnp.where(jnp.where(lane < 3 * SLOT, row_pos, col_pos) == part, 1.0, 0.0).astype(BF)


def cos_sin(hot, table, first, width):
    full = H * HD
    parts = [dot(hot, table[:, k * full + first : k * full + first + width]) for k in range(4)]
    cos_r, sin_r, cos_c, sin_c = parts
    cosine = cos_r * cos_c - sin_r * sin_c
    sine = sin_r * cos_c + cos_r * sin_c
    lane_out = lax.broadcasted_iota(jnp.int32, cosine.shape, 1)
    return cosine, jnp.where(lane_out % HD < HD // 2, -sine, sine)


def swap_halves(values):
    lane = lax.broadcasted_iota(jnp.int32, values.shape, 1)
    return jnp.where(
        lane % HD < HD // 2,
        pltpu.roll(values, LANES - HD // 2, 1),
        pltpu.roll(values, HD // 2, 1),
    )


def input_kernel(own, x_ref, row_ref, col_ref, gain_ref, bias_ref, w_ref, b_ref, t_ref, *outs):
    width = x_ref.shape[1]
    if own:
        normed_ref, k_ref, v_ref, cos_ref, sin_ref, q_ref, table_ref = outs

        @pl.when(pl.program_id(0) == 0)
        def _():
            fill_table(t_ref, table_ref)
    else:
        normed_ref, k_ref, v_ref, cos_ref, sin_ref = outs
        q_ref, table_ref = None, t_ref
    values = x_ref[...].astype(F32)
    center = values - jnp.mean(values, axis=-1, keepdims=True)
    spread = jnp.mean(center * center, axis=-1, keepdims=True)
    normed = (center * lax.rsqrt(spread + EPSILON) * gain_ref[...] + bias_ref[...]).astype(BF)
    normed_ref[...] = normed
    hot = one_hot(row_ref[...], col_ref[...])
    wide = 2 * LANES
    for first in range(0, width, wide):
        cosine, sine = cos_sin(hot, table_ref, first, wide)
        cos_ref[:, first : first + wide] = cosine
        sin_ref[:, first : first + wide] = sine
        for kind, out_ref in ((0, q_ref), (1, k_ref)):
            if out_ref is None:
                continue
            start = kind * width + first
            pre = dot(normed, w_ref[:, start : start + wide]) + b_ref[:, start : start + wide]
            for at in range(0, wide, LANES):
                cut = slice(at, at + LANES)
                turned = pre[:, cut] * cosine[:, cut] + swap_halves(pre[:, cut]) * sine[:, cut]
                out_ref[:, first + at : first + at + LANES] = turned.astype(BF)
    v_ref[...] = (dot(normed, w_ref[:, 2 * width :]) + b_ref[:, 2 * width :]).astype(BF)


def input_stage(x, row_col, col_col, gain, bias, w_qkv, b_qkv, table, own, tile):
    rows, width = x.shape
    tiled = lambda cols: pl.BlockSpec((tile, cols), lambda i: (i, 0))
    whole = lambda a: pl.BlockSpec(a.shape, lambda i: (0, 0))
    shape = lambda dtype: jax.ShapeDtypeStruct((rows, width), dtype)
    outs = [tiled(width)] * 5
    shapes = [shape(BF)] * 3 + [shape(F32)] * 2
    if own:
        full_table = jax.ShapeDtypeStruct((256, 4 * width), BF)
        outs = outs + [tiled(width), whole(full_table)]
        shapes = shapes + [shape(BF), full_table]
    return pl.pallas_call(
        partial(input_kernel, own),
        grid=(rows // tile,),
        in_specs=[tiled(width), tiled(1), tiled(1)] + [whole(a) for a in (gain, bias, w_qkv, b_qkv, table)],
        out_specs=outs,
        out_shape=shapes,
        compiler_params=pltpu.CompilerParams(vmem_limit_bytes=VMEM_LIMIT),
        cost_estimate=pl.CostEstimate(
            flops=2 * rows * width * width * (4 if own else 3),
            bytes_accessed=int(w_qkv.size * 2 + rows * width * 2 * 5),
            transcendentals=0,
        ),
        name="ln_qkv_rope",
    )(x, row_col, col_col, gain, bias, w_qkv, b_qkv, table)


def slab(pair):
    return slice(pair * LANES, (pair + 1) * LANES)


def one_head(values, side):
    lane = lax.broadcasted_iota(jnp.int32, values.shape, 1)
    return jnp.where((lane < HD) if side == 0 else (lane >= HD), values, jnp.zeros_like(values))


def visible(ids_ref, query_tile, key_tile):
    q0 = query_tile * QUERY_TILE
    k0 = key_tile * KEY_TILE
    return (ids_ref[0, k0] <= ids_ref[0, q0 + QUERY_TILE - 1]) & (
        ids_ref[0, k0 + KEY_TILE - 1] >= ids_ref[0, q0]
    )


def attend_kernel(ids_ref, q_ref, k_own_ref, k_edge_ref, v_own_ref, v_edge_ref, idk_ref, idq_ref,
                  mixed_ref, out_t_ref, lse_ref, key_sc, value_t_sc, query_sc, peak_sc, total_sc, acc_sc):
    own = k_own_ref.shape[0]
    rows = key_sc.shape[0]
    step = pl.program_id(0)

    @pl.when(step == 0)
    def _():
        key_sc[0:own, :] = k_own_ref[...]
        key_sc[own:rows, :] = k_edge_ref[...]
        for start in range(0, rows, KEY_TILE):
            for pair in range(PAIRS):
                cut = slab(pair)
                if start < own:
                    block = v_own_ref[start : start + KEY_TILE, cut]
                else:
                    block = v_edge_ref[start - own : start - own + KEY_TILE, cut]
                value_t_sc[start // KEY_TILE, cut, :] = jnp.transpose(block.astype(F32)).astype(BF)

    peak_sc[...] = jnp.full(peak_sc.shape, -1e30, F32)
    total_sc[...] = jnp.zeros(total_sc.shape, F32)
    acc_sc[...] = jnp.zeros(acc_sc.shape, F32)
    for head in range(H):
        query_sc[head] = one_head(q_ref[:, slab(head // 2)], head % 2) * BF(HD ** (-0.5))

    @pl.loop(0, rows // KEY_TILE)
    def _(tile):
        @pl.when(visible(ids_ref, step, tile))
        def _():
            k0 = pl.multiple_of(tile * KEY_TILE, KEY_TILE)
            allowed = idk_ref[pl.ds(k0, KEY_TILE), :] == idq_ref[...]
            score = lambda head: dot_nt(key_sc[pl.ds(k0, KEY_TILE), slab(head // 2)], query_sc[head])
            scores = [score(head) for head in range(AHEAD)]
            waiting = None

            def finish(head, fade, expo):
                part = slice(head * HD, (head + 1) * HD)
                acc_sc[part, :] = fade * acc_sc[part, :] + dot(value_t_sc[tile, part, :], expo)

            for head in range(H):
                if head + AHEAD < H:
                    scores.append(score(head + AHEAD))
                masked = jnp.where(allowed, scores[head], -1e30)
                before = peak_sc[head : head + 1, :]
                peak = jnp.maximum(before, jnp.max(masked, axis=0, keepdims=True))
                expo = jnp.exp(masked - peak)
                fade = jnp.exp(before - peak)
                peak_sc[head : head + 1, :] = peak
                total_sc[head : head + 1, :] = fade * total_sc[head : head + 1, :] + jnp.sum(
                    expo, axis=0, keepdims=True
                )
                if waiting is not None:
                    finish(*waiting)
                waiting = (head, fade, expo.astype(BF))
            finish(*waiting)

    lse_ref[...] = peak_sc[...] + jnp.log(jnp.maximum(total_sc[...], 1e-30))
    for head in range(H):
        part = slice(head * HD, (head + 1) * HD)
        acc_sc[part, :] = acc_sc[part, :] / total_sc[head : head + 1, :]
    out_t_ref[...] = acc_sc[...]
    for pair in range(PAIRS):
        cut = slab(pair)
        mixed_ref[:, cut] = jnp.transpose(acc_sc[cut, :]).astype(BF)


def attend(ids, q, k_own, k_edge, v_own, v_edge, id_col, id_row):
    own, width = q.shape
    rows = own + k_edge.shape[0]
    whole = lambda a: pl.BlockSpec(a.shape, lambda i: (0, 0))
    return pl.pallas_call(
        attend_kernel,
        grid=(own // QUERY_TILE,),
        in_specs=[
            pl.BlockSpec(memory_space=pltpu.SMEM),
            pl.BlockSpec((QUERY_TILE, width), lambda i: (i, 0)),
            whole(k_own), whole(k_edge), whole(v_own), whole(v_edge), whole(id_col),
            pl.BlockSpec((1, QUERY_TILE), lambda i: (0, i)),
        ],
        out_specs=[
            pl.BlockSpec((QUERY_TILE, width), lambda i: (i, 0)),
            pl.BlockSpec((width, QUERY_TILE), lambda i: (0, i)),
            pl.BlockSpec((16, QUERY_TILE), lambda i: (0, i)),
        ],
        out_shape=[
            jax.ShapeDtypeStruct((own, width), BF),
            jax.ShapeDtypeStruct((width, own), F32),
            jax.ShapeDtypeStruct((16, own), F32),
        ],
        scratch_shapes=[
            pltpu.VMEM((rows, width), BF),
            pltpu.VMEM((rows // KEY_TILE, width, KEY_TILE), BF),
            pltpu.VMEM((H, QUERY_TILE, LANES), BF),
            pltpu.VMEM((16, QUERY_TILE), F32),
            pltpu.VMEM((16, QUERY_TILE), F32),
            pltpu.VMEM((width, QUERY_TILE), F32),
        ],
        compiler_params=pltpu.CompilerParams(vmem_limit_bytes=VMEM_LIMIT),
        cost_estimate=pl.CostEstimate(
            flops=4 * own * rows * width, bytes_accessed=int(rows * width * 8), transcendentals=own * rows * H // 2
        ),
        name="attend",
    )(ids, q, k_own, k_edge, v_own, v_edge, id_col, id_row)


def unrotate(grad, rotated, cosine, sine):
    lane = lax.broadcasted_iota(jnp.int32, grad.shape, 1)
    turned = swap_halves(rotated)
    angle = grad * jnp.where(lane % HD < HD // 2, -turned, turned)
    return grad * cosine - swap_halves(grad) * sine, angle


def attend_back_kernel(ids_ref, q_ref, g_ref, k_own_ref, k_edge_ref, v_own_ref, v_edge_ref, idk_ref,
                       idq_ref, out_t_ref, lse_ref, row_ref, col_ref, cos_ref, sin_ref, cos_edge_ref, sin_edge_ref,
                       own_ref, edge_ref, sums_ref,
                       key_sc, value_sc, key_t_sc, query_sc, grad_sc, dk_sc, dv_sc, dq_t_sc, delta_sc):
    own, width = k_own_ref.shape
    rows = key_sc.shape[0]
    step = pl.program_id(0)
    scale = HD ** (-0.5)

    @pl.when(step == 0)
    def _():
        key_sc[0:own, :] = k_own_ref[...]
        key_sc[own:rows, :] = k_edge_ref[...]
        value_sc[0:own, :] = v_own_ref[...]
        value_sc[own:rows, :] = v_edge_ref[...]
        for start in range(0, rows, KEY_TILE):
            for pair in range(PAIRS):
                cut = slab(pair)
                if start < own:
                    block = k_own_ref[start : start + KEY_TILE, cut]
                else:
                    block = k_edge_ref[start - own : start - own + KEY_TILE, cut]
                key_t_sc[start // KEY_TILE, cut, :] = jnp.transpose(block.astype(F32)).astype(BF)
        dk_sc[...] = jnp.zeros(dk_sc.shape, F32)
        dv_sc[...] = jnp.zeros(dv_sc.shape, F32)
        sums_ref[...] = jnp.zeros(sums_ref.shape, F32)

    dq_t_sc[...] = jnp.zeros(dq_t_sc.shape, F32)
    for head in range(H):
        query_sc[head] = one_head(q_ref[:, slab(head // 2)], head % 2) * BF(scale)
        grad_sc[head] = one_head(g_ref[:, slab(head // 2)], head % 2)
    for pair in range(PAIRS):
        cut = slab(pair)
        grad_t = jnp.transpose(g_ref[:, cut].astype(F32)) * out_t_ref[cut, :]
        for side in range(2):
            delta_sc[2 * pair + side : 2 * pair + side + 1, :] = jnp.sum(
                grad_t[side * HD : (side + 1) * HD, :], axis=0, keepdims=True
            )

    @pl.loop(0, rows // KEY_TILE)
    def _(tile):
        @pl.when(visible(ids_ref, step, tile))
        def _():
            k0 = pl.multiple_of(tile * KEY_TILE, KEY_TILE)
            allowed = idk_ref[pl.ds(k0, KEY_TILE), :] == idq_ref[...]
            here = pl.ds(k0, KEY_TILE)

            def first(head):
                cut = slab(head // 2)
                return dot_nt(key_sc[here, cut], query_sc[head]), dot_nt(value_sc[here, cut], grad_sc[head])

            def finish(head, weights, grad_s):
                part = slice(head * HD, (head + 1) * HD)
                dq_t_sc[part, :] += dot(key_t_sc[tile, part, :], grad_s)
                return dot(weights, grad_sc[head]), dot(grad_s, query_sc[head])

            started = [first(head) for head in range(AHEAD)]
            ready = []
            sums = []

            def flush(head):
                sums.append(finish(head, *ready[head]))
                if head % 2 == 1:
                    cut = slab(head // 2)
                    dv_sc[here, cut] += sums[head - 1][0] + sums[head][0]
                    dk_sc[here, cut] += sums[head - 1][1] + sums[head][1]

            for head in range(H):
                if head + AHEAD < H:
                    started.append(first(head + AHEAD))
                scores, grad_w = started[head]
                weights = jnp.where(allowed, jnp.exp(scores - lse_ref[head : head + 1, :]), 0.0)
                grad_s = weights * (grad_w - delta_sc[head : head + 1, :])
                ready.append((weights.astype(BF), grad_s.astype(BF)))
                if head > 0:
                    flush(head - 1)
            flush(H - 1)

    def close(grad, rotated, cosine, sine, row_pos, col_pos, line, cut):
        back, angle = unrotate(grad, rotated.astype(F32), cosine, sine)
        back = back.astype(BF)
        sums_ref[3:4, cut] += jnp.sum(angle * row_pos, axis=0, keepdims=True)
        sums_ref[4:5, cut] += jnp.sum(angle * col_pos, axis=0, keepdims=True)
        sums_ref[line : line + 1, cut] += jnp.sum(back.astype(F32), axis=0, keepdims=True)
        return back

    q_here = pl.ds(pl.multiple_of(step * QUERY_TILE, QUERY_TILE), QUERY_TILE)
    row_q = row_ref[q_here, :].astype(F32)
    col_q = col_ref[q_here, :].astype(F32)
    for pair in range(PAIRS):
        cut = slab(pair)
        grad = jnp.transpose(dq_t_sc[cut, :]) * scale
        own_ref[q_here, cut] = close(
            grad, q_ref[:, cut], cos_ref[q_here, cut], sin_ref[q_here, cut], row_q, col_q, 0, cut
        )

    @pl.when(step == pl.num_programs(0) - 1)
    def _():
        def keys_of(count, first, out_ref, k_at, v_at, c_ref, s_ref):
            @pl.loop(0, count // KEY_TILE)
            def _(tile):
                here = pl.ds(pl.multiple_of(tile * KEY_TILE, KEY_TILE), KEY_TILE)
                there = pl.ds(pl.multiple_of(first + tile * KEY_TILE, KEY_TILE), KEY_TILE)
                row_pos = row_ref[there, :].astype(F32)
                col_pos = col_ref[there, :].astype(F32)
                for pair in range(PAIRS):
                    cut = slab(pair)
                    out_ref[here, k_at + pair * LANES : k_at + (pair + 1) * LANES] = close(
                        dk_sc[there, cut], key_sc[there, cut], c_ref[here, cut], s_ref[here, cut],
                        row_pos, col_pos, 1, cut,
                    )
                    grad_v = dv_sc[there, cut].astype(BF)
                    out_ref[here, v_at + pair * LANES : v_at + (pair + 1) * LANES] = grad_v
                    sums_ref[2:3, cut] += jnp.sum(grad_v.astype(F32), axis=0, keepdims=True)

        keys_of(own, 0, own_ref, width, 2 * width, cos_ref, sin_ref)
        keys_of(rows - own, own, edge_ref, 0, width, cos_edge_ref, sin_edge_ref)


def attend_back(ids, q, grad_mixed, k_own, k_edge, v_own, v_edge, id_col, id_row, out_t, lse, row_col, col_col, turns):
    own, width = q.shape
    edge = k_edge.shape[0]
    rows = own + edge
    whole = lambda a: pl.BlockSpec(a.shape, lambda i: (0, 0))
    once = lambda a: pl.BlockSpec(a.shape, lambda i: (0, 0), pipeline_mode=pl.Buffered(1))
    tiled = pl.BlockSpec((QUERY_TILE, width), lambda i: (i, 0))
    across = lambda n: pl.BlockSpec((n, QUERY_TILE), lambda i: (0, i))
    outs = [
        jax.ShapeDtypeStruct((own, 3 * width), BF),
        jax.ShapeDtypeStruct((edge, 2 * width), BF),
        jax.ShapeDtypeStruct((8, width), F32),
    ]
    return pl.pallas_call(
        attend_back_kernel,
        grid=(own // QUERY_TILE,),
        in_specs=[
            pl.BlockSpec(memory_space=pltpu.SMEM), tiled, tiled,
            once(k_own), once(k_edge), once(v_own), once(v_edge), once(id_col),
            across(1), across(width), across(16), once(row_col), once(col_col),
        ] + [once(a) for a in turns],
        out_specs=[whole(a) for a in outs],
        out_shape=outs,
        scratch_shapes=[
            pltpu.VMEM((rows, width), BF),
            pltpu.VMEM((rows, width), BF),
            pltpu.VMEM((rows // KEY_TILE, width, KEY_TILE), BF),
            pltpu.VMEM((H, QUERY_TILE, LANES), BF),
            pltpu.VMEM((H, QUERY_TILE, LANES), BF),
            pltpu.VMEM((rows, width), F32),
            pltpu.VMEM((rows, width), F32),
            pltpu.VMEM((width, QUERY_TILE), F32),
            pltpu.VMEM((16, QUERY_TILE), F32),
        ],
        compiler_params=pltpu.CompilerParams(vmem_limit_bytes=VMEM_LIMIT),
        cost_estimate=pl.CostEstimate(
            flops=10 * own * rows * width, bytes_accessed=int(rows * width * 16), transcendentals=own * rows * H // 2
        ),
        name="attend_back",
    )(ids, q, grad_mixed, k_own, k_edge, v_own, v_edge, id_col, id_row, out_t, lse, row_col, col_col, *turns)


def ffn_kernel(n2_ref, g_ref, up_ref, b_ref, down_ref, hidden_ref, grad_ref, out_ref, back_ref, sums_ref, out_sc, back_sc):
    step = pl.program_id(0)

    @pl.when(step == 0)
    def _():
        out_sc[...] = jnp.zeros(out_sc.shape, F32)
        back_sc[...] = jnp.zeros(back_sc.shape, F32)

    rows = n2_ref.shape[0]
    block = 128
    sums_ref[...] = jnp.zeros(sums_ref.shape, F32)

    cuts = [slice(i, i + block) for i in range(0, rows, block)]

    def first(here):
        return dot(n2_ref[here, :], up_ref[...]) + b_ref[...], dot_nt(g_ref[here, :], down_ref[...])

    def finish(here, hidden, grad_pre):
        out_sc[here, :] += dot(hidden, down_ref[...])
        back_sc[here, :] += dot_nt(grad_pre, up_ref[...])

    started = [first(cuts[0])]
    ready = []
    total = jnp.zeros((1, up_ref.shape[1]), F32)
    for i, here in enumerate(cuts):
        if i + 1 < len(cuts):
            started.append(first(cuts[i + 1]))
        pre, grad_hidden = started[i]
        phi = 0.5 * (1.0 + lax.erf(pre * (0.5 ** 0.5)))
        hidden = (pre * phi).astype(BF)
        slope = phi + pre * (jnp.exp(pre * pre * (-0.5)) * 0.3989422804014327)
        grad_pre = (grad_hidden * slope).astype(BF)
        hidden_ref[here, :] = hidden
        grad_ref[here, :] = grad_pre
        total += jnp.sum(grad_pre.astype(F32), axis=0, keepdims=True)
        ready.append((hidden, grad_pre))
        if i > 0:
            finish(cuts[i - 1], *ready[i - 1])
    finish(cuts[-1], *ready[-1])
    sums_ref[0:1, :] = total

    @pl.when(step == pl.num_programs(0) - 1)
    def _():
        out_ref[...] = out_sc[...].astype(out_ref.dtype)
        back_ref[...] = back_sc[...].astype(back_ref.dtype)


def ffn(n2, g, w_up, b_up, w_down, dtype):
    rows, width = n2.shape
    units = w_up.shape[1]
    block = 256
    whole = pl.BlockSpec((rows, width), lambda j: (0, 0))
    across = pl.BlockSpec((rows, block), lambda j: (0, j))
    return pl.pallas_call(
        ffn_kernel,
        grid=(units // block,),
        in_specs=[
            whole, whole,
            pl.BlockSpec((width, block), lambda j: (0, j)),
            pl.BlockSpec((1, block), lambda j: (0, j)),
            pl.BlockSpec((block, width), lambda j: (j, 0)),
        ],
        out_specs=[across, across, whole, whole, pl.BlockSpec((8, block), lambda j: (0, j))],
        out_shape=[
            jax.ShapeDtypeStruct((rows, units), BF),
            jax.ShapeDtypeStruct((rows, units), BF),
            jax.ShapeDtypeStruct((rows, width), dtype),
            jax.ShapeDtypeStruct((rows, width), dtype),
            jax.ShapeDtypeStruct((8, units), F32),
        ],
        scratch_shapes=[pltpu.VMEM((rows, width), F32), pltpu.VMEM((rows, width), F32)],
        compiler_params=pltpu.CompilerParams(vmem_limit_bytes=VMEM_LIMIT),
        cost_estimate=pl.CostEstimate(
            flops=8 * rows * width * units, bytes_accessed=int(4 * width * units + 4 * rows * units + 8 * rows * width),
            transcendentals=2 * rows * units,
        ),
        name="ffn",
    )(n2, g, w_up, b_up, w_down)


def norm_back(values, gain, grad):
    center = values - jnp.mean(values, axis=-1, keepdims=True)
    inverse = lax.rsqrt(jnp.mean(center * center, axis=-1, keepdims=True) + EPSILON)
    unit = center * inverse
    scaled = grad * gain
    first = jnp.mean(scaled, axis=-1, keepdims=True)
    second = jnp.mean(scaled * unit, axis=-1, keepdims=True)
    back = (scaled - first - unit * second) * inverse
    return back, jnp.sum(grad * unit, axis=0), jnp.sum(grad, axis=0)


def per_device(
    axes, patches, image_of_patch, patch_row, patch_col, ln1_gain, ln1_bias, w_qkv, b_qkv, freqs, w_out, b_out,
    ln2_gain, ln2_bias, w_up, b_up, w_down, b_down, out_cotangent,
):
    own, width = patches.shape
    me = lax.axis_index("mlp")
    other = [(0, 1), (1, 0)]
    swap = lambda a: lax.ppermute(a, "mlp", other)
    edge = min(own, EDGE)
    mine_start = jnp.where(me == 0, own - edge, 0)
    edge_start = jnp.where(me == 0, own, own - edge)
    x_edge = swap(lax.dynamic_slice_in_dim(patches, mine_start, edge))
    g_other = swap(out_cotangent)

    def local(a):
        return jnp.concatenate(
            [lax.dynamic_slice_in_dim(a[0], me * own, own), lax.dynamic_slice_in_dim(a[0], edge_start, edge)]
        )

    ids = local(image_of_patch)
    row_pos = local(patch_row)[:, None]
    col_pos = local(patch_col)[:, None]
    id_row = ids[None, :]
    id_col = ids[:, None]
    id_own = id_row[:, :own]
    wide_freqs = jnp.concatenate([freqs.reshape(2, H, 1, HD // 2)] * 2, axis=2).reshape(2, width)
    gain1, bias1, bias_qkv = ln1_gain[None], ln1_bias[None], b_qkv[None]
    normed, k_own, v_own, cos_own, sin_own, q, table = input_stage(
        patches, row_pos[:own], col_pos[:own], gain1, bias1, w_qkv, bias_qkv, wide_freqs, True, 256
    )
    normed_edge, k_edge, v_edge, cos_edge, sin_edge = input_stage(
        x_edge, row_pos[own:], col_pos[own:], gain1, bias1, w_qkv, bias_qkv, table, False, edge // 2
    )
    mixed, out_t, lse = attend(id_row, q, k_own, k_edge, v_own, v_edge, id_col, id_own)
    inputs = patches.astype(F32)
    middle = inputs + dot(mixed, w_out) + b_out
    center = middle - jnp.mean(middle, axis=-1, keepdims=True)
    spread = jnp.mean(center * center, axis=-1, keepdims=True)
    normed2 = (center * lax.rsqrt(spread + EPSILON) * ln2_gain + ln2_bias).astype(BF)
    n2_other = swap(normed2)
    bias_up = b_up[None]
    hid_a, gp_a, out_a, back_a, sum_a = ffn(normed2, out_cotangent, w_up, bias_up, w_down, F32)
    hid_b, gp_b, out_b, back_b, sum_b = ffn(n2_other, g_other, w_up, bias_up, w_down, BF)
    back_in = swap(back_b)
    out_in = swap(out_b)
    grad_b_up = sum_a[0] + sum_b[0]
    grad_w_up = (dot_tn(normed2, gp_a) + dot_tn(n2_other, gp_b)).astype(BF)
    grad_w_down = (dot_tn(hid_a, out_cotangent) + dot_tn(hid_b, g_other)).astype(BF)
    block_out = (middle + out_a + out_in.astype(F32) + b_down).astype(BF)
    grad_out = out_cotangent.astype(F32)
    grad_n2 = back_a + back_in.astype(F32)
    from_norm2, grad_ln2_gain, grad_ln2_bias = norm_back(middle, ln2_gain, grad_n2)
    grad_middle = grad_out + from_norm2
    grad_b_down = jnp.sum(grad_out, axis=0)
    grad_attended = grad_middle.astype(BF)
    grad_b_out = jnp.sum(grad_attended.astype(F32), axis=0)
    grad_w_out = dot_tn(mixed, grad_attended).astype(BF)
    grad_mixed = dot_nt(grad_attended, w_out).astype(BF)
    d_own, d_edge, sums = attend_back(
        id_row, q, grad_mixed, k_own, k_edge, v_own, v_edge, id_col, id_own, out_t, lse, row_pos, col_pos,
        (cos_own, sin_own, cos_edge, sin_edge),
    )
    gn_in = swap(dot_nt(d_edge, w_qkv[:, width:]).astype(BF))
    grad_w_q = dot_tn(normed, d_own[:, :width]).astype(BF)
    grad_w_kv = (dot_tn(normed, d_own[:, width:]) + dot_tn(normed_edge, d_edge)).astype(BF)
    gn = dot_nt(d_own, w_qkv)
    spread_in = lax.dynamic_update_slice_in_dim(jnp.zeros((own, width), BF), gn_in, mine_start, 0)
    grad_normed = gn + spread_in.astype(F32)
    from_norm1, grad_ln1_gain, grad_ln1_bias = norm_back(inputs, ln1_gain, grad_normed)
    grad_patches = (grad_middle + from_norm1).astype(BF)
    everyone = axes + ("mlp",)
    units = b_up.shape[0] // width
    lines = [grad_ln1_gain, grad_ln1_bias] + [sums[i] for i in range(5)]
    lines += [grad_b_out, grad_ln2_gain, grad_ln2_bias, grad_b_down]
    count = len(lines)
    line = lax.broadcasted_iota(jnp.int32, (16, width), 0)
    small = jnp.zeros((16, width), F32)
    for i, values in enumerate(lines):
        small = jnp.where(line == i, values[None], small)
    for i in range(units):
        small = jnp.where(line == count + me * units + i, grad_b_up[None, i * width : (i + 1) * width], small)
    grad_w_up, grad_w_down = lax.psum((grad_w_up, grad_w_down), axes)
    grad_w_q, grad_w_kv, grad_w_out = lax.psum((grad_w_q, grad_w_kv, grad_w_out), everyone)
    total = lax.psum(small, everyone)
    grad_b_up = lax.dynamic_slice_in_dim(total, count + me * units, units).reshape(units * width)
    grad_w_qkv = jnp.concatenate([grad_w_q, grad_w_kv], axis=1).astype(F32)
    grad_freqs = jnp.sum(total[5:7].reshape(2, H, 2, HD // 2), axis=2).reshape(2, width // 2)
    total = [total[i] for i in range(count)]
    return (
        block_out, grad_patches, total[0], total[1], grad_w_qkv, jnp.concatenate(total[2:5]), grad_freqs,
        grad_w_out.astype(F32), total[7], total[8], total[9], grad_w_up.astype(F32), grad_b_up,
        grad_w_down.astype(F32), total[10],
    )


def solution(mesh):
    rows = P(("dp", "mlp"), None)
    group = P("dp", None)
    in_specs = (rows, group, group, group) + (P(),) * 9 + (P(None, "mlp"), P("mlp"), P("mlp", None), P(), rows)
    out_specs = (rows, rows) + (P(),) * 9 + (P(None, "mlp"), P("mlp"), P("mlp", None), P())
    return jax.shard_map(
        partial(per_device, ("dp",)), mesh=mesh, in_specs=in_specs, out_specs=out_specs, check_vma=False
    )
```

time: 469 us -> 428 us (0.913); the launches traced: 461 us -> 426 us
  Pallas kernels: 175 us -> 117 us
  waiting for transfers between devices: 90.2 us -> 125 us
  local copies, waits for them, and re-layouts: 45.2 us -> 24.9 us
  blocking collectives: 43.6 us -> 50.1 us
    pallas_call x1, Pallas kernels: 74.6 us -> 40.5 us  [attend_back(): pl.pallas_call(attend_back_kernel, grid=(own // QUERY_TILE,), in_specs=[p...]
    pallas_call x1, Pallas kernels: 43 us -> 20.8 us  [attend(): pl.pallas_call(attend_kernel, grid=(own // QUERY_TILE,), in_specs=[pl.Blo...]
    psum x1, waiting for transfers between devices: 63.5 us -> 83.2 us  [per_device(): lax.psum((grad_w_q, grad_w_kv, grad_w_out), everyone)]
    unnamed x96 -> x106, local copies, waits for them, and re-layouts: 19 us -> 1.14 us
    ppermute x6, waiting for transfers between devices: 26.7 us -> 41.4 us  [per_device(): swap = lambda a: lax.ppermute(a, 'mlp', other)]
    concatenate x2, other arithmetic: 7.27 us -> 0.61 us  [the longest x1 0.6 us: per_device(): jnp.concatenate(total[2:5])]
    psum x1, blocking collectives: 43.6 us -> 50.1 us  [per_device(): total = lax.psum(small, everyone)]
    dot_general x6 -> x3, matrix products: 17.1 us -> 15.9 us  [dot_nt(): lax.dot_general(left, right, (((1,), (1,)), ((), ())), preferred_element_...]
  transfers between devices with their start and end apart: 8 -> 8, of which waited for: 3 -> 4; matrix products, arithmetic and copies ran while one was open for 26% -> 24% of each run, Pallas kernels for 34% -> 23%
where the time goes in v2:
time: 428 us; the launch traced here: 426 us
  waiting for transfers between devices  125 us (29%)
  Pallas kernels  117 us (27%)
  matrix products  51 us (12%)
  blocking collectives  50.1 us (12%)
  other arithmetic  37.1 us (9%)
  local copies, waits for them, and re-layouts  24.9 us (6%)
  between operations  15 us (4%)
  starting transfers between devices  5.57 us (1%)
    psum x1, waiting for transfers between devices, per_device(): lax.psum((grad_w_q, grad_w_kv, grad_w_out), everyone)  83.2 us
    psum x1, blocking collectives, per_device(): total = lax.psum(small, everyone)  50.1 us
    ppermute x6, waiting for transfers between devices, per_device(): swap = lambda a: lax.ppermute(a, 'mlp', other)  41.4 us
    pallas_call x1, Pallas kernels, attend_back(): pl.pallas_call(attend_back_kernel, grid=(own // QUERY_TILE,), in_specs=[p...  40.5 us
    pallas_call x2, Pallas kernels, ffn(): pl.pallas_call(ffn_kernel, grid=(units // block,), in_specs=[whole, whole...  36.4 us
    dot_general x8, matrix products, dot_tn(): lax.dot_general(left, right, (((0,), (0,)), ((), ())), preferred_element_...  32.3 us
    pallas_call x1, Pallas kernels, attend(): pl.pallas_call(attend_kernel, grid=(own // QUERY_TILE,), in_specs=[pl.Blo...  20.8 us
    pallas_call x2, Pallas kernels, input_stage(): pl.pallas_call(partial(input_kernel, own), grid=(rows // tile,), in_specs...  19.7 us
  transfers between devices with their start and end apart: 8, of which 4 were waited for; matrix products, arithmetic and copies ran while one was open for 24% of the time, Pallas kernels for 23%

profile of v2, /device:TPU:0, one launch (start us, length us, event | category | flops | bytes accessed | tf_op | source)
XLA Modules:
  0.0 425.7 jit_solution(14278293379351094985)
XLA Ops:
  7.3 1.4 constant_dynamic-slice_fusion.3
  8.7 3.1 collective-permute-start
  11.9 0.7 fusion.21
  12.6 0.7 fusion.25
  13.3 0.7 dynamic-slice_reduce_fusion
  14.0 0.7 dynamic-slice_reduce_fusion.1
  14.8 1.1 broadcast_in_dim.162.idk_ref
  16.7 0.6 iota_compare_fusion.2
  19.6 0.9 copy.47.row_ref
  20.6 0.9 copy.48.col_ref
  21.5 0.6 broadcast_in_dim.135.b_ref
  23.4 0.7 reshape.116.t_ref
  24.1 0.9 copy.49.row_ref
  25.0 0.9 copy.50.col_ref
  27.2 1.1 broadcast_in_dim.160.row_ref
  28.3 1.1 broadcast_in_dim.161.col_ref
  30.5 0.6 add_rsqrt_fusion
  31.1 11.4 %ln_qkv_rope.2 = (bf16[768,768]{1,0:T(8,128)(2,1)}, bf16[768,768]{1,0:T(8,128)(2,1)}, bf16[768,768]{1,0:T(8,128)(2,1)}, f32[768,768]{1,0:T(8,128)}, f32[768,768]...) custom-call(bf16[768,768]{1,0:T(8,128)(2,1)} %x_ref.1, s32[768,1]{1,0:T(8,128)} %copy.47.row_ref, ...), custom_call_target="tpu_custom_call" | custom-call | flops 3623878656 | bytes 9437184 | tf_op jit(solution)/shard_map/ln_qkv_rope/pallas_call | solution.py:125
  42.4 8.3 %ln_qkv_rope.3 = (bf16[640,768]{1,0:T(8,128)(2,1)}, bf16[640,768]{1,0:T(8,128)(2,1)}, bf16[640,768]{1,0:T(8,128)(2,1)}, f32[640,768]{1,0:T(8,128)}, f32[640,768]{1,0:T(8,128)}) custom-call(bf16[640,768]{1,0:T(8,128)(2,1)} %collective-permute-done.x_ref, s32[640,1]{1,0:T(8,128)} %copy.49.row_ref, s32[640,1]{1,0:T(8,128)} %copy.50.col_ref, ...), custom_call_target="tpu_custom_call" | custom-call | flops 2264924160 | bytes 8454144 | tf_op jit(solution)/shard_map/ln_qkv_rope/pallas_call | solution.py:125
  50.8 20.8 %attend.1 = (bf16[768,768]{1,0:T(8,128)(2,1)}, f32[768,768]{1,0:T(8,128)}, f32[16,768]{1,0:T(8,128)}) custom-call(s32[1,1408]{1,0:T(1,128)} %copy-done.24, bf16[768,768]{1,0:T(8,128)(2,1)} %get-tuple-element.43.q_ref, bf16[768,768]{1,0:T(8,128)(2,1)} %get-tuple-element.44.k_own_ref, bf16[640,768]{1,0:T(8,128)(2,1)} %get-tuple-element.46.k_edge_ref, ...), custom_call_target="tpu_custom_call" | custom-call | flops 3321888768 | bytes 8650752 | tf_op jit(solution)/shard_map/attend/pallas_call | solution.py:228
  71.6 2.8 fusion.32
  75.1 1.4 add_convert_fusion.4.n2_ref
  76.8 18.7 %ffn.2 = (bf16[768,1536]{1,0:T(8,128)(2,1)}, bf16[768,1536]{1,0:T(8,128)(2,1)}, f32[768,768]{1,0:T(8,128)}, f32[768,768]{1,0:T(8,128)}, f32[8,1536]{1,0:T(8,128)}) custom-call(bf16[768,768]{1,0:T(8,128)(2,1)} %add_convert_fusion.4.n2_ref, bf16[768,768]{1,0:T(8,128)(2,1)} %g_ref.1, bf16[768,1536]{1,0:T(8,128)(2,1)} %up_ref.3, ...), custom_call_target="tpu_custom_call" | custom-call | flops 7247757312 | bytes 14155776 | tf_op jit(solution)/shard_map/ffn/pallas_call | solution.py:484
  95.6 6.4 %fusion.33 = f32[768,1536]{1,0:T(8,128)} fusion(bf16[768,768]{1,0:T(8,128)(2,1)} %add_convert_fusion.4.n2_ref, bf16[768,1536]{1,0:T(8,128)(2,1)} %get-tuple-element.67), kind=kOutput, calls=%fused_computation.107 | convolution fusion | flops 1811939328 | bytes 8257536 | tf_op jit(solution)/shard_map/dot_general | solution.py:35
  102.0 4.3 %fusion.34 = f32[1536,768]{1,0:T(8,128)} fusion(bf16[768,1536]{1,0:T(8,128)(2,1)S(1)} %copy-done.49, bf16[768,768]{1,0:T(8,128)(2,1)S(1)} %copy-done.10), kind=kOutput, calls=%fused_computation.108 | convolution fusion | flops 1811939328 | bytes 8257536 | tf_op jit(solution)/shard_map/dot_general | solution.py:35
  106.2 17.7 %ffn.3 = (bf16[768,1536]{1,0:T(8,128)(2,1)}, bf16[768,1536]{1,0:T(8,128)(2,1)}, bf16[768,768]{1,0:T(8,128)(2,1)}, bf16[768,768]{1,0:T(8,128)(2,1)}, f32[8,1536]{1,0:T(8,128)}) custom-call(bf16[768,768]{1,0:T(8,128)(2,1)} %collective-permute-done.1.n2_ref, bf16[768,768]{1,0:T(8,128)(2,1)} %collective-permute-done.2.g_ref, bf16[768,1536]{1,0:T(8,128)(2,1)} %up_ref.3, ...), custom_call_target="tpu_custom_call" | custom-call | flops 7247757312 | bytes 14155776 | tf_op jit(solution)/shard_map/ffn/pallas_call | solution.py:484
  124.0 1.8 collective-permute-start.4
  126.1 7.0 %add_convert_fusion.1 = bf16[768,1536]{1,0:T(8,128)(2,1)} fusion(f32[768,1536]{1,0:T(8,128)} %fusion.33, bf16[768,768]{1,0:T(8,128)(2,1)} %collective-permute-done.1.n2_ref, bf16[768,1536]{1,0:T(8,128)(2,1)} %get-tuple-element.68), kind=kOutput, calls=%fused_computation.1 | convolution fusion | flops 1814298624 | bytes 10616832 | tf_op jit(solution)/shard_map/dot_general | solution.py:35
  133.1 4.7 %add_convert_fusion = bf16[1536,768]{1,0:T(8,128)(2,1)} fusion(f32[1536,768]{1,0:T(8,128)S(1)} %copy-done.47, bf16[768,1536]{1,0:T(8,128)(2,1)S(1)} %copy-done.52, bf16[768,768]{1,0:T(8,128)(2,1)} %collective-permute-done.2.g_ref), kind=kOutput, calls=%fused_computation | convolution fusion | flops 1814298624 | bytes 10616832 | tf_op jit(solution)/shard_map/dot_general | solution.py:35
  137.8 0.8 slice_add_fusion
  138.7 0.6 slice_reduce_fusion.10
  139.3 13.9 %collective-permute-done.4 = bf16[768,768]{1,0:T(8,128)(2,1)} collective-permute-done((bf16[768,768]{1,0:T(8,128)(2,1)}, bf16[768,768]{1,0:T(8,128)(2,1)}, u32[]{:S(2)}, u32[]{:S(2)}) %collective-permute-start.4) | collective-permute-done | bytes 1179680 | tf_op jit(solution)/shard_map/ppermute | solution.py:529
  153.2 3.9 multiply_reduce_fusion
  157.1 18.8 %collective-permute-done.3 = bf16[768,768]{1,0:T(8,128)(2,1)} collective-permute-done((bf16[768,768]{1,0:T(8,128)(2,1)}, bf16[768,768]{1,0:T(8,128)(2,1)}, u32[]{:S(2)}, u32[]{:S(2)}) %collective-permute-start.3) | collective-permute-done | bytes 1179680 | tf_op jit(solution)/shard_map/ppermute | solution.py:529
  176.0 4.9 %convert_reduce_fusion.2 = (f32[768]{0:T(1024)}, f32[768,768]{1,0:T(8,128)S(1)}, bf16[768,768]{1,0:T(8,128)(2,1)}, f32[768]{0:T(1024)}) fusion(f32[768]{0:T(1024)S(1)} %broadcast_multiply_fusion.3, f32[768]{0:T(1024)S(1)} %add_rsqrt_fusion.1, f32[768,768]{1,0:T(8,128)S(1)} %get-tuple-element.115, f32[768]{0:T(1024)S(1)} %broadcast_multiply_fusion.5, ...), kind=kLoop, calls=%fused_computation.24 | loop fusion | flops 11794944 | bytes 14180352 | tf_op jit(solution)/shard_map/reduce_sum | solution.py:577
  180.9 2.1 convolution_convert_fusion.2.g_ref
  183.1 40.5 %attend_back.1 = (bf16[768,2304]{1,0:T(8,128)(2,1)}, bf16[640,1536]{1,0:T(8,128)(2,1)}, f32[8,768]{1,0:T(8,128)}) custom-call(s32[1,1408]{1,0:T(1,128)} %copy-done.24, bf16[768,768]{1,0:T(8,128)(2,1)} %get-tuple-element.43.q_ref, bf16[768,768]{1,0:T(8,128)(2,1)} %convolution_convert_fusion.2.g_ref, bf16[768,768]{1,0:T(8,128)(2,1)} %get-tuple-element.44.k_own_ref, ...), custom_call_target="tpu_custom_call" | custom-call | flops 8304721920 | bytes 17301504 | tf_op jit(solution)/shard_map/attend_back/pallas_call | solution.py:402
  223.6 5.2 %fusion.17 = bf16[640,768]{1,0:T(8,128)(2,1)} fusion(bf16[640,1536]{1,0:T(8,128)(2,1)} %get-tuple-element.61, bf16[768,2304]{1,0:T(8,128)(2,1)} %w_ref.3), kind=kOutput, calls=%fused_computation.40 | convolution fusion | flops 1510440960 | bytes 5308416 | tf_op jit(solution)/shard_map/dot_general | solution.py:31
  228.8 2.2 convolution_convert_fusion
  231.0 0.6 copy-done.50
  231.6 2.0 fusion.13
  233.7 2.1 convolution_convert_fusion.1
  235.8 3.6 add_convert_fusion.2
  239.5 1.0 slice_reduce_fusion.15
  240.5 8.6 %collective-permute-done.5 = bf16[640,768]{1,0:T(8,128)(2,1)} collective-permute-done((bf16[640,768]{1,0:T(8,128)(2,1)}, bf16[640,768]{1,0:T(8,128)(2,1)}, u32[]{:S(2)}, u32[]{:S(2)}) %collective-permute-start.5) | collective-permute-done | bytes 983072 | tf_op jit(solution)/shard_map/ppermute | solution.py:529
  249.2 1.3 constant_dynamic-update-slice_fusion
  250.7 8.6 %fusion.10 = (f32[768]{0:T(1024)S(1)}, f32[768]{0:T(1024)}, f32[768]{0:T(1024)}, f32[768]{0:T(1024)S(1)}, f32[768,768]{1,0:T(8,128)}) fusion(bf16[768,768]{1,0:T(8,128)(2,1)S(1)} %copy-done.3, f32[768]{0:T(1024)S(1)} %copy-done.17, f32[768]{0:T(1024)S(1)} %broadcast_multiply_fusion.1, f32[768]{0:T(1024)S(1)} %copy-done.16, ...), kind=kOutput, calls=%fused_computation.19 | convolution fusion | flops 2724983808 | bytes 11817984 | tf_op jit(solution)/shard_map/dot_general | solution.py:31
  259.5 0.7 select_select_fusion
  260.2 50.1 %psum.42 = f32[16,768]{1,0:T(8,128)} all-reduce(f32[16,768]{1,0:T(8,128)} %select_select_fusion), channel_id=1, replica_groups=mesh['dp'=16,'mlp'=2] {'dp','mlp'}, use_global_device_ids=true, to_apply=%region_14.15 | all-reduce | flops 12288 | bytes 98304 | tf_op jit(solution)/shard_map/psum | solution.py:605
  310.2 1.4 constant_dynamic-slice_fusion
  311.6 0.7 reshape.117
  312.3 0.8 reduce_sum.157
  313.1 0.7 reshape.118
  313.7 1.3 reshape.119
  315.0 1.7 slice_reduce_fusion
  316.7 0.6 pad_maximum_fusion.1
  317.3 0.7 broadcast_multiply_fusion
  318.0 0.7 broadcast_multiply_fusion.2
  318.7 3.1 fusion.9
  321.8 4.6 %convert_element_type.81 = f32[768,1536]{1,0:T(8,128)} convert(bf16[768,1536]{1,0:T(8,128)(2,1)} %get-tuple-element.98) | non-fusion elementwise | flops 1179648 | bytes 7077888 | tf_op jit(solution)/shard_map/convert_element_type | solution.py:612
  326.4 2.5 convert_element_type.83
  329.0 83.2 %all-reduce.5.cloned.1.call-done = (bf16[768,1536]{1,0:T(8,128)(2,1)}, bf16[768,768]{1,0:T(8,128)(2,1)}, bf16[768,768]{1,0:T(8,128)(2,1)}) async-done(((bf16[768,1536]{1,0:T(8,128)(2,1)}, bf16[768,768]{1,0:T(8,128)(2,1)}, bf16[768,768]{1,0:T(8,128)(2,1)}), (bf16[768,1536]{1,0:T(8,128)(2,1)}, bf16[768,768]{1,0:T(8,128)(2,1)}, bf16[768,768]{1,0:T(8,128)(2,1)})) %all-reduce.5.cloned.1.call-update) | async-done | bytes 4718608 | tf_op jit(solution)/shard_map/psum | solution.py:604
  412.2 3.0 convert_element_type.79
  415.2 3.4 maximum_convert_fusion
  (143 shorter events, 8.4 us)
Async XLA Ops:
  7.2 64.4 %copy-start = (bf16[768,768]{1,0:T(8,128)(2,1)S(1)}, bf16[768,768]{1,0:T(8,128)(2,1)}, u32[]{:S(2)}) copy-start(bf16[768,768]{1,0:T(8,128)(2,1)} %param.27) | copy-start | bytes 3538948
  7.2 8.7 %copy-start.2 = (bf16[768,768]{1,0:T(8,128)(2,1)S(1)}, bf16[768,768]{1,0:T(8,128)(2,1)}, u32[]{:S(2)}) copy-start(bf16[768,768]{1,0:T(8,128)(2,1)} %x_ref.1) | copy-start | bytes 3538948
  7.2 314.6 %all-reduce.7.cloned.1.call-start = ((), (), s32[]{:S(2)}) async-start(), calls=%async_computation.1 | async-start | bytes 9437184 | tf_op jit(solution)/shard_map/psum | solution.py:603
  7.3 14.2 %copy-start.25 = (f32[2304]{0:T(1024)S(1)}, f32[2304]{0:T(1024)}, u32[]{:S(2)}) copy-start(f32[2304]{0:T(1024)} %param.25) | copy-start | bytes 27652
  7.3 14.8 %copy-start.15 = (f32[768]{0:T(1024)S(1)}, f32[768]{0:T(1024)}, u32[]{:S(2)}) copy-start(f32[768]{0:T(1024)} %param.22) | copy-start | bytes 9220
  7.3 15.4 %copy-start.29 = (f32[768]{0:T(1024)S(1)}, f32[768]{0:T(1024)}, u32[]{:S(2)}) copy-start(f32[768]{0:T(1024)} %param.23) | copy-start | bytes 9220
  7.3 16.0 %copy-start.30 = (f32[2,384]{1,0:T(2,128)S(1)}, f32[2,384]{1,0:T(2,128)}, u32[]{:S(2)}) copy-start(f32[2,384]{1,0:T(2,128)} %param.26) | copy-start | bytes 9220
  7.3 19.3 %copy-start.26 = (f32[1536]{0:T(1024)S(1)}, f32[1536]{0:T(1024)}, u32[]{:S(2)}) copy-start(f32[1536]{0:T(1024)} %param.32) | copy-start | bytes 18436
  8.7 33.7 %collective-permute-start = (bf16[640,768]{1,0:T(8,128)(2,1)S(1)}, bf16[640,768]{1,0:T(8,128)(2,1)}, u32[]{:S(2)}, u32[]{:S(2)}) collective-permute-start(bf16[640,768]{1,0:T(8,128)(2,1)S(1)} %constant_dynamic-slice_fusion.3), channel_id=1, source_target_pairs={{0,1},{1,0},{2,3},{3,2},{4,5},{5,4},{6,7},{7,6},{8,9},{9,8},{10,11... | collective-permute-start | bytes 2949128 | tf_op jit(solution)/shard_map/ppermute | solution.py:529
  11.8 94.4 %collective-permute-start.2 = (bf16[768,768]{1,0:T(8,128)(2,1)}, bf16[768,768]{1,0:T(8,128)(2,1)}, u32[]{:S(2)}, u32[]{:S(2)}) collective-permute-start(bf16[768,768]{1,0:T(8,128)(2,1)} %g_ref.1), channel_id=1, source_target_pairs={{0,1},{1,0},{2,3},{3,2},{4,5},{5,4},{6,7},{7,6},{8,9},{9,8},{10,11... | collective-permute-start | bytes 3538952 | tf_op jit(solution)/shard_map/ppermute | solution.py:529
  14.8 14.7 %copy-start.24 = (s32[1,1408]{1,0:T(1,128)}, s32[1,1408]{1,0:T(1,128)S(1)}, u32[]{:S(2)}) copy-start(s32[1,1408]{1,0:T(1,128)S(1)} %broadcast_in_dim.132.ids_ref) | copy-start | bytes 16900
  30.0 220.5 %copy-start.14 = (f32[768]{0:T(1024)}, f32[768]{0:T(1024)S(1)}, u32[]{:S(2)}) copy-start(f32[768]{0:T(1024)S(1)} %broadcast_multiply_fusion.1) | copy-start | bytes 9220
  50.7 20.8 %copy-start.44 = (f32[768]{0:T(1024)S(1)}, f32[768]{0:T(1024)}, u32[]{:S(2)}) copy-start(f32[768]{0:T(1024)} %param.28) | copy-start | bytes 9220
  74.4 0.7 copy-start.13
  74.4 0.7 copy-start.27
  76.6 29.7 %collective-permute-start.1 = (bf16[768,768]{1,0:T(8,128)(2,1)}, bf16[768,768]{1,0:T(8,128)(2,1)}, u32[]{:S(2)}, u32[]{:S(2)}) collective-permute-start(bf16[768,768]{1,0:T(8,128)(2,1)} %add_convert_fusion.4.n2_ref), channel_id=1, source_target_pairs={{0,1},{1,0},{2,3},{3,2},{4,5},{5,4},{6,7},{7,6},{8,9},{9,8},{10,11... | collective-permute-start | bytes 3538952 | tf_op jit(solution)/shard_map/ppermute | solution.py:529
  95.5 6.4 %copy-start.10 = (bf16[768,768]{1,0:T(8,128)(2,1)S(1)}, bf16[768,768]{1,0:T(8,128)(2,1)}, u32[]{:S(2)}) copy-start(bf16[768,768]{1,0:T(8,128)(2,1)} %g_ref.1) | copy-start | bytes 3538948
  95.5 6.4 %copy-start.49 = (bf16[768,1536]{1,0:T(8,128)(2,1)S(1)}, bf16[768,1536]{1,0:T(8,128)(2,1)}, u32[]{:S(2)}) copy-start(bf16[768,1536]{1,0:T(8,128)(2,1)} %get-tuple-element.69) | copy-start | bytes 7077892
  124.0 29.2 %collective-permute-start.4 = (bf16[768,768]{1,0:T(8,128)(2,1)}, bf16[768,768]{1,0:T(8,128)(2,1)}, u32[]{:S(2)}, u32[]{:S(2)}) collective-permute-start(bf16[768,768]{1,0:T(8,128)(2,1)} %get-tuple-element.53), channel_id=1, source_target_pairs={{0,1},{1,0},{2,3},{3,2},{4,5},{5,4},{6,7},{7,6},{8,9},{9,8},{10,11... | collective-permute-start | bytes 3538952 | tf_op jit(solution)/shard_map/ppermute | solution.py:529
  125.8 50.1 %collective-permute-start.3 = (bf16[768,768]{1,0:T(8,128)(2,1)}, bf16[768,768]{1,0:T(8,128)(2,1)}, u32[]{:S(2)}, u32[]{:S(2)}) collective-permute-start(bf16[768,768]{1,0:T(8,128)(2,1)} %get-tuple-element.51), channel_id=1, source_target_pairs={{0,1},{1,0},{2,3},{3,2},{4,5},{5,4},{6,7},{7,6},{8,9},{9,8},{10,11... | collective-permute-start | bytes 3538952 | tf_op jit(solution)/shard_map/ppermute | solution.py:529
  126.0 7.0 %copy-start.47 = (f32[1536,768]{1,0:T(8,128)S(1)}, f32[1536,768]{1,0:T(8,128)}, u32[]{:S(2)}) copy-start(f32[1536,768]{1,0:T(8,128)} %fusion.34) | copy-start | bytes 14155780
  126.1 7.0 %copy-start.52 = (bf16[768,1536]{1,0:T(8,128)(2,1)S(1)}, bf16[768,1536]{1,0:T(8,128)(2,1)}, u32[]{:S(2)}) copy-start(bf16[768,1536]{1,0:T(8,128)(2,1)} %get-tuple-element.70) | copy-start | bytes 7077892
  137.8 274.4 %all-reduce.5.cloned.1.call-start = ((), (), s32[]{:S(2)}) async-start(), calls=%async_computation | async-start | bytes 9437184 | tf_op jit(solution)/shard_map/psum | solution.py:604
  153.2 22.8 %copy-start.6 = (f32[768,768]{1,0:T(8,128)S(1)}, f32[768,768]{1,0:T(8,128)}, u32[]{:S(2)}) copy-start(f32[768,768]{1,0:T(8,128)} %get-tuple-element.52) | copy-start | bytes 7077892
  153.2 22.8 %copy-start.8 = (f32[768,768]{1,0:T(8,128)S(1)}, f32[768,768]{1,0:T(8,128)}, u32[]{:S(2)}) copy-start(f32[768,768]{1,0:T(8,128)} %get-tuple-element.50) | copy-start | bytes 7077892
  153.2 22.8 %copy-start.11 = (bf16[768,768]{1,0:T(8,128)(2,1)S(1)}, bf16[768,768]{1,0:T(8,128)(2,1)}, u32[]{:S(2)}) copy-start(bf16[768,768]{1,0:T(8,128)(2,1)} %g_ref.1) | copy-start | bytes 3538948
  153.2 22.8 %copy-start.28 = (f32[768]{0:T(1024)S(1)}, f32[768]{0:T(1024)}, u32[]{:S(2)}) copy-start(f32[768]{0:T(1024)} %param.34) | copy-start | bytes 9220
  180.9 2.2 copy-start.4
  223.6 5.2 %copy-start.5 = (f32[768,768]{1,0:T(8,128)S(1)}, f32[768,768]{1,0:T(8,128)}, u32[]{:S(2)}) copy-start(f32[768,768]{1,0:T(8,128)} %copy-done.4) | copy-start | bytes 7077892
  223.6 5.2 %copy-start.51 = (bf16[768,768]{1,0:T(8,128)(2,1)S(1)}, bf16[768,768]{1,0:T(8,128)(2,1)}, u32[]{:S(2)}) copy-start(bf16[768,768]{1,0:T(8,128)(2,1)} %get-tuple-element.49) | copy-start | bytes 3538948
  228.8 2.2 copy-start.45
  228.8 2.8 copy-start.50
  228.8 20.3 %collective-permute-start.5 = (bf16[640,768]{1,0:T(8,128)(2,1)}, bf16[640,768]{1,0:T(8,128)(2,1)}, u32[]{:S(2)}, u32[]{:S(2)}) collective-permute-start(bf16[640,768]{1,0:T(8,128)(2,1)} %fusion.17), channel_id=1, source_target_pairs={{0,1},{1,0},{2,3},{3,2},{4,5},{5,4},{6,7},{7,6},{8,9},{9,8},{10,11... | collective-permute-start | bytes 2949128 | tf_op jit(solution)/shard_map/ppermute | solution.py:529
  233.7 2.2 copy-start.46
  233.7 2.2 copy-start.48
  239.5 11.0 %copy-start.3 = (bf16[768,768]{1,0:T(8,128)(2,1)S(1)}, bf16[768,768]{1,0:T(8,128)(2,1)}, u32[]{:S(2)}) copy-start(bf16[768,768]{1,0:T(8,128)(2,1)} %x_ref.1) | copy-start | bytes 3538948
  239.5 11.0 %copy-start.16 = (f32[768]{0:T(1024)S(1)}, f32[768]{0:T(1024)}, u32[]{:S(2)}) copy-start(f32[768]{0:T(1024)} %param.22) | copy-start | bytes 9220
  239.5 11.0 %copy-start.17 = (f32[768]{0:T(1024)S(1)}, f32[768]{0:T(1024)}, u32[]{:S(2)}) copy-start(f32[768]{0:T(1024)} %add_rsqrt_fusion) | copy-start | bytes 9220
  250.5 8.8 %copy-start.18 = (f32[768]{0:T(1024)S(1)}, f32[768]{0:T(1024)}, u32[]{:S(2)}) copy-start(f32[768]{0:T(1024)} %get-tuple-element.71) | copy-start | bytes 9220
  250.5 8.8 %copy-start.19 = (f32[768]{0:T(1024)S(1)}, f32[768]{0:T(1024)}, u32[]{:S(2)}) copy-start(f32[768]{0:T(1024)} %get-tuple-element.76) | copy-start | bytes 9220
  250.5 8.8 %copy-start.20 = (f32[768]{0:T(1024)S(1)}, f32[768]{0:T(1024)}, u32[]{:S(2)}) copy-start(f32[768]{0:T(1024)} %get-tuple-element.100) | copy-start | bytes 9220
  250.6 8.8 %copy-start.21 = (f32[768]{0:T(1024)S(1)}, f32[768]{0:T(1024)}, u32[]{:S(2)}) copy-start(f32[768]{0:T(1024)} %get-tuple-element.103) | copy-start | bytes 9220
  250.6 8.7 %copy-start.22 = (f32[768]{0:T(1024)S(1)}, f32[768]{0:T(1024)}, u32[]{:S(2)}) copy-start(f32[768]{0:T(1024)} %get-tuple-element.93) | copy-start | bytes 9220
  250.6 8.7 %copy-start.23 = (f32[768]{0:T(1024)S(1)}, f32[768]{0:T(1024)}, u32[]{:S(2)}) copy-start(f32[768]{0:T(1024)} %get-tuple-element.94) | copy-start | bytes 9220
  250.6 8.7 %copy-start.31 = (pred[16]{0:T(512)(128)(4,1)S(1)}, pred[16]{0:T(512)(128)(4,1)}, u32[]{:S(2)}) copy-start(pred[16]{0:T(512)(128)(4,1)} %get-tuple-element.121) | copy-start | bytes 52
  250.6 8.7 %copy-start.32 = (pred[16]{0:T(512)(128)(4,1)S(1)}, pred[16]{0:T(512)(128)(4,1)}, u32[]{:S(2)}) copy-start(pred[16]{0:T(512)(128)(4,1)} %get-tuple-element.122) | copy-start | bytes 52
  250.6 8.7 %copy-start.33 = (pred[16]{0:T(512)(128)(4,1)S(1)}, pred[16]{0:T(512)(128)(4,1)}, u32[]{:S(2)}) copy-start(pred[16]{0:T(512)(128)(4,1)} %get-tuple-element.123) | copy-start | bytes 52
  250.6 8.7 %copy-start.34 = (pred[16]{0:T(512)(128)(4,1)S(1)}, pred[16]{0:T(512)(128)(4,1)}, u32[]{:S(2)}) copy-start(pred[16]{0:T(512)(128)(4,1)} %get-tuple-element.124) | copy-start | bytes 52
  250.6 8.7 %copy-start.35 = (pred[16]{0:T(512)(128)(4,1)S(1)}, pred[16]{0:T(512)(128)(4,1)}, u32[]{:S(2)}) copy-start(pred[16]{0:T(512)(128)(4,1)} %get-tuple-element.125) | copy-start | bytes 52
  250.6 8.7 %copy-start.36 = (pred[16]{0:T(512)(128)(4,1)S(1)}, pred[16]{0:T(512)(128)(4,1)}, u32[]{:S(2)}) copy-start(pred[16]{0:T(512)(128)(4,1)} %get-tuple-element.126) | copy-start | bytes 52
  250.7 8.7 %copy-start.37 = (pred[16]{0:T(512)(128)(4,1)S(1)}, pred[16]{0:T(512)(128)(4,1)}, u32[]{:S(2)}) copy-start(pred[16]{0:T(512)(128)(4,1)} %get-tuple-element.127) | copy-start | bytes 52
  250.7 8.7 %copy-start.38 = (pred[16]{0:T(512)(128)(4,1)S(1)}, pred[16]{0:T(512)(128)(4,1)}, u32[]{:S(2)}) copy-start(pred[16]{0:T(512)(128)(4,1)} %get-tuple-element.128) | copy-start | bytes 52
  250.7 8.7 %copy-start.39 = (pred[16]{0:T(512)(128)(4,1)S(1)}, pred[16]{0:T(512)(128)(4,1)}, u32[]{:S(2)}) copy-start(pred[16]{0:T(512)(128)(4,1)} %get-tuple-element.129) | copy-start | bytes 52
  250.7 8.7 %copy-start.40 = (pred[16]{0:T(512)(128)(4,1)S(1)}, pred[16]{0:T(512)(128)(4,1)}, u32[]{:S(2)}) copy-start(pred[16]{0:T(512)(128)(4,1)} %get-tuple-element.130) | copy-start | bytes 52
  250.7 8.7 %copy-start.41 = (pred[16]{0:T(512)(128)(4,1)S(1)}, pred[16]{0:T(512)(128)(4,1)}, u32[]{:S(2)}) copy-start(pred[16]{0:T(512)(128)(4,1)} %get-tuple-element.131) | copy-start | bytes 52
  250.7 8.7 %copy-start.42 = (pred[16]{0:T(512)(128)(4,1)S(1)}, pred[16]{0:T(512)(128)(4,1)}, u32[]{:S(2)}) copy-start(pred[16]{0:T(512)(128)(4,1)} %get-tuple-element.132) | copy-start | bytes 52
  250.7 8.7 %copy-start.43 = (pred[16]{0:T(512)(128)(4,1)S(1)}, pred[16]{0:T(512)(128)(4,1)}, u32[]{:S(2)}) copy-start(pred[16]{0:T(512)(128)(4,1)} %iota_compare_fusion.12) | copy-start | bytes 52
  321.8 4.7 %copy-start.7 = (bf16[1536,768]{1,0:T(8,128)(2,1)S(1)}, bf16[1536,768]{1,0:T(8,128)(2,1)}, u32[]{:S(2)}) copy-start(bf16[1536,768]{1,0:T(8,128)(2,1)} %get-tuple-element.99) | copy-start | bytes 7077892
  412.2 3.0 copy-start.9
  412.2 3.0 copy-start.12
  415.2 3.4 copy-start.1
Sparse Core Ops, SparseCore 0:
  137.9 121.3 all-reduce.6
  266.1 146.0 all-reduce.4

commit v3 on v2

--- a/solution.py
+++ b/solution.py
@@ -519,6 +519,26 @@
     return back, jnp.sum(grad * unit, axis=0), jnp.sum(grad, axis=0)
 
 
+def other_core(a):
+    return lax.ppermute(a, "core", [(0, 1), (1, 0)])
+
+
+def chip_halves(arrays):
+    core = lax.axis_index("core")
+    halves = [a.reshape(2, a.shape[0] // 2, a.shape[1]) for a in arrays]
+    given = [other_core(lax.dynamic_index_in_dim(a, 1 - core, 0, keepdims=False)) for a in halves]
+    kept = [lax.dynamic_index_in_dim(a, core, 0, keepdims=False) for a in halves]
+    return [(a.astype(F32) + b.astype(F32)).astype(BF) for a, b in zip(kept, given)]
+
+
+def join_halves(mine):
+    first = lax.axis_index("core") == 0
+    theirs = [other_core(a) for a in mine]
+    return [
+        jnp.concatenate([jnp.where(first, a, b), jnp.where(first, b, a)], axis=0) for a, b in zip(mine, theirs)
+    ]
+
+
 def per_device(
     axes, patches, image_of_patch, patch_row, patch_col, ln1_gain, ln1_bias, w_qkv, b_qkv, freqs, w_out, b_out,
     ln2_gain, ln2_bias, w_up, b_up, w_down, b_down, out_cotangent,
@@ -531,7 +551,7 @@
     mine_start = jnp.where(me == 0, own - edge, 0)
     edge_start = jnp.where(me == 0, own, own - edge)
     x_edge = swap(lax.dynamic_slice_in_dim(patches, mine_start, edge))
-    g_other = swap(out_cotangent)
+    g_other = swap(lax.optimization_barrier((out_cotangent, x_edge))[0])
 
     def local(a):
         return jnp.concatenate(
@@ -563,10 +583,13 @@
     hid_a, gp_a, out_a, back_a, sum_a = ffn(normed2, out_cotangent, w_up, bias_up, w_down, F32)
     hid_b, gp_b, out_b, back_b, sum_b = ffn(n2_other, g_other, w_up, bias_up, w_down, BF)
     back_in = swap(back_b)
-    out_in = swap(out_b)
+    out_in = swap(lax.optimization_barrier((out_b, back_in))[0])
     grad_b_up = sum_a[0] + sum_b[0]
     grad_w_up = (dot_tn(normed2, gp_a) + dot_tn(n2_other, gp_b)).astype(BF)
     grad_w_down = (dot_tn(hid_a, out_cotangent) + dot_tn(hid_b, g_other)).astype(BF)
+    ffn_halves = chip_halves([grad_w_up, grad_w_down])
+    ffn_halves, back_in = lax.optimization_barrier((ffn_halves, back_in))
+    ffn_halves = lax.psum(tuple(ffn_halves), "chip")
     block_out = (middle + out_a + out_in.astype(F32) + b_down).astype(BF)
     grad_out = out_cotangent.astype(F32)
     grad_n2 = back_a + back_in.astype(F32)
@@ -577,6 +600,8 @@
     grad_b_out = jnp.sum(grad_attended.astype(F32), axis=0)
     grad_w_out = dot_tn(mixed, grad_attended).astype(BF)
     grad_mixed = dot_nt(grad_attended, w_out).astype(BF)
+    out_half, grad_mixed = lax.optimization_barrier((chip_halves([grad_w_out])[0], grad_mixed))
+    out_half = lax.psum(out_half, ("chip", "mlp"))
     d_own, d_edge, sums = attend_back(
         id_row, q, grad_mixed, k_own, k_edge, v_own, v_edge, id_col, id_own, out_t, lse, row_pos, col_pos,
         (cos_own, sin_own, cos_edge, sin_edge),
@@ -590,35 +615,35 @@
     from_norm1, grad_ln1_gain, grad_ln1_bias = norm_back(inputs, ln1_gain, grad_normed)
     grad_patches = (grad_middle + from_norm1).astype(BF)
     everyone = axes + ("mlp",)
-    units = b_up.shape[0] // width
-    lines = [grad_ln1_gain, grad_ln1_bias] + [sums[i] for i in range(5)]
-    lines += [grad_b_out, grad_ln2_gain, grad_ln2_bias, grad_b_down]
-    count = len(lines)
-    line = lax.broadcasted_iota(jnp.int32, (16, width), 0)
-    small = jnp.zeros((16, width), F32)
-    for i, values in enumerate(lines):
-        small = jnp.where(line == i, values[None], small)
-    for i in range(units):
-        small = jnp.where(line == count + me * units + i, grad_b_up[None, i * width : (i + 1) * width], small)
-    grad_w_up, grad_w_down = lax.psum((grad_w_up, grad_w_down), axes)
-    grad_w_q, grad_w_kv, grad_w_out = lax.psum((grad_w_q, grad_w_kv, grad_w_out), everyone)
-    total = lax.psum(small, everyone)
-    grad_b_up = lax.dynamic_slice_in_dim(total, count + me * units, units).reshape(units * width)
+    units = b_up.shape[0]
+    slots = lax.dynamic_update_slice_in_dim(jnp.zeros((2 * units,), F32), grad_b_up, me * units, 0)
+    lines = [grad_ln1_gain, grad_ln1_bias, grad_b_out, grad_ln2_gain, grad_ln2_bias, grad_b_down, sums, slots]
+    chips = ("chip", "mlp")
+    halves = chip_halves([grad_w_q, grad_w_kv])
+    halves, lines, out_half = lax.optimization_barrier((halves, lines, out_half))
+    halves, lines = lax.optimization_barrier((lax.psum(tuple(halves), chips), lax.psum(tuple(lines), everyone)))
+    grad_w_up, grad_w_down = join_halves(ffn_halves)
+    grad_w_out = join_halves([out_half])[0]
+    grad_w_q, grad_w_kv = join_halves(halves)
+    grad_ln1_gain, grad_ln1_bias, grad_b_out, grad_ln2_gain, grad_ln2_bias, grad_b_down, sums, slots = lines
+    grad_b_up = lax.dynamic_slice_in_dim(slots, me * units, units)
     grad_w_qkv = jnp.concatenate([grad_w_q, grad_w_kv], axis=1).astype(F32)
-    grad_freqs = jnp.sum(total[5:7].reshape(2, H, 2, HD // 2), axis=2).reshape(2, width // 2)
-    total = [total[i] for i in range(count)]
+    grad_freqs = jnp.sum(sums[3:5].reshape(2, H, 2, HD // 2), axis=2).reshape(2, width // 2)
     return (
-        block_out, grad_patches, total[0], total[1], grad_w_qkv, jnp.concatenate(total[2:5]), grad_freqs,
-        grad_w_out.astype(F32), total[7], total[8], total[9], grad_w_up.astype(F32), grad_b_up,
-        grad_w_down.astype(F32), total[10],
+        block_out, grad_patches, grad_ln1_gain, grad_ln1_bias, grad_w_qkv, sums[:3].reshape(3 * width), grad_freqs,
+        grad_w_out.astype(F32), grad_b_out, grad_ln2_gain, grad_ln2_bias, grad_w_up.astype(F32), grad_b_up,
+        grad_w_down.astype(F32), grad_b_down,
     )
 
 
 def solution(mesh):
-    rows = P(("dp", "mlp"), None)
-    group = P("dp", None)
+    shape = (mesh.shape["dp"] // 2, 2, mesh.shape["mlp"])
+    mesh = jax.sharding.Mesh(mesh.devices.reshape(shape), ("chip", "core", "mlp"))
+    dp = ("chip", "core")
+    rows = P(dp + ("mlp",), None)
+    group = P(dp, None)
     in_specs = (rows, group, group, group) + (P(),) * 9 + (P(None, "mlp"), P("mlp"), P("mlp", None), P(), rows)
     out_specs = (rows, rows) + (P(),) * 9 + (P(None, "mlp"), P("mlp"), P("mlp", None), P())
     return jax.shard_map(
-        partial(per_device, ("dp",)), mesh=mesh, in_specs=in_specs, out_specs=out_specs, check_vma=False
+        partial(per_device, dp), mesh=mesh, in_specs=in_specs, out_specs=out_specs, check_vma=False
     )

time: 428 us -> 602 us (1.41); the launches traced: 426 us -> 593 us
  waiting for transfers between devices: 125 us -> 260 us
  other arithmetic: 37.1 us -> 56.5 us
  Pallas kernels: 117 us -> 129 us
  starting transfers between devices: 5.57 us -> 16.6 us
  blocking collectives: 50.1 us -> 42 us
    psum x2 -> x3, waiting for transfers between devices: 83.2 us -> 220 us  [the longest x1 99.9 us: per_device(): out_half = lax.psum(out_half, ('chip', 'mlp'))]
    convert_element_type x0 -> x5, other arithmetic: none -> 12.4 us  [chip_halves(): (a.astype(F32) + b.astype(F32)).astype(BF)]
    pallas_call x2, Pallas kernels: 36.4 us -> 47.7 us  [ffn(): pl.pallas_call(ffn_kernel, grid=(units // block,), in_specs=[whole, whole...]
    psum x1, blocking collectives: 50.1 us -> 42 us  [per_device(): lax.psum(tuple(lines), everyone)]
    convert_element_type x1, other arithmetic: 3.44 us -> 9.95 us  [per_device(): grad_w_qkv = jnp.concatenate([grad_w_q, grad_w_kv], axis=1).astype(F32)]
  transfers between devices with their start and end apart: 8 -> 19, of which waited for: 4 -> 6; matrix products, arithmetic and copies ran while one was open for 24% -> 16% of each run, Pallas kernels for 23% -> 14%
where the time goes in v3:
time: 602 us; the launch traced here: 593 us
  waiting for transfers between devices  260 us (43%)
  Pallas kernels  129 us (21%)
  other arithmetic  56.5 us (9%)
  matrix products  45 us (7%)
  blocking collectives  42 us (7%)
  local copies, waits for them, and re-layouts  29.2 us (5%)
  starting transfers between devices  16.6 us (3%)
  between operations  14.6 us (2%)
    psum x1, waiting for transfers between devices, per_device(): out_half = lax.psum(out_half, ('chip', 'mlp'))  99.9 us
    psum x1, waiting for transfers between devices, per_device(): lax.psum(tuple(halves), chips)  76 us
    pallas_call x2, Pallas kernels, ffn(): pl.pallas_call(ffn_kernel, grid=(units // block,), in_specs=[whole, whole...  47.7 us
    psum x1, waiting for transfers between devices, per_device(): ffn_halves = lax.psum(tuple(ffn_halves), 'chip')  43.7 us
    psum x1, blocking collectives, per_device(): lax.psum(tuple(lines), everyone)  42 us
    pallas_call x1, Pallas kernels, attend_back(): pl.pallas_call(attend_back_kernel, grid=(own // QUERY_TILE,), in_specs=[p...  40.7 us
    ppermute x6, waiting for transfers between devices, per_device(): swap = lambda a: lax.ppermute(a, 'mlp', other)  40.5 us
    dot_general x8, matrix products, dot_tn(): lax.dot_general(left, right, (((0,), (0,)), ((), ())), preferred_element_...  27.3 us
  transfers between devices with their start and end apart: 19, of which 6 were waited for; matrix products, arithmetic and copies ran while one was open for 16% of the time, Pallas kernels for 14%

profile of v3, /device:TPU:0, one launch (start us, length us, event | category | flops | bytes accessed | tf_op | source)
XLA Modules:
  0.0 592.6 jit_solution(710050366803675951)
XLA Ops:
  7.3 1.3 constant_dynamic-slice_fusion.2
  8.7 3.1 collective-permute-start
  13.2 1.1 broadcast_in_dim.58.idk_ref
  15.3 0.9 copy.38.col_ref
  22.5 1.1 broadcast_in_dim.56.row_ref
  23.6 11.2 %ln_qkv_rope.2 = (bf16[768,768]{1,0:T(8,128)(2,1)}, bf16[768,768]{1,0:T(8,128)(2,1)}, bf16[768,768]{1,0:T(8,128)(2,1)}, f32[768,768]{1,0:T(8,128)}, f32[768,768]...) custom-call(bf16[768,768]{1,0:T(8,128)(2,1)} %x_ref.1, s32[768,1]{1,0:T(8,128)} %copy.37.row_ref, ...), custom_call_target="tpu_custom_call" | custom-call | flops 3623878656 | bytes 9437184 | tf_op jit(solution)/shard_map/ln_qkv_rope/pallas_call | solution.py:125
  35.8 8.2 %ln_qkv_rope.3 = (bf16[640,768]{1,0:T(8,128)(2,1)}, bf16[640,768]{1,0:T(8,128)(2,1)}, bf16[640,768]{1,0:T(8,128)(2,1)}, f32[640,768]{1,0:T(8,128)}, f32[640,768]{1,0:T(8,128)}) custom-call(bf16[640,768]{1,0:T(8,128)(2,1)} %copy-done.35, s32[640,1]{1,0:T(8,128)} %copy.39.row_ref, s32[640,1]{1,0:T(8,128)} %copy.40.col_ref, ...), custom_call_target="tpu_custom_call" | custom-call | flops 2264924160 | bytes 8454144 | tf_op jit(solution)/shard_map/ln_qkv_rope/pallas_call | solution.py:125
  44.0 20.8 %attend.1 = (bf16[768,768]{1,0:T(8,128)(2,1)}, f32[768,768]{1,0:T(8,128)}, f32[16,768]{1,0:T(8,128)}) custom-call(s32[1,1408]{1,0:T(1,128)} %copy-done.25, bf16[768,768]{1,0:T(8,128)(2,1)} %get-tuple-element.71.q_ref, bf16[768,768]{1,0:T(8,128)(2,1)} %get-tuple-element.72.k_own_ref, bf16[640,768]{1,0:T(8,128)(2,1)} %get-tuple-element.74.k_edge_ref, ...), custom_call_target="tpu_custom_call" | custom-call | flops 3321888768 | bytes 8650752 | tf_op jit(solution)/shard_map/attend/pallas_call | solution.py:228
  64.8 2.8 fusion.39
  68.4 1.4 add_convert_fusion.4.n2_ref
  69.8 1.3 collective-permute-start.1
  71.8 30.0 %ffn.2 = (bf16[768,1536]{1,0:T(8,128)(2,1)}, bf16[768,1536]{1,0:T(8,128)(2,1)}, f32[768,768]{1,0:T(8,128)}, f32[768,768]{1,0:T(8,128)}, f32[8,1536]{1,0:T(8,128)}) custom-call(bf16[768,768]{1,0:T(8,128)(2,1)} %add_convert_fusion.4.n2_ref, bf16[768,768]{1,0:T(8,128)(2,1)} %g_ref.1, bf16[768,1536]{1,0:T(8,128)(2,1)} %up_ref.3, ...), custom_call_target="tpu_custom_call" | custom-call | flops 7247757312 | bytes 14155776 | tf_op jit(solution)/shard_map/ffn/pallas_call | solution.py:484
  101.8 6.4 %fusion.40 = f32[768,1536]{1,0:T(8,128)} fusion(bf16[768,768]{1,0:T(8,128)(2,1)} %add_convert_fusion.4.n2_ref, bf16[768,1536]{1,0:T(8,128)(2,1)} %get-tuple-element.84), kind=kOutput, calls=%fused_computation.105 | convolution fusion | flops 1811939328 | bytes 8257536 | tf_op jit(solution)/shard_map/dot_general | solution.py:35
  108.2 5.5 fusion.41
  113.8 8.5 %collective-permute-done.2.g_ref = bf16[768,768]{1,0:T(8,128)(2,1)} collective-permute-done((bf16[768,768]{1,0:T(8,128)(2,1)}, bf16[768,768]{1,0:T(8,128)(2,1)}, u32[]{:S(2)}, u32[]{:S(2)}) %collective-permute-start.2) | collective-permute-done | bytes 1179680 | tf_op jit(solution)/shard_map/ppermute | solution.py:549
  122.2 17.7 %ffn.3 = (bf16[768,1536]{1,0:T(8,128)(2,1)}, bf16[768,1536]{1,0:T(8,128)(2,1)}, bf16[768,768]{1,0:T(8,128)(2,1)}, bf16[768,768]{1,0:T(8,128)(2,1)}, f32[8,1536]{1,0:T(8,128)}) custom-call(bf16[768,768]{1,0:T(8,128)(2,1)} %collective-permute-done.1.n2_ref, bf16[768,768]{1,0:T(8,128)(2,1)} %collective-permute-done.2.g_ref, bf16[768,1536]{1,0:T(8,128)(2,1)} %up_ref.3, ...), custom_call_target="tpu_custom_call" | custom-call | flops 7247757312 | bytes 14155776 | tf_op jit(solution)/shard_map/ffn/pallas_call | solution.py:484
  140.0 5.6 add_convert_fusion.2
  145.6 1.1 dynamic-slice_bitcast_fusion.2
  146.7 1.8 collective-permute-start.5
  148.5 1.3 collective-permute-start.3
  149.8 3.3 add_convert_fusion.1
  153.2 1.4 copy-done.11
  154.5 1.2 dynamic-slice_bitcast_fusion.1
  156.3 1.2 broadcast_in_dim.57.col_ref
  157.4 1.6 convert_reduce_fusion
  159.1 2.5 fusion.11
  161.6 15.1 %collective-permute-done.3 = bf16[768,768]{1,0:T(8,128)(2,1)} collective-permute-done((bf16[768,768]{1,0:T(8,128)(2,1)}, bf16[768,768]{1,0:T(8,128)(2,1)}, u32[]{:S(2)}, u32[]{:S(2)}) %collective-permute-start.3) | collective-permute-done | bytes 1179680 | tf_op jit(solution)/shard_map/ppermute | solution.py:549
  176.7 1.3 collective-permute-start.4
  178.0 2.6 fusion.15
  180.6 2.7 fusion.14
  183.3 3.8 multiply_reduce_fusion
  187.2 16.9 %collective-permute-done.4 = bf16[768,768]{1,0:T(8,128)(2,1)} collective-permute-done((bf16[768,768]{1,0:T(8,128)(2,1)}, bf16[768,768]{1,0:T(8,128)(2,1)}, u32[]{:S(2)}, u32[]{:S(2)}) %collective-permute-start.4) | collective-permute-done | bytes 1179680 | tf_op jit(solution)/shard_map/ppermute | solution.py:549
  204.1 4.8 convert_reduce_fusion.2
  208.8 1.1 convolution_convert_fusion.2
  210.2 1.0 copy-done.16
  212.7 1.4 add_reduce_fusion
  215.2 2.2 convolution_convert_fusion.1.g_ref
  217.3 2.0 fusion.24
  219.4 40.7 %attend_back.1 = (bf16[768,2304]{1,0:T(8,128)(2,1)}, bf16[640,1536]{1,0:T(8,128)(2,1)}, f32[8,768]{1,0:T(8,128)}) custom-call(s32[1,1408]{1,0:T(1,128)} %copy-done.25, bf16[768,768]{1,0:T(8,128)(2,1)} %get-tuple-element.71.q_ref, bf16[768,768]{1,0:T(8,128)(2,1)} %convolution_convert_fusion.1.g_ref, bf16[768,768]{1,0:T(8,128)(2,1)} %get-tuple-element.72.k_own_ref, ...), custom_call_target="tpu_custom_call" | custom-call | flops 8304721920 | bytes 17301504 | tf_op jit(solution)/shard_map/attend_back/pallas_call | solution.py:402
  260.1 5.1 fusion.20
  265.2 2.8 collective-permute-start.8
  268.0 1.1 convolution_convert_fusion
  270.0 2.4 collective-permute-start.9
  272.4 2.0 fusion.16
  274.5 2.2 add_convert_fusion
  276.7 1.4 copy-done.7
  278.1 1.1 dynamic-slice_bitcast_fusion
  279.4 43.7 %all-reduce.11.cloned.1.call-done = (bf16[384,1536]{1,0:T(8,128)(2,1)}, bf16[768,768]{1,0:T(8,128)(2,1)}) async-done(((bf16[384,1536]{1,0:T(8,128)(2,1)}, bf16[768,768]{1,0:T(8,128)(2,1)}), (bf16[384,1536]{1,0:T(8,128)(2,1)}, bf16[768,768]{1,0:T(8,128)(2,1)})) %all-reduce.11.cloned.1.call-update) | async-done | bytes 2359312 | tf_op jit(solution)/shard_map/psum | solution.py:592
  323.7 2.5 fusion.23
  326.3 1.3 constant_dynamic-update-slice_fusion
  327.6 7.6 %fusion.10 = (f32[768]{0:T(1024)}, f32[768]{0:T(1024)}, f32[768]{0:T(1024)}, f32[768]{0:T(1024)}, f32[768,768]{1,0:T(8,128)}) fusion(bf16[768,768]{1,0:T(8,128)(2,1)S(1)} %copy-done.2, f32[768]{0:T(1024)S(1)} %copy-done.21, f32[768]{0:T(1024)S(1)} %broadcast_multiply_fusion.1, f32[768]{0:T(1024)S(1)} %copy-done.20, ...), kind=kOutput, calls=%fused_computation.19 | convolution fusion | flops 2724983808 | bytes 11817984 | tf_op jit(solution)/shard_map/dot_general | solution.py:31
  335.2 2.6 fusion.13
  337.8 99.9 %all-reduce.7.cloned.1.call-done = bf16[384,768]{1,0:T(8,128)(2,1)} async-done(((bf16[384,768]{1,0:T(8,128)(2,1)}), bf16[384,768]{1,0:T(8,128)(2,1)}) %all-reduce.7.cloned.1.call-update) | async-done | bytes 589840 | tf_op jit(solution)/shard_map/psum | solution.py:604
  439.1 3.1 fusion.9
  442.2 42.0 %all-reduce = (f32[768]{0:T(1024)}, f32[768]{0:T(1024)}, f32[768]{0:T(1024)}, f32[768]{0:T(1024)}, f32[768]{0:T(1024)}, /*index=5*/f32[768]{0:T(1024)}, f32[8,768]{1,0:T(8,128)}, f32[3072]{0:T(1024)}) all-reduce(f32[768]{0:T(1024)} %get-tuple-element.106, ...), channel_id=1, replica_groups=mesh['chip'=8,'core'=2,'mlp'=2] {'chip','core','mlp'}, use_global_device_ids=true, to_apply=%region_17.18 | all-reduce | flops 13824 | bytes 110592 | tf_op jit(solution)/shard_map/psum | solution.py:624
  484.1 1.8 broadcast_select_fusion.3
  485.9 2.8 maximum_convert_fusion.1
  488.8 76.0 %all-reduce.9.cloned.1.call-done = (bf16[384,768]{1,0:T(8,128)(2,1)}, bf16[384,1536]{1,0:T(8,128)(2,1)}) async-done(((bf16[384,768]{1,0:T(8,128)(2,1)}, bf16[384,1536]{1,0:T(8,128)(2,1)}), (bf16[384,768]{1,0:T(8,128)(2,1)}, bf16[384,1536]{1,0:T(8,128)(2,1)})) %all-reduce.9.cloned.1.call-update) | async-done | bytes 1769488 | tf_op jit(solution)/shard_map/psum | solution.py:624
  564.8 1.4 broadcast_select_fusion.1
  566.8 2.5 maximum_convert_fusion.2
  569.4 1.3 broadcast_select_fusion.7
  570.7 1.6 maximum_convert_fusion.3
  574.4 1.3 broadcast_select_fusion.9
  575.9 10.0 %maximum_convert_fusion = f32[768,2304]{1,0:T(8,128)} fusion(bf16[384,1536]{1,0:T(8,128)(2,1)S(1)} %get-tuple-element.154, bf16[384,1536]{1,0:T(8,128)(2,1)S(1)} %get-tuple-element.153, bf16[384,768]{1,0:T(8,128)(2,1)S(1)} %get-tuple-element.159, bf16[384,768]{1,0:T(8,128)(2,1)S(1)} %get-tuple-element.158), kind=kLoop, calls=%fused_computation.3 | loop fusion | flops 14155776 | bytes 10616832 | tf_op jit(solution)/shard_map/convert_element_type | solution.py:630
  (157 shorter events, 20.5 us)
Async XLA Ops:
  7.2 57.6 %copy-start = (bf16[768,768]{1,0:T(8,128)(2,1)S(1)}, bf16[768,768]{1,0:T(8,128)(2,1)}, u32[]{:S(2)}) copy-start(bf16[768,768]{1,0:T(8,128)(2,1)} %param.27) | copy-start | bytes 3538948
  7.2 8.1 %copy-start.29 = (s32[1,1536]{1,0:T(1,128)S(1)}, s32[1,1536]{1,0:T(1,128)}, u32[]{:S(2)}) copy-start(s32[1,1536]{1,0:T(1,128)} %param.21) | copy-start | bytes 18436
  7.2 9.0 %copy-start.19 = (f32[768]{0:T(1024)S(1)}, f32[768]{0:T(1024)}, u32[]{:S(2)}) copy-start(f32[768]{0:T(1024)} %param.22) | copy-start | bytes 9220
  7.2 9.6 %copy-start.32 = (f32[768]{0:T(1024)S(1)}, f32[768]{0:T(1024)}, u32[]{:S(2)}) copy-start(f32[768]{0:T(1024)} %param.23) | copy-start | bytes 9220
  7.2 10.2 %copy-start.26 = (f32[2304]{0:T(1024)S(1)}, f32[2304]{0:T(1024)}, u32[]{:S(2)}) copy-start(f32[2304]{0:T(1024)} %param.25) | copy-start | bytes 27652
  7.2 10.8 %copy-start.33 = (f32[2,384]{1,0:T(2,128)S(1)}, f32[2,384]{1,0:T(2,128)}, u32[]{:S(2)}) copy-start(f32[2,384]{1,0:T(2,128)} %param.26) | copy-start | bytes 9220
  7.3 14.6 %copy-start.27 = (f32[1536]{0:T(1024)S(1)}, f32[1536]{0:T(1024)}, u32[]{:S(2)}) copy-start(f32[1536]{0:T(1024)} %param.32) | copy-start | bytes 18436
  7.3 315.9 %all-reduce.11.cloned.1.call-start = ((), (), s32[]{:S(2)}) async-start(), calls=%async_computation.2 | async-start | bytes 4718592 | tf_op jit(solution)/shard_map/psum | solution.py:592
  8.7 26.2 %collective-permute-start = (bf16[640,768]{1,0:T(8,128)(2,1)S(1)}, bf16[640,768]{1,0:T(8,128)(2,1)S(1)}, u32[]{:S(2)}, u32[]{:S(2)}) collective-permute-start(bf16[640,768]{1,0:T(8,128)(2,1)S(1)} %constant_dynamic-slice_fusion.2), channel_id=1, source_target_pairs={{0,1},{1,0},{2,3},{3,2},{4,5},{5,4},{6,7},{7,6},{8,9},{9,8},{10,11... | collective-permute-start | bytes 2949128 | tf_op jit(solution)/shard_map/ppermute | solution.py:549
  13.2 21.6 %copy-start.25 = (s32[1,1408]{1,0:T(1,128)}, s32[1,1408]{1,0:T(1,128)S(1)}, u32[]{:S(2)}) copy-start(s32[1,1408]{1,0:T(1,128)S(1)} %broadcast_in_dim.20.ids_ref) | copy-start | bytes 16900
  34.8 0.9 copy-start.35
  44.0 20.8 %copy-start.36 = (f32[768]{0:T(1024)S(1)}, f32[768]{0:T(1024)}, u32[]{:S(2)}) copy-start(f32[768]{0:T(1024)} %param.28) | copy-start | bytes 9220
  67.6 0.7 copy-start.18
  67.7 0.7 copy-start.30
  69.8 43.9 %collective-permute-start.1 = (bf16[768,768]{1,0:T(8,128)(2,1)}, bf16[768,768]{1,0:T(8,128)(2,1)}, u32[]{:S(2)}, u32[]{:S(2)}) collective-permute-start(bf16[768,768]{1,0:T(8,128)(2,1)} %add_convert_fusion.4.n2_ref), channel_id=1, source_target_pairs={{0,1},{1,0},{2,3},{3,2},{4,5},{5,4},{6,7},{7,6},{8,9},{9,8},{10,11... | collective-permute-start | bytes 3538952 | tf_op jit(solution)/shard_map/ppermute | solution.py:549
  71.1 51.1 %collective-permute-start.2 = (bf16[768,768]{1,0:T(8,128)(2,1)}, bf16[768,768]{1,0:T(8,128)(2,1)}, u32[]{:S(2)}, u32[]{:S(2)}) collective-permute-start(bf16[768,768]{1,0:T(8,128)(2,1)} %g_ref.1), channel_id=1, source_target_pairs={{0,1},{1,0},{2,3},{3,2},{4,5},{5,4},{6,7},{7,6},{8,9},{9,8},{10,11... | collective-permute-start | bytes 3538952 | tf_op jit(solution)/shard_map/ppermute | solution.py:549
  101.8 6.4 %copy-start.41 = (bf16[768,1536]{1,0:T(8,128)(2,1)S(1)}, bf16[768,1536]{1,0:T(8,128)(2,1)}, u32[]{:S(2)}) copy-start(bf16[768,1536]{1,0:T(8,128)(2,1)} %get-tuple-element.86) | copy-start | bytes 7077892
  139.9 9.9 %copy-start.39 = (f32[1536,768]{1,0:T(8,128)S(1)}, f32[1536,768]{1,0:T(8,128)}, u32[]{:S(2)}) copy-start(f32[1536,768]{1,0:T(8,128)} %fusion.41) | copy-start | bytes 14155780
  145.5 7.6 %copy-start.9 = (bf16[768,1536]{1,0:T(8,128)(2,1)}, bf16[768,1536]{1,0:T(8,128)(2,1)S(1)}, u32[]{:S(2)}) copy-start(bf16[768,1536]{1,0:T(8,128)(2,1)S(1)} %add_convert_fusion.2) | copy-start | bytes 7077892
  145.6 4.2 copy-start.44
  146.7 31.3 %collective-permute-start.5 = (bf16[384,1536]{1,0:T(8,128)(2,1)}, bf16[384,1536]{1,0:T(8,128)(2,1)}, u32[]{:S(2)}, u32[]{:S(2)}) collective-permute-start(bf16[384,1536]{1,0:T(8,128)(2,1)} %dynamic-slice_bitcast_fusion.2), channel_id=1, source_target_pairs={{0,2},{2,0},{1,3},{3,1},{4,6},{6,4},{5,7},{7,5},{8,10},{10,8},{9,1... | collective-permute-start | bytes 3538952 | tf_op jit(solution)/shard_map/ppermute | solution.py:523
  148.5 28.2 %collective-permute-start.3 = (bf16[768,768]{1,0:T(8,128)(2,1)}, bf16[768,768]{1,0:T(8,128)(2,1)}, u32[]{:S(2)}, u32[]{:S(2)}) collective-permute-start(bf16[768,768]{1,0:T(8,128)(2,1)} %get-tuple-element.81), channel_id=1, source_target_pairs={{0,1},{1,0},{2,3},{3,2},{4,5},{5,4},{6,7},{7,6},{8,9},{9,8},{10,11... | collective-permute-start | bytes 3538952 | tf_op jit(solution)/shard_map/ppermute | solution.py:549
  153.1 1.4 copy-start.11
  153.1 3.1 copy-start.23
  155.7 24.9 %collective-permute-start.6 = (bf16[768,768]{1,0:T(8,128)(2,1)}, bf16[768,768]{1,0:T(8,128)(2,1)}, u32[]{:S(2)}, u32[]{:S(2)}) collective-permute-start(bf16[768,768]{1,0:T(8,128)(2,1)} %dynamic-slice_bitcast_fusion.1), channel_id=1, source_target_pairs={{0,2},{2,0},{1,3},{3,1},{4,6},{6,4},{5,7},{7,5},{8,10},{10,8},{9,1... | collective-permute-start | bytes 3538952 | tf_op jit(solution)/shard_map/ppermute | solution.py:523
  157.4 20.6 %copy-start.10 = (bf16[768,1536]{1,0:T(8,128)(2,1)S(1)}, bf16[768,1536]{1,0:T(8,128)(2,1)}, u32[]{:S(2)}) copy-start(bf16[768,1536]{1,0:T(8,128)(2,1)} %copy-done.9) | copy-start | bytes 7077892
  159.1 21.5 %copy-start.12 = (bf16[1536,768]{1,0:T(8,128)(2,1)S(1)}, bf16[1536,768]{1,0:T(8,128)(2,1)}, u32[]{:S(2)}) copy-start(bf16[1536,768]{1,0:T(8,128)(2,1)} %copy-done.11) | copy-start | bytes 7077892
  176.7 27.3 %collective-permute-start.4 = (bf16[768,768]{1,0:T(8,128)(2,1)}, bf16[768,768]{1,0:T(8,128)(2,1)}, u32[]{:S(2)}, u32[]{:S(2)}) collective-permute-start(bf16[768,768]{1,0:T(8,128)(2,1)} %get-tuple-element.82), channel_id=1, source_target_pairs={{0,1},{1,0},{2,3},{3,2},{4,5},{5,4},{6,7},{7,6},{8,9},{9,8},{10,11... | collective-permute-start | bytes 3538952 | tf_op jit(solution)/shard_map/ppermute | solution.py:549
  183.3 20.8 %copy-start.5 = (f32[768,768]{1,0:T(8,128)S(1)}, f32[768,768]{1,0:T(8,128)}, u32[]{:S(2)}) copy-start(f32[768,768]{1,0:T(8,128)} %get-tuple-element.83) | copy-start | bytes 7077892
  183.3 20.8 %copy-start.6 = (f32[768,768]{1,0:T(8,128)S(1)}, f32[768,768]{1,0:T(8,128)}, u32[]{:S(2)}) copy-start(f32[768,768]{1,0:T(8,128)} %get-tuple-element.78) | copy-start | bytes 7077892
  183.3 20.8 %copy-start.31 = (f32[768]{0:T(1024)S(1)}, f32[768]{0:T(1024)}, u32[]{:S(2)}) copy-start(f32[768]{0:T(1024)} %param.34) | copy-start | bytes 9220
  204.1 4.8 copy-start.43
  208.8 1.4 copy-start.3
  208.8 3.3 copy-start.22
  210.2 1.0 copy-start.16
  211.3 3.9 copy-start.4
  212.1 5.2 collective-permute-start.7
  215.1 222.6 %all-reduce.7.cloned.1.call-start = ((), (), s32[]{:S(2)}) async-start(), calls=%async_computation | async-start | bytes 1179648 | tf_op jit(solution)/shard_map/psum | solution.py:604
  215.1 2.2 copy-start.17
  260.1 7.9 %copy-start.37 = (bf16[768,2304]{1,0:T(8,128)(2,1)S(1)}, bf16[768,2304]{1,0:T(8,128)(2,1)}, u32[]{:S(2)}) copy-start(bf16[768,2304]{1,0:T(8,128)(2,1)} %get-tuple-element.96) | copy-start | bytes 10616836
  260.1 7.9 %copy-start.42 = (bf16[768,768]{1,0:T(8,128)(2,1)S(1)}, bf16[768,768]{1,0:T(8,128)(2,1)}, u32[]{:S(2)}) copy-start(bf16[768,768]{1,0:T(8,128)(2,1)} %get-tuple-element.98) | copy-start | bytes 3538948
  265.2 61.0 %collective-permute-start.8 = (bf16[640,768]{1,0:T(8,128)(2,1)}, bf16[640,768]{1,0:T(8,128)(2,1)}, u32[]{:S(2)}, u32[]{:S(2)}) collective-permute-start(bf16[640,768]{1,0:T(8,128)(2,1)} %fusion.20), channel_id=1, source_target_pairs={{0,1},{1,0},{2,3},{3,2},{4,5},{5,4},{6,7},{7,6},{8,9},{9,8},{10,11... | collective-permute-start | bytes 2949128 | tf_op jit(solution)/shard_map/ppermute | solution.py:549
  269.1 5.4 copy-start.15
  270.0 4.5 copy-start.38
  270.0 4.5 copy-start.40
  270.0 53.7 %collective-permute-start.9 = (bf16[384,768]{1,0:T(8,128)(2,1)}, bf16[384,768]{1,0:T(8,128)(2,1)}, u32[]{:S(2)}, u32[]{:S(2)}) collective-permute-start(bf16[384,768]{1,0:T(8,128)(2,1)} %dynamic-slice_bitcast_fusion.3), channel_id=1, source_target_pairs={{0,2},{2,0},{1,3},{3,1},{4,6},{6,4},{5,7},{7,5},{8,10},{10,8},{9,1... | collective-permute-start | bytes 1769480 | tf_op jit(solution)/shard_map/ppermute | solution.py:523
  276.7 1.4 copy-start.7
  279.2 56.1 %collective-permute-start.10 = (bf16[384,1536]{1,0:T(8,128)(2,1)}, bf16[384,1536]{1,0:T(8,128)(2,1)}, u32[]{:S(2)}, u32[]{:S(2)}) collective-permute-start(bf16[384,1536]{1,0:T(8,128)(2,1)} %dynamic-slice_bitcast_fusion), channel_id=1, source_target_pairs={{0,2},{2,0},{1,3},{3,1},{4,6},{6,4},{5,7},{7,5},{8,10},{10,8},{9,1... | collective-permute-start | bytes 3538952 | tf_op jit(solution)/shard_map/ppermute | solution.py:523
  279.2 285.6 %all-reduce.9.cloned.1.call-start = ((), (), s32[]{:S(2)}) async-start(), calls=%async_computation.1 | async-start | bytes 3538944 | tf_op jit(solution)/shard_map/psum | solution.py:624
  323.1 161.0 %collective-permute-start.14 = (bf16[384,1536]{1,0:T(8,128)(2,1)}, bf16[384,1536]{1,0:T(8,128)(2,1)}, u32[]{:S(2)}, u32[]{:S(2)}) collective-permute-start(bf16[384,1536]{1,0:T(8,128)(2,1)} %get-tuple-element.145), channel_id=1, source_target_pairs={{0,2},{2,0},{1,3},{3,1},{4,6},{6,4},{5,7},{7,5},{8,10},{10,8},{9,1... | collective-permute-start | bytes 3538952 | tf_op jit(solution)/shard_map/ppermute | solution.py:523
  323.1 4.5 copy-start.2
  323.1 4.5 copy-start.20
  323.1 4.5 copy-start.21
  323.1 4.5 copy-start.34
  323.1 241.7 %collective-permute-start.15 = (bf16[768,768]{1,0:T(8,128)(2,1)}, bf16[768,768]{1,0:T(8,128)(2,1)}, u32[]{:S(2)}, u32[]{:S(2)}) collective-permute-start(bf16[768,768]{1,0:T(8,128)(2,1)} %get-tuple-element.146), channel_id=1, source_target_pairs={{0,2},{2,0},{1,3},{3,1},{4,6},{6,4},{5,7},{7,5},{8,10},{10,8},{9,1... | collective-permute-start | bytes 3538952 | tf_op jit(solution)/shard_map/ppermute | solution.py:523
  327.6 7.6 %copy-start.8 = (bf16[768,1536]{1,0:T(8,128)(2,1)S(1)}, bf16[768,1536]{1,0:T(8,128)(2,1)}, u32[]{:S(2)}) copy-start(bf16[768,1536]{1,0:T(8,128)(2,1)} %copy-done.7) | copy-start | bytes 7077892
  442.2 127.2 %collective-permute-start.13 = (bf16[384,768]{1,0:T(8,128)(2,1)}, bf16[384,768]{1,0:T(8,128)(2,1)}, u32[]{:S(2)}, u32[]{:S(2)}) collective-permute-start(bf16[384,768]{1,0:T(8,128)(2,1)} %all-reduce.7.cloned.1.call-done), channel_id=1, source_target_pairs={{0,2},{2,0},{1,3},{3,1},{4,6},{6,4},{5,7},{7,5},{8,10},{10,8},{9,1... | collective-permute-start | bytes 1769480 | tf_op jit(solution)/shard_map/ppermute | solution.py:523
  485.9 78.9 %copy-start.13 = (bf16[768,768]{1,0:T(8,128)(2,1)S(1)}, bf16[768,768]{1,0:T(8,128)(2,1)}, u32[]{:S(2)}) copy-start(bf16[768,768]{1,0:T(8,128)(2,1)} %get-tuple-element.146) | copy-start | bytes 3538948
  564.8 10.9 %collective-permute-start.12 = (bf16[384,1536]{1,0:T(8,128)(2,1)}, bf16[384,1536]{1,0:T(8,128)(2,1)S(1)}, u32[]{:S(2)}, u32[]{:S(2)}) collective-permute-start(bf16[384,1536]{1,0:T(8,128)(2,1)} %get-tuple-element.117), channel_id=1, source_target_pairs={{0,2},{2,0},{1,3},{3,1},{4,6},{6,4},{5,7},{7,5},{8,10},{10,8},{9,1... | collective-permute-start | bytes 3538952 | tf_op jit(solution)/shard_map/ppermute | solution.py:523
  566.2 8.2 %collective-permute-start.11 = (bf16[384,768]{1,0:T(8,128)(2,1)}, bf16[384,768]{1,0:T(8,128)(2,1)}, u32[]{:S(2)}, u32[]{:S(2)}) collective-permute-start(bf16[384,768]{1,0:T(8,128)(2,1)} %get-tuple-element.116), channel_id=1, source_target_pairs={{0,2},{2,0},{1,3},{3,1},{4,6},{6,4},{5,7},{7,5},{8,10},{10,8},{9,1... | collective-permute-start | bytes 1769480 | tf_op jit(solution)/shard_map/ppermute | solution.py:523
  570.7 1.6 copy-start.24
  570.7 3.0 copy-start.28
  570.7 5.0 copy-start.14
  575.9 10.0 %copy-start.1 = (bf16[768,768]{1,0:T(8,128)(2,1)S(1)}, bf16[768,768]{1,0:T(8,128)(2,1)}, u32[]{:S(2)}) copy-start(bf16[768,768]{1,0:T(8,128)(2,1)} %param.27) | copy-start | bytes 3538948
Sparse Core Ops, SparseCore 0:
  215.2 107.8 all-reduce.10
  328.5 109.1 all-reduce.6
  444.0 120.7 all-reduce.8
